TPU v7x, 32 devices: a whole 2x2x4 slice. The times are simulated.
32 devices in a mesh: maps: 8 (over z, x), chan: 4 (over y, core).
Axes of the slice: x: 2, y: 2, z: 4, core: 2. Of those that a mesh axis runs over, the one named last changes fastest.
Arguments:
- input_maps: bfloat16 [16, 18, 24, 512], P('maps', None, None, 'chan'), may hold values from 0 to 2
- valid_mask: int32 [16, 18, 24], P('maps'), may hold values from 0 to 1, as said below
- pool_index: int32 [16, 9, 12, 512], P('maps', None, None, 'chan'), may hold values from 0 to 3
- out_grad: bfloat16 [16, 9, 12, 512], P('maps', None, None, 'chan'), may hold values from -6 to 6
- conv_weights: float32 [3, 9, 512, 512], P(None, None, 'maps', 'chan'), may hold values from -0.09375 to 0.09375
- weight_first: float32 [3, 9, 512, 512], P(None, None, 'maps', 'chan'), may hold values from -86.463976 to 86.463976
- weight_second: float32 [3, 9, 512, 512], P(None, None, 'maps', 'chan'), may hold values from 176.9472 to 1869.0048
- norm_gain: float32 [3, 512], P(None, 'chan'), may hold values from 0.5 to 1.5
- norm_bias: float32 [3, 512], P(None, 'chan'), may hold values from -2.5 to 2.5
- norm_first: float32 [3, 2, 512], P(None, None, 'chan'), may hold values from -86.463976 to 86.463976
- norm_second: float32 [3, 2, 512], P(None, None, 'chan'), may hold values from 223.9488 to 1869.0048
Outputs:
- pooled: bfloat16 [16, 9, 12, 512], P('maps', None, None, 'chan')
- image_grad: float32 [16, 18, 24, 512], P('maps', None, None, 'chan')
- weight_grads: float32 [3, 9, 512, 512], P(None, None, 'maps', 'chan')
- new_weight_first: float32 [3, 9, 512, 512], P(None, None, 'maps', 'chan')
- new_weight_second: float32 [3, 9, 512, 512], P(None, None, 'maps', 'chan')
- new_weights: float32 [3, 9, 512, 512], P(None, None, 'maps', 'chan')
- weight_copy: bfloat16 [3, 9, 512, 512], P(None, None, 'maps', 'chan')
- norm_grads: float32 [3, 2, 512], P(None, None, 'chan')
- new_norm_first: float32 [3, 2, 512], P(None, None, 'chan')
- new_norm_second: float32 [3, 2, 512], P(None, None, 'chan')
- new_norms: float32 [3, 2, 512], P(None, None, 'chan')
Inputs may be any that keep to these rules, and one draw needn't show every extreme that they name: `valid_mask`: 1 marks a pixel with valid depth, 0 one without. `pool_index`: 2 r + s for the kept pixel at row r and column s of its window.
All inputs are finite; a program needn't handle non-finite values.
Results may differ from a plain program's by a relative error of at most 0.02.
Values may be sent and summed in bfloat16 or wider, within the bound.
A program may use at most 128 MiB of HBM per device.

v0:
```python
import jax
import jax.numpy as jnp
from jax import lax
from jax.sharding import PartitionSpec as P

beta_first = 0.5
beta_second = 0.5
rate_conv = 0.01
rate_norm = 0.2
decay_rate = 0.01
adam_epsilon = 1e-08
norm_epsilon = 1e-05
step_count = 5.0


def pad_map(values):
    return jnp.pad(values, ((0, 0), (1, 1), (1, 1), (0, 0)))


def silu_slope(values):
    sigma = jax.nn.sigmoid(values)
    return sigma * (1.0 + values * (1.0 - sigma))


def apply_kernel(padded, kernel, height, map_width):
    summed = None
    for tap_index in range(9):
        offset_row = tap_index // 3
        offset_col = tap_index % 3
        window = padded[:, offset_row : offset_row + height, offset_col : offset_col + map_width, :]
        product_term = jnp.einsum(
            "nhwc,co->nhwo", window, kernel[tap_index], preferred_element_type=jnp.float32
        )
        summed = product_term if summed is None else summed + product_term
    return summed


def kernel_grad(padded, grad_conv, height, map_width):
    pieces = []
    for tap_index in range(9):
        offset_row = tap_index // 3
        offset_col = tap_index % 3
        window = padded[:, offset_row : offset_row + height, offset_col : offset_col + map_width, :]
        pieces.append(
            jnp.einsum("nhwc,nhwo->co", window, grad_conv, preferred_element_type=jnp.float32)
        )
    return jnp.stack(pieces, axis=0)


def input_grad_sum(grad_pad, kernel, height, map_width):
    summed = None
    for tap_index in range(9):
        offset_row = 2 - tap_index // 3
        offset_col = 2 - tap_index % 3
        window = grad_pad[
            :, offset_row : offset_row + height, offset_col : offset_col + map_width, :
        ]
        product_term = jnp.einsum(
            "nhwo,co->nhwc", window, kernel[tap_index], preferred_element_type=jnp.float32
        )
        summed = product_term if summed is None else summed + product_term
    return summed


def select_window(activation, pool_index):
    map_count, height, map_width, channels = activation.shape
    windows = activation.reshape(map_count, height // 2, 2, map_width // 2, 2, channels)
    pooled = jnp.zeros(pool_index.shape, jnp.float32)
    for corner in range(4):
        pooled = pooled + jnp.where(
            pool_index == corner, windows[:, :, corner // 2, :, corner % 2, :], 0.0
        )
    return pooled


def spread_back(gradient, pool_index):
    pieces = [jnp.where(pool_index == corner, gradient, 0.0) for corner in range(4)]
    upper_half = jnp.stack([pieces[0], pieces[1]], axis=3)
    lower_half = jnp.stack([pieces[2], pieces[3]], axis=3)
    joined = jnp.stack([upper_half, lower_half], axis=2)
    map_count, half_height, two_rows, half_width, two_cols, channels = joined.shape
    return joined.reshape(map_count, half_height * 2, half_width * 2, channels)


def adamw_update(parameter, gradient, first_moment, second_moment, step_rate):
    first_new = beta_first * first_moment + (1.0 - beta_first) * gradient
    second_new = beta_second * second_moment + (1.0 - beta_second) * gradient * gradient
    first_hat = first_new / (1.0 - beta_first**step_count)
    second_hat = second_new / (1.0 - beta_second**step_count)
    updated = parameter - step_rate * (
        first_hat / (jnp.sqrt(second_hat) + adam_epsilon) + decay_rate * parameter
    )
    return (updated, first_new, second_new)


def local(
    input_maps,
    valid_mask,
    pool_index,
    out_grad,
    conv_weights,
    weight_first,
    weight_second,
    norm_gain,
    norm_bias,
    norm_first,
    norm_second,
):
    map_count, height, map_width, channels = input_maps.shape
    layer_total = conv_weights.shape[0]
    mask_float = valid_mask.astype(jnp.float32)[..., None]
    local_count = jnp.sum(valid_mask.astype(jnp.float32))
    low_weights = lax.all_gather(conv_weights.astype(jnp.bfloat16), "maps", axis=2, tiled=True)
    activation = (input_maps.astype(jnp.float32) * mask_float).astype(jnp.bfloat16)
    stored = []
    for layer_index in range(layer_total):
        gathered = lax.all_gather(activation, "chan", axis=3, tiled=True)
        padded = pad_map(gathered)
        conv_out = apply_kernel(padded, low_weights[layer_index], height, map_width)
        center_sum, valid_count = lax.psum(
            (jnp.sum(conv_out * mask_float, axis=(0, 1, 2)), local_count), "maps"
        )
        center = center_sum / valid_count
        centered = conv_out - center
        variance = (
            lax.psum(jnp.sum(mask_float * centered * centered, axis=(0, 1, 2)), "maps")
            / valid_count
        )
        inv_std = lax.rsqrt(variance + norm_epsilon)
        normed = centered * inv_std
        shifted = norm_gain[layer_index] * normed + norm_bias[layer_index]
        result = jax.nn.silu(shifted) * mask_float
        stored.append((padded, normed, shifted, inv_std))
        activation = result.astype(jnp.bfloat16)
    pooled = select_window(result, pool_index)
    grad_act = spread_back(out_grad.astype(jnp.float32), pool_index)
    kernel_terms = []
    gain_list = []
    bias_list = []
    for layer_index in reversed(range(layer_total)):
        padded, normed, shifted, inv_std = stored[layer_index]
        grad_pre = grad_act * silu_slope(shifted) * mask_float
        gain_grad, bias_grad = lax.psum(
            (jnp.sum(grad_pre * normed, axis=(0, 1, 2)), jnp.sum(grad_pre, axis=(0, 1, 2))), "maps"
        )
        grad_conv = (
            mask_float
            * norm_gain[layer_index]
            * inv_std
            * (grad_pre - (bias_grad + normed * gain_grad) / valid_count)
        ).astype(jnp.bfloat16)
        kernel_terms.append(kernel_grad(padded, grad_conv, height, map_width))
        gain_list.append(gain_grad)
        bias_list.append(bias_grad)
        partial_grad = input_grad_sum(
            pad_map(grad_conv), low_weights[layer_index], height, map_width
        )
        grad_act = lax.psum_scatter(
            partial_grad.astype(jnp.bfloat16), "chan", scatter_dimension=3, tiled=True
        ).astype(jnp.float32)
    image_grad = grad_act * mask_float
    weight_terms = jnp.stack(kernel_terms[::-1], axis=0)
    weight_grads = lax.psum_scatter(weight_terms, "maps", scatter_dimension=2, tiled=True)
    norm_grads = jnp.stack(
        [jnp.stack(gain_list[::-1], axis=0), jnp.stack(bias_list[::-1], axis=0)], axis=1
    )
    new_weights, new_weight_first, new_weight_second = adamw_update(
        conv_weights, weight_grads, weight_first, weight_second, rate_conv
    )
    norm_values = jnp.stack([norm_gain, norm_bias], axis=1)
    new_norms, new_norm_first, new_norm_second = adamw_update(
        norm_values, norm_grads, norm_first, norm_second, rate_norm
    )
    return (
        pooled.astype(jnp.bfloat16),
        image_grad,
        weight_grads,
        new_weight_first,
        new_weight_second,
        new_weights,
        new_weights.astype(jnp.bfloat16),
        norm_grads,
        new_norm_first,
        new_norm_second,
        new_norms,
    )


def solution(mesh):
    return jax.shard_map(
        local,
        mesh=mesh,
        in_specs=(
            P("maps", None, None, "chan"),
            P("maps", None, None),
            P("maps", None, None, "chan"),
            P("maps", None, None, "chan"),
            P(None, None, "maps", "chan"),
            P(None, None, "maps", "chan"),
            P(None, None, "maps", "chan"),
            P(None, "chan"),
            P(None, "chan"),
            P(None, None, "chan"),
            P(None, None, "chan"),
        ),
        out_specs=(
            P("maps", None, None, "chan"),
            P("maps", None, None, "chan"),
            P(None, None, "maps", "chan"),
            P(None, None, "maps", "chan"),
            P(None, None, "maps", "chan"),
            P(None, None, "maps", "chan"),
            P(None, None, "maps", "chan"),
            P(None, None, "chan"),
            P(None, None, "chan"),
            P(None, None, "chan"),
            P(None, None, "chan"),
        ),
        check_vma=False,
    )
```

profile of v0, /device:TPU:0, one launch (start us, length us, event | category | flops | bytes accessed | tf_op | source)
XLA Modules:
  0.0 624.1 jit_solution(2798157223339960049)
XLA Ops:
  13.5 10.6 %all_gather.12 = bf16[2,18,24,512]{3,2,1,0:T(8,128)(2,1)S(1)} all-gather(bf16[2,18,24,128]{3,2,1,0:T(8,128)(2,1)S(1)} %multiply_convert_fusion.5), channel_id=1, replica_groups=mesh['maps'=8,'chan'=4] {'chan'}, dimensions={3}, use_global_device_ids=true | all-gather | bytes 1105920 | tf_op jit(solution)/shard_map/all_gather | solution.py:117
  24.1 3.7 pad_slice_fusion.16
  27.8 50.9 %all-gather.2.cloned.1.call-done = bf16[3,9,512,128]{3,2,1,0:T(8,128)(2,1)} async-done(((bf16[3,9,64,128]{3,2,1,0:T(8,128)(2,1)}), bf16[3,9,512,128]{3,2,1,0:T(8,128)(2,1)}) %all-gather.2.cloned.1.call-update) | async-done | bytes 3538960 | tf_op jit(solution)/shard_map/all_gather | solution.py:113
  90.9 19.5 %all-reduce.9 = (f32[128]{0:T(128)S(1)}, f32[]{:T(128)}) all-reduce(f32[128]{0:T(128)S(1)} %get-tuple-element.95, f32[]{:T(128)} %convert_reduce_fusion), channel_id=1, replica_groups=mesh['maps'=8,'chan'=4] {'maps'}, use_global_device_ids=true, to_apply=%region_1.2 | all-reduce | flops 129 | bytes 1032 | tf_op jit(solution)/shard_map/psum | solution.py:120
  111.3 17.4 %psum.99 = f32[128]{0:T(128)S(1)} all-reduce(f32[128]{0:T(128)S(1)} %fusion.55), channel_id=1, replica_groups=mesh['maps'=8,'chan'=4] {'maps'}, use_global_device_ids=true, to_apply=%region_5.6 | all-reduce | flops 128 | bytes 1024 | tf_op jit(solution)/shard_map/psum | solution.py:126
  129.5 9.1 %all_gather.14 = bf16[2,18,24,512]{3,2,1,0:T(8,128)(2,1)S(1)} all-gather(bf16[2,18,24,128]{3,2,1,0:T(8,128)(2,1)S(1)} %multiply_convert_fusion.4), channel_id=1, replica_groups=mesh['maps'=8,'chan'=4] {'chan'}, dimensions={3}, use_global_device_ids=true | all-gather | bytes 1105920 | tf_op jit(solution)/shard_map/all_gather | solution.py:117
  150.7 18.9 %psum.100 = f32[128]{0:T(128)S(1)} all-reduce(f32[128]{0:T(128)S(1)} %get-tuple-element.97), channel_id=1, replica_groups=mesh['maps'=8,'chan'=4] {'maps'}, use_global_device_ids=true, to_apply=%region_7.8 | all-reduce | flops 128 | bytes 1024 | tf_op jit(solution)/shard_map/psum | solution.py:120
  170.5 17.3 %psum.101 = f32[128]{0:T(128)S(1)} all-reduce(f32[128]{0:T(128)S(1)} %fusion.56), channel_id=1, replica_groups=mesh['maps'=8,'chan'=4] {'maps'}, use_global_device_ids=true, to_apply=%region_9.10 | all-reduce | flops 128 | bytes 1024 | tf_op jit(solution)/shard_map/psum | solution.py:126
  188.7 8.7 %all_gather.15 = bf16[2,18,24,512]{3,2,1,0:T(8,128)(2,1)S(1)} all-gather(bf16[2,18,24,128]{3,2,1,0:T(8,128)(2,1)S(1)} %multiply_convert_fusion.3), channel_id=1, replica_groups=mesh['maps'=8,'chan'=4] {'chan'}, dimensions={3}, use_global_device_ids=true | all-gather | bytes 1105920 | tf_op jit(solution)/shard_map/all_gather | solution.py:117
  197.5 3.6 pad_slice_fusion
  214.0 18.9 %psum.102 = f32[128]{0:T(128)S(1)} all-reduce(f32[128]{0:T(128)S(1)} %get-tuple-element.99), channel_id=1, replica_groups=mesh['maps'=8,'chan'=4] {'maps'}, use_global_device_ids=true, to_apply=%region_11.12 | all-reduce | flops 128 | bytes 1024 | tf_op jit(solution)/shard_map/psum | solution.py:120
  234.8 17.3 %psum.103 = f32[128]{0:T(128)S(1)} all-reduce(f32[128]{0:T(128)S(1)} %fusion.57), channel_id=1, replica_groups=mesh['maps'=8,'chan'=4] {'maps'}, use_global_device_ids=true, to_apply=%region_13.14 | all-reduce | flops 128 | bytes 1024 | tf_op jit(solution)/shard_map/psum | solution.py:126
  255.1 18.9 %all-reduce.8 = (f32[128]{0:T(128)S(1)}, f32[128]{0:T(128)S(1)}) all-reduce(f32[128]{0:T(128)S(1)} %get-tuple-element.38, f32[128]{0:T(128)S(1)} %get-tuple-element.37), channel_id=1, replica_groups=mesh['maps'=8,'chan'=4] {'maps'}, use_global_device_ids=true, to_apply=%region_17.18 | all-reduce | flops 256 | bytes 2048 | tf_op jit(solution)/shard_map/psum | solution.py:143
  289.6 7.8 %copy.208 = bf16[2,18,24,512]{2,1,0,3:T(8,128)(2,1)} copy(bf16[2,18,24,512]{3,2,1,0:T(8,128)(2,1)} %add_convert_fusion.2) | data formatting | bytes 1769472
  297.5 7.8 %reshape.157 = bf16[512,864]{1,0:T(8,128)(2,1)} reshape(bf16[512,2,18,24]{3,2,1,0:T(8,128)(2,1)} %bitcast.521) | data formatting | bytes 1769472
  317.3 3.7 pad_slice_fusion.8
  321.0 5.7 reduce-scatter.13.cloned.1.call-done
  326.7 3.5 reshape.158
  332.3 21.6 %all-reduce.7 = (f32[128]{0:T(128)S(1)}, f32[128]{0:T(128)S(1)}) all-reduce(f32[128]{0:T(128)S(1)} %get-tuple-element.36, f32[128]{0:T(128)S(1)} %get-tuple-element.35), channel_id=1, replica_groups=mesh['maps'=8,'chan'=4] {'maps'}, use_global_device_ids=true, to_apply=%region_22.23 | all-reduce | flops 256 | bytes 2048 | tf_op jit(solution)/shard_map/psum | solution.py:143
  367.5 6.8 %copy.210 = bf16[2,18,24,512]{2,1,0,3:T(8,128)(2,1)} copy(bf16[2,18,24,512]{3,2,1,0:T(8,128)(2,1)S(1)} %add_convert_fusion.1) | data formatting | bytes 1769472
  374.3 7.8 %reshape.159 = bf16[512,864]{1,0:T(8,128)(2,1)} reshape(bf16[512,2,18,24]{3,2,1,0:T(8,128)(2,1)} %bitcast.522) | data formatting | bytes 1769472
  394.0 8.7 %reduce-scatter.15.cloned.1.call-done = bf16[128,864]{1,0:T(8,128)(2,1)} async-done(((bf16[512,864]{1,0:T(8,128)(2,1)}), bf16[128,864]{1,0:T(8,128)(2,1)}) %reduce-scatter.15.cloned.1.call-update) | async-done | bytes 221200
  402.7 2.7 reshape.160
  406.5 21.6 %all-reduce.6 = (f32[128]{0:T(128)S(1)}, f32[128]{0:T(128)S(1)}) all-reduce(f32[128]{0:T(128)S(1)} %get-tuple-element.34, f32[128]{0:T(128)S(1)} %get-tuple-element.33), channel_id=1, replica_groups=mesh['maps'=8,'chan'=4] {'maps'}, use_global_device_ids=true, to_apply=%region_27.28 | all-reduce | flops 256 | bytes 2048 | tf_op jit(solution)/shard_map/psum | solution.py:143
  440.0 2.8 add_convert_fusion
  442.8 7.8 %copy.212 = bf16[2,18,24,512]{2,1,0,3:T(8,128)(2,1)} copy(bf16[2,18,24,512]{3,2,1,0:T(8,128)(2,1)} %add_convert_fusion) | data formatting | bytes 1769472
  450.7 7.9 %reshape.161 = bf16[512,864]{1,0:T(8,128)(2,1)} reshape(bf16[512,2,18,24]{3,2,1,0:T(8,128)(2,1)} %bitcast.523) | data formatting | bytes 1769472
  465.8 5.9 pad_maximum_fusion
  476.3 2.8 reduce-scatter.17.cloned.1.call-done
  479.1 2.7 reshape.162
  483.6 129.6 %reduce-scatter.11.cloned.1.call-done = f32[3,9,64,128]{3,2,1,0:T(8,128)} async-done(((f32[3,9,512,128]{3,2,1,0:T(8,128)}), f32[3,9,64,128]{3,2,1,0:T(8,128)}) %reduce-scatter.11.cloned.1.call-update) | async-done | bytes 884752 | tf_op jit(solution)/shard_map/reduce_scatter | solution.py:163
  613.2 3.9 fusion.153
  (196 shorter events, 133.0 us)
Async XLA Ops:
  7.2 5.5 copy-start.28
  7.2 6.1 copy-start.29
  7.2 6.1 copy-start.30
  7.2 6.1 copy-start.27
  7.2 71.5 %all-gather.2.cloned.1.call-start = ((), (), s32[]{:S(2)}) async-start(), calls=%async_computation.4 | async-start | bytes 3981312 | tf_op jit(solution)/shard_map/all_gather | solution.py:113
  9.4 317.3 %reduce-scatter.13.cloned.1.call-start = ((), (), s32[]{:S(2)}) async-start(), calls=%async_computation.6 | async-start | bytes 1146880
  150.7 37.8 %copy-start = (f32[2,18,24,128]{3,2,1,0:T(8,128)}, f32[2,18,24,128]{3,2,1,0:T(8,128)S(1)}, u32[]{:S(2)}) copy-start(f32[2,18,24,128]{3,2,1,0:T(8,128)S(1)} %get-tuple-element.98) | copy-start | bytes 1327108
  305.3 97.4 %reduce-scatter.15.cloned.1.call-start = ((), (), s32[]{:S(2)}) async-start(), calls=%async_computation.7 | async-start | bytes 1146880
  305.5 2.4 copy-start.18
  309.1 1.2 copy-start.16
  312.6 1.2 copy-start.14
  313.8 1.2 copy-start.13
  321.0 11.0 %copy-start.1 = (f32[2,18,24,128]{3,2,1,0:T(8,128)S(1)}, f32[2,18,24,128]{3,2,1,0:T(8,128)}, u32[]{:S(2)}) copy-start(f32[2,18,24,128]{3,2,1,0:T(8,128)} %copy-done) | copy-start | bytes 1327108
  382.1 2.4 copy-start.25
  382.2 97.0 %reduce-scatter.17.cloned.1.call-start = ((), (), s32[]{:S(2)}) async-start(), calls=%async_computation.8 | async-start | bytes 1146880
  384.6 1.2 copy-start.24
  385.8 1.2 copy-start.23
  388.2 1.2 copy-start.22
  389.3 1.2 copy-start.21
  390.5 1.2 copy-start.20
  450.7 8.0 %copy-start.11 = (bf16[2,18,24,512]{3,2,1,0:T(8,128)(2,1)S(1)}, bf16[2,18,24,512]{3,2,1,0:T(8,128)(2,1)}, u32[]{:S(2)}) copy-start(bf16[2,18,24,512]{3,2,1,0:T(8,128)(2,1)} %get-tuple-element.62) | copy-start | bytes 2654212
  458.6 154.6 %reduce-scatter.11.cloned.1.call-start = ((), (), s32[]{:S(2)}) async-start(), calls=%async_computation.5 | async-start | bytes 7962624 | tf_op jit(solution)/shard_map/reduce_scatter | solution.py:163
  459.1 1.2 copy-start.9
  460.2 1.2 copy-start.8
  461.9 1.2 copy-start.7
  462.4 1.3 copy-start.6
  463.6 1.2 copy-start.5
  464.1 1.2 copy-start.4
  471.7 1.3 copy-start.26
  471.7 2.2 copy-start.31
  471.7 2.2 copy-start.32
  473.0 140.2 %copy-start.2 = (f32[3,9,64,128]{3,2,1,0:T(8,128)S(1)}, f32[3,9,64,128]{3,2,1,0:T(8,128)}, u32[]{:S(2)}) copy-start(f32[3,9,64,128]{3,2,1,0:T(8,128)} %param.15) | copy-start | bytes 2654212
  (6 other events, 6.9 us)
Sparse Core Ops, SparseCore 0:
  10.8 67.8 all-gather.1
  305.4 21.1 reduce-scatter.12
  382.3 20.4 reduce-scatter.14
  458.7 20.3 reduce-scatter.16
  483.7 129.4 reduce-scatter.10
where the time goes:
time: 634 us; the launch traced here: 624 us
  blocking collectives  200 us (32%)
  waiting for transfers between devices  198 us (31%)
  matrix products  104 us (16%)
  local copies, waits for them, and re-layouts  77.1 us (12%)
  other arithmetic  29.7 us (5%)
  between operations  14.9 us (2%)
    reduce_scatter x1, waiting for transfers between devices, local(): lax.psum_scatter(weight_terms, 'maps', scatter_dimension=2, tiled=True)  130 us
    unnamed x82, local copies, waits for them, and re-layouts  64.8 us
    psum x3, blocking collectives, local(): lax.psum((jnp.sum(grad_pre * normed, axis=(0, 1, 2)), jnp.sum(grad_pre, a...  62.1 us
    psum x3, blocking collectives, local(): lax.psum((jnp.sum(conv_out * mask_float, axis=(0, 1, 2)), local_count), '...  57.4 us
    psum x3, blocking collectives, local(): lax.psum(jnp.sum(mask_float * centered * centered, axis=(0, 1, 2)), 'maps')  52.1 us
    all_gather x1, waiting for transfers between devices, local(): lax.all_gather(conv_weights.astype(jnp.bfloat16), 'maps', axis=2, tiled=T...  50.9 us
    dot_general x27, matrix products, input_grad_sum(): jnp.einsum('nhwo,co->nhwc', window, kernel[tap_index], preferred_element_...  39.8 us
    dot_general x27, matrix products, apply_kernel(): jnp.einsum('nhwc,co->nhwo', window, kernel[tap_index], preferred_element_...  37.1 us
  transfers between devices with their start and end apart: 5, of which 5 were waited for; matrix products, arithmetic and copies ran while one was open for 8% of the time, Pallas kernels for 0%

commit v1 on v0

v1 whole, which is shorter than its diff:
```python
import functools

import jax
import jax.numpy as jnp
from jax import lax
from jax.experimental import pallas as pl
from jax.experimental.pallas import tpu as pltpu
from jax.sharding import PartitionSpec as P

beta_first = 0.5
beta_second = 0.5
rate_conv = 0.01
rate_norm = 0.2
decay_rate = 0.01
adam_epsilon = 1e-08
norm_epsilon = 1e-05
step_count = 5.0

MESH = pl.DeviceIdType.MESH
F32 = jnp.float32
BF16 = jnp.bfloat16
LANES = 128
PAD = 32


def adamw_update(parameter, gradient, first_moment, second_moment, step_rate):
    first_new = beta_first * first_moment + (1.0 - beta_first) * gradient
    second_new = beta_second * second_moment + (1.0 - beta_second) * gradient * gradient
    first_hat = first_new / (1.0 - beta_first**step_count)
    second_hat = second_new / (1.0 - beta_second**step_count)
    updated = parameter - step_rate * (
        first_hat / (jnp.sqrt(second_hat) + adam_epsilon) + decay_rate * parameter
    )
    return (updated, first_new, second_new)


def steps(low, high, body):
    if high - low <= 8:
        for index in range(low, high):
            body(index)
    else:
        pl.loop(low, high)(body)


def tile8(values):
    rows = values.shape[0]
    return jnp.sum(values.reshape(rows // 8, 8, LANES), axis=0)


def block_kernel(
    sizes,
    x_hbm, mask_hbm, index_hbm, grad_hbm, weight_hbm, gain_hbm, bias_hbm,
    pooled_hbm, image_hbm, wgrad_hbm, ngrad_hbm,
    x_in, mask_in, index_in, grad_in, weight_in, gain_in, bias_in,
    mask_ref, wcat, act, prod, conv, normed, slope, back, spread, zpad, dcat,
    grad_w, part, stat, pair_out, pair_in, far_out, far_in,
    gx_out, gx_in, gz_out, gz_in, pooled_ref, wgrad_ref, ngrad_ref,
    in_sem, out_sem,
    zr_s, zl_s, wx_s, w_r, st_s, st_r, ag_s, ag_r, pr_s, pr_r, fr_s, fr_r,
    gx_s, gx_r, gz_s, gz_r,
):
    maps, chans, layers, taps, nm, height, width = sizes
    line = maps // 2
    m = lax.axis_index("maps")
    c = lax.axis_index("chan")
    a = m // 2
    b = m % 2
    core = c + 1 - 2 * (c % 2)
    far = lax.rem(c + 2, 4)
    across = core + 2 - 4 * (core // 2)
    map_rows = height * width
    pixels = nm * map_rows
    rows_w = wcat.shape[2]
    wide = taps * LANES
    chunk = 6 * width
    chunks = pixels // chunk
    per_map = map_rows // chunk

    def rows_of(i):
        return pl.ds(pl.multiple_of(i * chunk, 16), chunk)

    def padded_rows(i, shift):
        n = i // per_map
        return n, pl.ds(pl.multiple_of((i - n * per_map) * chunk, 8) + (PAD + shift), chunk)

    drains = []

    def remote(src, dst, ssem, rsem, dev):
        return pltpu.make_async_remote_copy(
            src_ref=src, dst_ref=dst, send_sem=ssem, recv_sem=rsem,
            device_id=dev, device_id_type=MESH,
        )

    loads = []
    for i, (src, dst) in enumerate(
        (
            (weight_hbm, weight_in), (x_hbm, x_in), (mask_hbm, mask_in),
            (index_hbm, index_in), (grad_hbm, grad_in), (gain_hbm, gain_in), (bias_hbm, bias_in),
        )
    ):
        cp = pltpu.make_async_copy(src, dst, in_sem.at[i])
        cp.start()
        loads.append(cp)

    barrier = pltpu.get_barrier_semaphore()

    def greet(d):
        peer = lax.rem(m + d, maps)
        pl.semaphore_signal(barrier, inc=1, device_id=(peer, c), device_id_type=MESH)

    steps(1, maps, greet)
    for other in (core, far):
        pl.semaphore_signal(barrier, inc=1, device_id=(m, other), device_id_type=MESH)

    loads[0].wait()
    for l in range(layers):
        for t in range(taps):
            wcat[l, m, :, t * LANES : (t + 1) * LANES] = weight_in[l, t].astype(BF16)

    pl.semaphore_wait(barrier, maps + 1)

    def weight_copy(l, slot, dev, ssem):
        return remote(wcat.at[l, slot], wcat.at[l, slot], ssem, w_r.at[l, slot], dev)

    def gather_own(l, drain=False):
        def go(cond, dev, ssem):
            def run():
                cp = weight_copy(l, m, dev, ssem)
                cp.wait_send() if drain else cp.start()

            if cond is None:
                run()
            else:
                pl.when(cond)(run)

        go(a + 1 < line, (jnp.minimum(m + 2, maps - 1), c), zr_s.at[l, a])
        go(a > 0, (jnp.maximum(m - 2, 0), c), zl_s.at[l, a])
        go(None, (m + 1 - 2 * b, c), wx_s.at[l, a])

    def gather_step(l, s, drain=False):
        def piece(cond, src, onward_cond, onward, onward_sem):
            @pl.when(cond)
            def _():
                slot = src * 2 + b
                if not drain:
                    weight_copy(l, slot, (m, c), wx_s.at[l, src]).wait_recv()

                @pl.when(onward_cond)
                def _():
                    cp = weight_copy(l, slot, (onward, c), onward_sem.at[l, src])
                    cp.wait_send() if drain else cp.start()

                cp = weight_copy(l, slot, (m + 1 - 2 * b, c), wx_s.at[l, src])
                cp.wait_send() if drain else cp.start()

        piece(a >= s, jnp.maximum(a - s, 0), a + 1 < line, jnp.minimum(m + 2, maps - 1), zr_s)
        piece(a + s < line, jnp.minimum(a + s, line - 1), a > 0, jnp.maximum(m - 2, 0), zl_s)

    def gather_finish(l):
        def take(z):
            slot = z * 2 + (1 - b)
            weight_copy(l, slot, (m, c), wx_s.at[l, z]).wait_recv()

        steps(0, line, take)

    def gather_drain(l):
        gather_own(l, True)
        steps(1, line, lambda s: gather_step(l, s, True))

    def stat_copy(e, src, dst_dev, ssem):
        return remote(stat.at[e, src], stat.at[e, src], ssem, st_r.at[e, src], dst_dev)

    def stat_send(e, drain=False):
        def go(d):
            peer = lax.rem(m + d, maps)
            cp = stat_copy(e, m, (peer, c), st_s.at[e, peer])
            cp.wait_send() if drain else cp.start()

        steps(1, maps, go)

    def stat_wait(e):
        def go(d):
            src = lax.rem(m + d, maps)
            stat_copy(e, src, (src, c), st_s.at[e, src]).wait_recv()

        steps(1, maps, go)

    lane_own = pl.ds(pl.multiple_of(c * LANES, LANES), LANES)

    def act_copy(l, n, owner, dev, kind):
        view = act.at[l, pl.ds(n * map_rows, map_rows), pl.ds(pl.multiple_of(owner * LANES, LANES), LANES)]
        return remote(view, view, ag_s.at[l, kind, n], ag_r.at[l, kind, n], dev)

    def act_send(l, n):
        act_copy(l, n, c, (m, far), 1).start()
        act_copy(l, n, c, (m, core), 0).start()

    def act_forward(l, n):
        act_copy(l, n, far, (m, far), 1).wait_recv()
        act_copy(l, n, far, (m, core), 2).start()

    def act_finish(l, n):
        act_copy(l, n, core, (m, core), 0).wait_recv()
        act_copy(l, n, across, (m, core), 2).wait_recv()

    def act_drain(l):
        for n in range(nm):
            act_copy(l, n, c, (m, far), 1).wait_send()
            act_copy(l, n, c, (m, core), 0).wait_send()
            act_copy(l, n, far, (m, core), 2).wait_send()

    gather_own(0)

    loads[2].wait()
    row_of = lax.broadcasted_iota(jnp.int32, (height, width, LANES), 0).reshape(map_rows, LANES)
    col_of = lax.broadcasted_iota(jnp.int32, (height, width, LANES), 1).reshape(map_rows, LANES)
    lane_of = lax.broadcasted_iota(jnp.int32, (map_rows, LANES), 1)
    pick_row = jnp.where(row_of == lane_of, 1.0, 0.0).astype(BF16)[:, :height]
    pick_col = jnp.where(col_of == lane_of, 1.0, 0.0)[:, :width]
    ones = jnp.ones((width, LANES), BF16)
    for n in range(nm):
        valid_n = mask_in[n].astype(F32).astype(BF16)
        spread_rows = jnp.dot(pick_row, valid_n, preferred_element_type=F32) * pick_col
        mask_ref[pl.ds(n * map_rows, map_rows), :] = jnp.dot(
            spread_rows.astype(BF16), ones, preferred_element_type=F32
        )
    loads[1].wait()

    @pl.loop(0, chunks)
    def _(i):
        r = rows_of(i)
        act[0, r, lane_own] = (x_in[r, :].astype(F32) * mask_ref[r, :]).astype(BF16)

    for n in range(nm):
        act_send(0, n)

    for n in range(nm):
        for i in range(3):
            for j in range(3):
                prod[i, j, n, 0:PAD, :] = jnp.zeros((PAD, LANES), F32)
                prod[i, j, n, PAD + map_rows :, :] = jnp.zeros((PAD, LANES), F32)
        zpad[n, 0:PAD, :] = jnp.zeros((PAD, LANES), F32)
        zpad[n, PAD + map_rows :, :] = jnp.zeros((PAD, LANES), F32)

    col_chunk = lax.broadcasted_iota(jnp.int32, (6, width, LANES), 1).reshape(chunk, LANES)
    has_left = jnp.where(col_chunk > 0, 1.0, 0.0)
    has_right = jnp.where(col_chunk < width - 1, 1.0, 0.0)

    loads[3].wait()
    loads[4].wait()
    half_h, half_w = height // 2, width // 2

    @pl.loop(0, nm * half_h)
    def _(i):
        n = i // half_h
        h = i - n * half_h
        kept = index_in[n, h]
        value = grad_in[n, h].astype(F32)
        base = n * map_rows + 2 * h * width
        for r in range(2):
            for s in range(2):
                spread[pl.ds(base + r * width + s, half_w, stride=2), :] = jnp.where(
                    kept == 2 * r + s, value, 0.0
                )

    steps(1, line, lambda s: gather_step(0, s))
    for n in range(nm):
        act_forward(0, n)
    gather_finish(0)
    for n in range(nm):
        act_finish(0, n)
    loads[5].wait()
    loads[6].wait()

    for l in range(layers):
        if l > 0:
            steps(1, line, lambda s: gather_step(l, s))
            gather_finish(l)

        @pl.loop(0, 3)
        def _(i):
            cols = pl.ds(pl.multiple_of(i * (3 * LANES), LANES), 3 * LANES)
            w = wcat[l, :, :, cols].reshape(maps * rows_w, 3 * LANES)
            for n in range(nm):
                out = jnp.dot(
                    act[l, pl.ds(n * map_rows, map_rows), :], w, preferred_element_type=F32
                )
                for j in range(3):
                    prod[i, j, n, PAD : PAD + map_rows, :] = out[:, j * LANES : (j + 1) * LANES]

        def conv_chunk(i, carry):
            total, count = carry
            r = rows_of(i)
            value = None
            for j in range(3):
                side = None
                for k in range(3):
                    n, pr = padded_rows(i, width * (k - 1) + (j - 1))
                    term = prod[k, j, n, pr, :]
                    side = term if side is None else side + term
                if j == 0:
                    side = side * has_left
                if j == 2:
                    side = side * has_right
                value = side if value is None else value + side
            conv[r, :] = value
            valid = mask_ref[r, :]
            return total + tile8(value * valid), count + tile8(valid)

        zero8 = jnp.zeros((8, LANES), F32)
        total, count = lax.fori_loop(0, chunks, conv_chunk, (zero8, zero8))
        total = jnp.sum(total, axis=0, keepdims=True)
        count = jnp.sum(count, axis=0, keepdims=True)
        mean = total / jnp.maximum(count, 1.0)

        def dev_chunk(i, carry):
            r = rows_of(i)
            delta = conv[r, :] - mean
            return carry + tile8(delta * delta * mask_ref[r, :])

        spread_sum = jnp.sum(lax.fori_loop(0, chunks, dev_chunk, zero8), axis=0, keepdims=True)
        stat[l, m] = jnp.concatenate(
            [total, spread_sum, count, mean, jnp.zeros((4, LANES), F32)], axis=0
        )
        stat_send(l)
        if l + 1 < layers:
            gather_own(l + 1)
        stat_wait(l)

        def add_totals(s, carry):
            block = stat[l, s]
            return carry[0] + block[0:1, :], carry[1] + block[2:3, :]

        zero1 = jnp.zeros((1, LANES), F32)
        total, count = lax.fori_loop(0, maps, add_totals, (zero1, zero1))
        center = total / count

        def add_spread(s, carry):
            block = stat[l, s]
            delta = block[3:4, :] - center
            return carry + block[1:2, :] + block[2:3, :] * delta * delta

        variance = lax.fori_loop(0, maps, add_spread, zero1) / count
        inv_std = lax.rsqrt(variance + norm_epsilon)
        gain = gain_in[l : l + 1, :]
        bias = bias_in[l : l + 1, :]
        if l == 0:
            count_all = count
            scales = []
        scales.append(gain * inv_std)

        for n in range(nm):

            @pl.loop(n * per_map, (n + 1) * per_map)
            def _(i):
                r = rows_of(i)
                unit = (conv[r, :] - center) * inv_std
                pre = gain * unit + bias
                sigma = 1.0 / (1.0 + jnp.exp(-pre))
                valid = mask_ref[r, :]
                result = pre * sigma * valid
                normed[l, r, :] = unit
                slope[l, r, :] = sigma * (1.0 + pre * (1.0 - sigma)) * valid
                if l + 1 < layers:
                    act[l + 1, r, lane_own] = result.astype(BF16)
                else:
                    back[r, :] = result

            if l + 1 < layers:
                act_send(l + 1, n)
        if l + 1 < layers:
            for n in range(nm):
                act_forward(l + 1, n)
            for n in range(nm):
                act_finish(l + 1, n)

    @pl.loop(0, nm * half_h)
    def _(i):
        n = i // half_h
        h = i - n * half_h
        kept = index_in[n, h]
        base = n * map_rows + 2 * h * width
        total = jnp.zeros((half_w, LANES), F32)
        for r in range(2):
            for s in range(2):
                total = total + jnp.where(
                    kept == 2 * r + s, back[pl.ds(base + r * width + s, half_w, stride=2), :], 0.0
                )
        pooled_ref[n, h] = total.astype(BF16)

    outs = [pltpu.make_async_copy(pooled_ref, pooled_hbm, out_sem.at[0])]
    outs[0].start()

    def gx_copy(l, z):
        return remote(gx_out.at[l, z], gx_in.at[l, z], gx_s.at[l, z], gx_r.at[l, z], (m + 1 - 2 * b, c))

    def gz_send(l, z):
        return remote(gz_out.at[l, z], gz_in.at[l, a], gz_s.at[l, z], gz_r.at[l, a], (z * 2 + b, c))

    def gz_recv(l, z):
        return remote(gz_out.at[l, z], gz_in.at[l, z], gz_s.at[l, z], gz_r.at[l, z], (z * 2 + b, c))

    def shard(l, slot):
        return grad_w[l, pl.ds(pl.multiple_of(slot * rows_w, 8), rows_w), :]

    def scatter_x(l):
        def go(d):
            z = lax.rem(a + d, line)
            gx_out[l, z] = shard(l, z * 2 + 1 - b).astype(BF16)
            gx_copy(l, z).start()

        steps(1, line + 1, go)

    def scatter_z(l):
        def go(d):
            z = lax.rem(a + d, line)
            gx_copy(l, z).wait_recv()
            value = shard(l, z * 2 + b) + gx_in[l, z].astype(F32)
            gz_out[l, z] = value.astype(BF16)
            gz_send(l, z).start()

        steps(1, line, go)
        gx_copy(l, a).wait_recv()
        part_w = shard(l, m) + gx_in[l, a].astype(F32)
        for t in range(taps):
            wgrad_ref[l, t] = part_w[:, t * LANES : (t + 1) * LANES]

    def scatter_finish(l):
        def go(d):
            z = lax.rem(a + d, line)
            gz_recv(l, z).wait_recv()
            for t in range(taps):
                wgrad_ref[l, t] += gz_in[l, z, :, t * LANES : (t + 1) * LANES].astype(F32)

        steps(1, line, go)
        cp = pltpu.make_async_copy(wgrad_ref.at[l], wgrad_hbm.at[l], out_sem.at[3 + l])
        cp.start()
        outs.append(cp)

    def scatter_drain(l):
        def go(d):
            z = lax.rem(a + d, line)
            gx_copy(l, z).wait_send()

        steps(1, line + 1, go)

        def go2(d):
            z = lax.rem(a + d, line)
            gz_send(l, z).wait_send()

        steps(1, line, go2)

    half = 2 * LANES
    own_half = (c // 2) * half
    other_half = half - own_half
    lane_in_half = pl.ds(pl.multiple_of((c % 2) * LANES, LANES), LANES)
    lane_out_half = pl.ds(pl.multiple_of((1 - c % 2) * LANES, LANES), LANES)

    def pair_copy(l, h, n):
        return remote(
            pair_out.at[l, h, pl.ds(n * map_rows, map_rows), :],
            pair_in.at[l, h, pl.ds(n * map_rows, map_rows), :],
            pr_s.at[l, h, n], pr_r.at[l, h, n], (m, core),
        )

    def far_copy(l, n):
        return remote(
            far_out.at[l, pl.ds(n * map_rows, map_rows), :],
            far_in.at[l, pl.ds(n * map_rows, map_rows), :],
            fr_s.at[l, n], fr_r.at[l, n], (m, far),
        )

    for l in reversed(range(layers)):
        e = layers + l
        source = spread if l == layers - 1 else back

        def slope_chunk(i, carry):
            r = rows_of(i)
            value = source[r, :] * slope[l, r, :]
            conv[r, :] = value
            return carry[0] + tile8(value * normed[l, r, :]), carry[1] + tile8(value)

        zero8 = jnp.zeros((8, LANES), F32)
        gain_sum, bias_sum = lax.fori_loop(0, chunks, slope_chunk, (zero8, zero8))
        stat[e, m] = jnp.concatenate(
            [
                jnp.sum(gain_sum, axis=0, keepdims=True),
                jnp.sum(bias_sum, axis=0, keepdims=True),
                jnp.zeros((6, LANES), F32),
            ],
            axis=0,
        )
        stat_send(e)
        if l + 1 < layers:
            scatter_x(l + 1)
        stat_wait(e)

        def add_sums(s, carry):
            return carry + stat[e, s]

        sums = lax.fori_loop(0, maps, add_sums, jnp.zeros((8, LANES), F32))
        ngrad_ref[l] = sums[0:2, :]
        gain_grad = sums[0:1, :]
        bias_grad = sums[1:2, :]
        scale = scales[l]

        @pl.loop(0, chunks)
        def _(i):
            r = rows_of(i)
            value = (
                mask_ref[r, :]
                * scale
                * (conv[r, :] - (bias_grad + normed[l, r, :] * gain_grad) / count_all)
            )
            n, pr = padded_rows(i, 0)
            zpad[n, pr, :] = value

        @pl.loop(0, chunks)
        def _(i):
            r = rows_of(i)
            for k in range(3):
                for j in range(3):
                    n, pr = padded_rows(i, -(width * (k - 1) + (j - 1)))
                    term = zpad[n, pr, :]
                    if j == 0:
                        term = term * has_right
                    if j == 2:
                        term = term * has_left
                    t = 3 * k + j
                    dcat[r, t * LANES : (t + 1) * LANES] = term.astype(BF16)

        def half_grad(n, start):
            w = wcat[l].reshape(maps * rows_w, wide) if False else None
            slots = maps // 2
            first = (start // half) * slots
            w = wcat[l, pl.ds(first, slots), :, :].reshape(half, wide)
            return lax.dot_general(
                dcat[pl.ds(n * map_rows, map_rows), :], w, (((1,), (1,)), ((), ())),
                preferred_element_type=F32,
            )

        for h, start in ((0, other_half), (1, own_half)):
            for n in range(nm):
                r = pl.ds(n * map_rows, map_rows)
                part[h, r, :] = half_grad(n, start)
                pair_out[l, h, r, :] = part[h, r, lane_out_half].astype(BF16)
                pair_copy(l, h, n).start()
            if h == 0:
                for n in range(nm):
                    r = pl.ds(n * map_rows, map_rows)
                    pair_copy(l, h, n).wait_recv()
                    far_out[l, r, :] = (
                        part[h, r, lane_in_half] + pair_in[l, h, r, :].astype(F32)
                    ).astype(BF16)
                    far_copy(l, n).start()
        if l + 1 < layers:
            scatter_z(l + 1)

        slots = 2
        tile = slots * rows_w if rows_w * slots >= LANES else maps * rows_w // 4

        @pl.loop(0, (maps * rows_w) // tile)
        def _(i):
            cols = pl.ds(pl.multiple_of(i * tile, LANES), tile)
            grad_w[l, pl.ds(pl.multiple_of(i * tile, LANES), tile), :] = lax.dot_general(
                act[l, :, cols], dcat[...], (((0,), (0,)), ((), ())), preferred_element_type=F32
            )

        for n in range(nm):
            r = pl.ds(n * map_rows, map_rows)
            pair_copy(l, 1, n).wait_recv()
            far_copy(l, n).wait_recv()

            @pl.loop(n * per_map, (n + 1) * per_map)
            def _(i):
                r = rows_of(i)
                value = (
                    part[1, r, lane_in_half]
                    + pair_in[l, 1, r, :].astype(F32)
                    + far_in[l, r, :].astype(F32)
                )
                if l == 0:
                    value = value * mask_ref[r, :]
                back[r, :] = value

        if l + 1 < layers:
            scatter_finish(l + 1)

    cp = pltpu.make_async_copy(back, image_hbm, out_sem.at[1])
    cp.start()
    outs.append(cp)
    cp = pltpu.make_async_copy(ngrad_ref, ngrad_hbm, out_sem.at[2])
    cp.start()
    outs.append(cp)
    scatter_x(0)
    scatter_z(0)
    scatter_finish(0)

    for l in range(layers):
        gather_drain(l)
        act_drain(l)
        stat_send(l, True)
        stat_send(layers + l, True)
        scatter_drain(l)
        for n in range(nm):
            pair_copy(l, 0, n).wait_send()
            pair_copy(l, 1, n).wait_send()
            far_copy(l, n).wait_send()
    for cp in outs:
        cp.wait()


def block_call(maps, chans, x, mask, index, grad, weights, gain, bias):
    nm, height, width, lanes = x.shape
    layers, taps, rows_w, _ = weights.shape
    pixels = nm * height * width
    line = maps // 2
    wide = taps * LANES
    channels = chans * LANES
    map_rows = height * width
    sizes = (maps, chans, layers, taps, nm, height, width)
    vm = pltpu.VMEM
    dma = pltpu.SemaphoreType.DMA
    any_spec = pl.BlockSpec(memory_space=pl.ANY)
    scratch = [
        vm((pixels, LANES), BF16), vm(mask.shape, jnp.int32), vm(index.shape, jnp.int32),
        vm(grad.shape, BF16), vm(weights.shape, F32), vm(gain.shape, F32), vm(bias.shape, F32),
        vm((pixels, LANES), F32),
        vm((layers, maps, rows_w, wide), BF16),
        vm((layers, pixels, channels), BF16),
        vm((3, 3, nm, map_rows + 2 * PAD, LANES), F32),
        vm((pixels, LANES), F32),
        vm((layers, pixels, LANES), F32),
        vm((layers, pixels, LANES), F32),
        vm((pixels, LANES), F32),
        vm((pixels, LANES), F32),
        vm((nm, map_rows + 2 * PAD, LANES), F32),
        vm((pixels, wide), BF16),
        vm((layers, channels, wide), F32),
        vm((2, pixels, 2 * LANES), F32),
        vm((2 * layers, maps, 8, LANES), F32),
        vm((layers, 2, pixels, LANES), BF16), vm((layers, 2, pixels, LANES), BF16),
        vm((layers, pixels, LANES), BF16), vm((layers, pixels, LANES), BF16),
        vm((layers, line, rows_w, wide), BF16), vm((layers, line, rows_w, wide), BF16),
        vm((layers, line, rows_w, wide), BF16), vm((layers, line, rows_w, wide), BF16),
        vm((nm, height // 2, width // 2, LANES), BF16),
        vm((layers, taps, rows_w, LANES), F32),
        vm((layers, 2, LANES), F32),
        dma((7,)), dma((3 + layers,)),
        dma((layers, line)), dma((layers, line)), dma((layers, line)), dma((layers, maps)),
        dma((2 * layers, maps)), dma((2 * layers, maps)),
        dma((layers, 3, nm)), dma((layers, 3, nm)),
        dma((layers, 2, nm)), dma((layers, 2, nm)),
        dma((layers, nm)), dma((layers, nm)),
        dma((layers, line)), dma((layers, line)), dma((layers, line)), dma((layers, line)),
    ]
    return pl.pallas_call(
        functools.partial(block_kernel, sizes),
        out_shape=(
            jax.ShapeDtypeStruct((nm, height // 2, width // 2, LANES), BF16),
            jax.ShapeDtypeStruct((pixels, LANES), F32),
            jax.ShapeDtypeStruct((layers, taps, rows_w, LANES), F32),
            jax.ShapeDtypeStruct((layers, 2, LANES), F32),
        ),
        in_specs=[any_spec] * 7,
        out_specs=(any_spec,) * 4,
        scratch_shapes=scratch,
        compiler_params=pltpu.CompilerParams(
            collective_id=0, has_side_effects=True, vmem_limit_bytes=60 << 20
        ),
    )(x.reshape(pixels, LANES), mask, index, grad, weights, gain, bias)


def local(
    maps, chans,
    input_maps, valid_mask, pool_index, out_grad, conv_weights, weight_first, weight_second,
    norm_gain, norm_bias, norm_first, norm_second,
):
    pooled, image, weight_grads, norm_grads = block_call(
        maps, chans, input_maps, valid_mask, pool_index, out_grad, conv_weights, norm_gain, norm_bias
    )
    image_grad = image.reshape(input_maps.shape)
    new_weights, new_weight_first, new_weight_second = adamw_update(
        conv_weights, weight_grads, weight_first, weight_second, rate_conv
    )
    norm_values = jnp.stack([norm_gain, norm_bias], axis=1)
    new_norms, new_norm_first, new_norm_second = adamw_update(
        norm_values, norm_grads, norm_first, norm_second, rate_norm
    )
    return (
        pooled,
        image_grad,
        weight_grads,
        new_weight_first,
        new_weight_second,
        new_weights,
        new_weights.astype(BF16),
        norm_grads,
        new_norm_first,
        new_norm_second,
        new_norms,
    )


def solution(mesh):
    return jax.shard_map(
        functools.partial(local, mesh.shape["maps"], mesh.shape["chan"]),
        mesh=mesh,
        in_specs=(
            P("maps", None, None, "chan"),
            P("maps", None, None),
            P("maps", None, None, "chan"),
            P("maps", None, None, "chan"),
            P(None, None, "maps", "chan"),
            P(None, None, "maps", "chan"),
            P(None, None, "maps", "chan"),
            P(None, "chan"),
            P(None, "chan"),
            P(None, None, "chan"),
            P(None, None, "chan"),
        ),
        out_specs=(
            P("maps", None, None, "chan"),
            P("maps", None, None, "chan"),
            P(None, None, "maps", "chan"),
            P(None, None, "maps", "chan"),
            P(None, None, "maps", "chan"),
            P(None, None, "maps", "chan"),
            P(None, None, "maps", "chan"),
            P(None, None, "chan"),
            P(None, None, "chan"),
            P(None, None, "chan"),
            P(None, None, "chan"),
        ),
        check_vma=False,
    )
```

time: 634 us -> 179 us (0.28); the launches traced: 624 us -> 179 us
  blocking collectives: 200 us -> 0 us
  waiting for transfers between devices: 198 us -> 0 us
  Pallas kernels: 0 us -> 166 us
  matrix products: 104 us -> 0 us
  local copies, waits for them, and re-layouts: 77.1 us -> 7.54 us
  other arithmetic: 29.7 us -> 4.32 us
  between operations: 14.9 us -> 0.75 us
    psum x9 -> x0, blocking collectives: 171 us -> none  [the longest x3 62.1 us: local(): lax.psum((jnp.sum(grad_pre * normed, axis=(0, 1, 2)), jnp.sum(grad_pre, a...]
    pallas_call x0 -> x1, Pallas kernels: none -> 166 us  [block_call(): pl.pallas_call(functools.partial(block_kernel, sizes), out_shape=(jax.Sha...]
    reduce_scatter x1 -> x0, waiting for transfers between devices: 130 us -> none  [local(): lax.psum_scatter(weight_terms, 'maps', scatter_dimension=2, tiled=True)]
    dot_general x81 -> x0, matrix products: 104 us -> none  [the longest x27 39.8 us: input_grad_sum(): jnp.einsum('nhwo,co->nhwc', window, kernel[tap_index], preferred_element_...]
    unnamed x82 -> x27, local copies, waits for them, and re-layouts: 64.8 us -> 7.54 us
    all_gather x1 -> x0, waiting for transfers between devices: 50.9 us -> none  [local(): lax.all_gather(conv_weights.astype(jnp.bfloat16), 'maps', axis=2, tiled=T...]
    all_gather x3 -> x0, blocking collectives: 28.4 us -> none  [local(): gathered = lax.all_gather(activation, 'chan', axis=3, tiled=True)]
    unnamed x8 -> x0, waiting for transfers between devices: 17.4 us -> none
  transfers between devices with their start and end apart: 5 -> 0, of which waited for: 5 -> 0; matrix products, arithmetic and copies ran while one was open for 8% -> 0% of each run, Pallas kernels for 0% -> 0%
where the time goes in v1:
time: 179 us
  Pallas kernels  166 us (93%)
  local copies, waits for them, and re-layouts  7.54 us (4%)
  other arithmetic  4.32 us (2%)
    pallas_call x1, Pallas kernels, block_call(): pl.pallas_call(functools.partial(block_kernel, sizes), out_shape=(jax.Sha...  166 us
    unnamed x27, local copies, waits for them, and re-layouts  7.54 us
    convert_element_type x1, other arithmetic, local(): new_weights.astype(BF16)  3.71 us

profile of v1, /device:TPU:0, one launch (start us, length us, event | category | flops | bytes accessed | tf_op | source)
XLA Modules:
  0.0 178.7 jit_solution(2983950009674283904)
XLA Ops:
  0.6 0.0 copy-start.4
  0.7 1.3 copy.22.mask_hbm
  2.0 0.0 copy-start.1
  2.0 0.0 copy-start.2
  2.0 1.7 copy.23.index_hbm
  3.7 0.0 copy-done.4
  3.7 0.6 copy.24.grad_hbm
  4.4 166.1 %shard_map.194 = (bf16[2,9,12,128]{3,2,1,0:T(8,128)(2,1)}, f32[864,128]{1,0:T(8,128)}, f32[3,9,64,128]{3,2,1,0:T(8,128)}, f32[3,2,128]{2,1,0:T(2,128)}) custom-call(bf16[864,128]{1,0:T(8,128)(2,1)} %bitcast.3, s32[2,18,24]{2,1,0:T(8,128)} %copy.22.mask_hbm, s32[2,9,12,128]{3,2,1,0:T(8,128)} %copy.23.index_hbm, bf16[2,9,12,128]{3,2,1,0:T(8,128)(2,1)} %copy.24.grad_hbm, ...), custom_call_target="tpu_custom_call" | custom-call | tf_op jit(solution)/shard_map/pallas_call | solution.py:657
  170.5 1.5 copy.25
  172.0 0.0 copy-done.1
  172.0 0.0 copy-done.2
  172.0 0.0 copy-start.6
  172.0 0.0 copy-start.7
  172.0 0.0 copy-start.5
  172.0 0.0 copy-start.8
  172.1 0.0 copy-start.9
  172.1 0.0 copy-start.3
  172.1 3.7 %fusion.3 = (bf16[3,9,64,128]{3,2,1,0:T(8,128)(2,1)}, f32[3,9,64,128]{3,2,1,0:T(8,128)}, f32[3,9,64,128]{3,2,1,0:T(8,128)}, f32[3,9,64,128]{3,2,1,0:T(8,128)}) fusion(f32[3,9,64,128]{3,2,1,0:T(8,128)S(1)} %copy-done.1, f32[3,9,64,128]{3,2,1,0:T(8,128)} %get-tuple-element.50, f32[3,9,64,128]{3,2,1,0:T(8,128)S(1)} %copy-done.2, f32[3,9,64,128]{3,2,1,0:T(8,128)} %param.16), kind=kLoop, calls=%fused_computation.9 | loop fusion | flops 3317760 | bytes 6635520 | tf_op jit(solution)/shard_map/convert_element_type | solution.py:697
  175.8 0.0 copy-start
  175.8 0.0 copy-done.6
  175.8 0.0 copy-done.7
  175.8 0.0 copy-done.5
  175.8 0.0 copy-done.8
  175.8 0.0 copy-done.9
  175.9 0.6 multiply_subtract_fusion.1
  176.5 0.0 copy-done.3
  176.5 0.8 copy.29
  177.2 0.0 copy-done
  177.2 0.9 copy.30
  178.1 0.6 copy.31
  (2 shorter events, 0.0 us)
Async XLA Ops:
  0.6 3.1 %copy-start.4 = (bf16[2,9,12,128]{3,0,2,1:T(2,128)(2,1)S(1)}, bf16[2,9,12,128]{3,0,2,1:T(2,128)(2,1)}, u32[]{:S(2)}) copy-start(bf16[2,9,12,128]{3,0,2,1:T(2,128)(2,1)} %param.14) | copy-start | bytes 165892
  2.0 170.0 %copy-start.1 = (f32[3,9,64,128]{3,2,1,0:T(8,128)S(1)}, f32[3,9,64,128]{3,2,1,0:T(8,128)}, u32[]{:S(2)}) copy-start(f32[3,9,64,128]{3,2,1,0:T(8,128)} %weight_hbm.1) | copy-start | bytes 2654212
  2.0 170.0 %copy-start.2 = (f32[3,9,64,128]{3,2,1,0:T(8,128)S(1)}, f32[3,9,64,128]{3,2,1,0:T(8,128)}, u32[]{:S(2)}) copy-start(f32[3,9,64,128]{3,2,1,0:T(8,128)} %param.17) | copy-start | bytes 2654212
  172.0 3.8 %copy-start.6 = (f32[3,128]{1,0:T(4,128)S(1)}, f32[3,128]{1,0:T(4,128)}, u32[]{:S(2)}) copy-start(f32[3,128]{1,0:T(4,128)} %bias_hbm.1) | copy-start | bytes 4612
  172.0 3.8 %copy-start.7 = (f32[3,128]{1,0:T(4,128)S(1)}, f32[3,128]{1,0:T(4,128)}, u32[]{:S(2)}) copy-start(f32[3,128]{1,0:T(4,128)} %gain_hbm.1) | copy-start | bytes 4612
  172.0 3.8 %copy-start.5 = (f32[3,2,128]{2,1,0:T(2,128)S(1)}, f32[3,2,128]{2,1,0:T(2,128)}, u32[]{:S(2)}) copy-start(f32[3,2,128]{2,1,0:T(2,128)} %get-tuple-element.55) | copy-start | bytes 9220
  172.0 3.8 %copy-start.8 = (f32[3,2,128]{2,1,0:T(2,128)S(1)}, f32[3,2,128]{2,1,0:T(2,128)}, u32[]{:S(2)}) copy-start(f32[3,2,128]{2,1,0:T(2,128)} %param.21) | copy-start | bytes 9220
  172.1 3.8 %copy-start.9 = (f32[3,2,128]{2,1,0:T(2,128)S(1)}, f32[3,2,128]{2,1,0:T(2,128)}, u32[]{:S(2)}) copy-start(f32[3,2,128]{2,1,0:T(2,128)} %param.20) | copy-start | bytes 9220
  172.1 4.4 %copy-start.3 = (f32[864,128]{1,0:T(8,128)S(1)}, f32[864,128]{1,0:T(8,128)}, u32[]{:S(2)}) copy-start(f32[864,128]{1,0:T(8,128)} %get-tuple-element.16) | copy-start | bytes 1327108
  175.8 1.4 copy-start

commit v2 on v1

--- a/solution.py
+++ b/solution.py
@@ -42,6 +42,14 @@
         pl.loop(low, high)(body)
 
 
+scope = jax.named_scope
+
+
+def run(tasks, amount=None):
+    for _ in range(len(tasks) if amount is None else min(amount, len(tasks))):
+        tasks.pop(0)()
+
+
 def tile8(values):
     rows = values.shape[0]
     return jnp.sum(values.reshape(rows // 8, 8, LANES), axis=0)
@@ -52,7 +60,7 @@
     x_hbm, mask_hbm, index_hbm, grad_hbm, weight_hbm, gain_hbm, bias_hbm,
     pooled_hbm, image_hbm, wgrad_hbm, ngrad_hbm,
     x_in, mask_in, index_in, grad_in, weight_in, gain_in, bias_in,
-    mask_ref, wcat, act, prod, conv, normed, slope, back, spread, zpad, dcat,
+    mask_ref, wcat, act, prod, conv, normed, slope, back, result_ref, spread, pool32, zpad, dcat,
     grad_w, part, stat, pair_out, pair_in, far_out, far_in,
     gx_out, gx_in, gz_out, gz_in, pooled_ref, wgrad_ref, ngrad_ref,
     in_sem, out_sem,
@@ -119,53 +127,76 @@
 
     pl.semaphore_wait(barrier, maps + 1)
 
-    def weight_copy(l, slot, dev, ssem):
-        return remote(wcat.at[l, slot], wcat.at[l, slot], ssem, w_r.at[l, slot], dev)
+    pieces = w_r.shape[2]
+    piece_rows = rows_w // pieces
+
+    def weight_copy(l, slot, g, dev, ssem):
+        view = wcat.at[l, slot, pl.ds(g * piece_rows, piece_rows)]
+        return remote(view, view, ssem, w_r.at[l, slot, g], dev)
 
     def gather_own(l, drain=False):
-        def go(cond, dev, ssem):
-            def run():
-                cp = weight_copy(l, m, dev, ssem)
+        def go(cond, g, dev, ssem):
+            def send():
+                cp = weight_copy(l, m, g, dev, ssem)
                 cp.wait_send() if drain else cp.start()
 
             if cond is None:
-                run()
+                send()
             else:
-                pl.when(cond)(run)
-
-        go(a + 1 < line, (jnp.minimum(m + 2, maps - 1), c), zr_s.at[l, a])
-        go(a > 0, (jnp.maximum(m - 2, 0), c), zl_s.at[l, a])
-        go(None, (m + 1 - 2 * b, c), wx_s.at[l, a])
-
-    def gather_step(l, s, drain=False):
+                pl.when(cond)(send)
+
+        for g in range(pieces):
+            go(a + 1 < line, g, (jnp.minimum(m + 2, maps - 1), c), zr_s.at[l, a, g])
+            go(a > 0, g, (jnp.maximum(m - 2, 0), c), zl_s.at[l, a, g])
+            go(None, g, (m + 1 - 2 * b, c), wx_s.at[l, a, g])
+
+    def gather_step(l, s, g, drain=False):
         def piece(cond, src, onward_cond, onward, onward_sem):
             @pl.when(cond)
             def _():
                 slot = src * 2 + b
                 if not drain:
-                    weight_copy(l, slot, (m, c), wx_s.at[l, src]).wait_recv()
+                    weight_copy(l, slot, g, (m, c), wx_s.at[l, src, g]).wait_recv()
 
                 @pl.when(onward_cond)
                 def _():
-                    cp = weight_copy(l, slot, (onward, c), onward_sem.at[l, src])
+                    cp = weight_copy(l, slot, g, (onward, c), onward_sem.at[l, src, g])
                     cp.wait_send() if drain else cp.start()
 
-                cp = weight_copy(l, slot, (m + 1 - 2 * b, c), wx_s.at[l, src])
+                cp = weight_copy(l, slot, g, (m + 1 - 2 * b, c), wx_s.at[l, src, g])
                 cp.wait_send() if drain else cp.start()
 
         piece(a >= s, jnp.maximum(a - s, 0), a + 1 < line, jnp.minimum(m + 2, maps - 1), zr_s)
         piece(a + s < line, jnp.minimum(a + s, line - 1), a > 0, jnp.maximum(m - 2, 0), zl_s)
 
+    def gather_tasks(l, drain=False):
+        if line <= 8:
+            return [
+                functools.partial(gather_step, l, s, g, drain)
+                for s in range(1, line)
+                for g in range(pieces)
+            ]
+
+        def everything():
+            def go(s):
+                for g in range(pieces):
+                    gather_step(l, s, g, drain)
+
+            steps(1, line, go)
+
+        return [everything]
+
     def gather_finish(l):
         def take(z):
-            slot = z * 2 + (1 - b)
-            weight_copy(l, slot, (m, c), wx_s.at[l, z]).wait_recv()
+            for g in range(pieces):
+                slot = z * 2 + (1 - b)
+                weight_copy(l, slot, g, (m, c), wx_s.at[l, z, g]).wait_recv()
 
         steps(0, line, take)
 
     def gather_drain(l):
         gather_own(l, True)
-        steps(1, line, lambda s: gather_step(l, s, True))
+        run(gather_tasks(l, True))
 
     def stat_copy(e, src, dst_dev, ssem):
         return remote(stat.at[e, src], stat.at[e, src], ssem, st_r.at[e, src], dst_dev)
@@ -212,18 +243,19 @@
     gather_own(0)
 
     loads[2].wait()
-    row_of = lax.broadcasted_iota(jnp.int32, (height, width, LANES), 0).reshape(map_rows, LANES)
-    col_of = lax.broadcasted_iota(jnp.int32, (height, width, LANES), 1).reshape(map_rows, LANES)
-    lane_of = lax.broadcasted_iota(jnp.int32, (map_rows, LANES), 1)
-    pick_row = jnp.where(row_of == lane_of, 1.0, 0.0).astype(BF16)[:, :height]
-    pick_col = jnp.where(col_of == lane_of, 1.0, 0.0)[:, :width]
-    ones = jnp.ones((width, LANES), BF16)
+    col_of = lax.broadcasted_iota(jnp.int32, (width, width), 0)
+    diagonal = col_of == lax.broadcasted_iota(jnp.int32, (width, width), 1)
     for n in range(nm):
-        valid_n = mask_in[n].astype(F32).astype(BF16)
-        spread_rows = jnp.dot(pick_row, valid_n, preferred_element_type=F32) * pick_col
-        mask_ref[pl.ds(n * map_rows, map_rows), :] = jnp.dot(
-            spread_rows.astype(BF16), ones, preferred_element_type=F32
-        )
+
+        @pl.loop(0, height)
+        def _(h):
+            line_n = jnp.broadcast_to(mask_in[h, n : n + 1, :].astype(F32), (width, width))
+            r = pl.ds(pl.multiple_of(n * map_rows + h * width, 8), width)
+            conv[r, 0:width] = jnp.where(diagonal, line_n, 0.0)
+
+    mask_ref[...] = jnp.dot(
+        conv[:, 0:width].astype(BF16), jnp.ones((width, LANES), BF16), preferred_element_type=F32
+    )
     loads[1].wait()
 
     @pl.loop(0, chunks)
@@ -250,33 +282,33 @@
     loads[4].wait()
     half_h, half_w = height // 2, width // 2
 
-    @pl.loop(0, nm * half_h)
-    def _(i):
-        n = i // half_h
-        h = i - n * half_h
-        kept = index_in[n, h]
-        value = grad_in[n, h].astype(F32)
-        base = n * map_rows + 2 * h * width
-        for r in range(2):
-            for s in range(2):
-                spread[pl.ds(base + r * width + s, half_w, stride=2), :] = jnp.where(
-                    kept == 2 * r + s, value, 0.0
-                )
-
-    steps(1, line, lambda s: gather_step(0, s))
+    @pl.loop(0, half_h)
+    def _(h):
+        pool32[...] = grad_in[h].astype(F32)
+        for n in range(nm):
+            pick = pl.ds(n, half_w, stride=nm)
+            kept = index_in[h, pick, :]
+            value = pool32[pick, :]
+            base = n * map_rows + 2 * h * width
+            for r in range(2):
+                for s in range(2):
+                    spread[pl.ds(base + r * width + s, half_w, stride=2), :] = jnp.where(
+                        kept == 2 * r + s, value, 0.0
+                    )
+
+    tasks = gather_tasks(0)
+    with scope("gather0"):
+        run(tasks)
     for n in range(nm):
         act_forward(0, n)
-    gather_finish(0)
+    with scope("gather0_end"):
+        gather_finish(0)
     for n in range(nm):
         act_finish(0, n)
     loads[5].wait()
     loads[6].wait()
 
     for l in range(layers):
-        if l > 0:
-            steps(1, line, lambda s: gather_step(l, s))
-            gather_finish(l)
-
         @pl.loop(0, 3)
         def _(i):
             cols = pl.ds(pl.multiple_of(i * (3 * LANES), LANES), 3 * LANES)
@@ -323,9 +355,12 @@
             [total, spread_sum, count, mean, jnp.zeros((4, LANES), F32)], axis=0
         )
         stat_send(l)
+        tasks = []
         if l + 1 < layers:
             gather_own(l + 1)
-        stat_wait(l)
+            tasks = gather_tasks(l + 1)
+        with scope("stat_wait"):
+            stat_wait(l)
 
         def add_totals(s, carry):
             block = stat[l, s]
@@ -364,32 +399,49 @@
                 if l + 1 < layers:
                     act[l + 1, r, lane_own] = result.astype(BF16)
                 else:
-                    back[r, :] = result
+                    result_ref[r, :] = result
 
             if l + 1 < layers:
                 act_send(l + 1, n)
         if l + 1 < layers:
+            with scope("gather_a"):
+                run(tasks, pieces + 1)
             for n in range(nm):
-                act_forward(l + 1, n)
+                with scope("act_forward"):
+                    act_forward(l + 1, n)
+                with scope("gather_b"):
+                    run(tasks, 1)
+            with scope("gather_c"):
+                run(tasks)
+            with scope("act_finish"):
+                for n in range(nm):
+                    act_finish(l + 1, n)
+            with scope("gather_end"):
+                gather_finish(l + 1)
+
+    def pool():
+        @pl.loop(0, half_h)
+        def _(h):
             for n in range(nm):
-                act_finish(l + 1, n)
-
-    @pl.loop(0, nm * half_h)
-    def _(i):
-        n = i // half_h
-        h = i - n * half_h
-        kept = index_in[n, h]
-        base = n * map_rows + 2 * h * width
-        total = jnp.zeros((half_w, LANES), F32)
-        for r in range(2):
-            for s in range(2):
-                total = total + jnp.where(
-                    kept == 2 * r + s, back[pl.ds(base + r * width + s, half_w, stride=2), :], 0.0
-                )
-        pooled_ref[n, h] = total.astype(BF16)
-
-    outs = [pltpu.make_async_copy(pooled_ref, pooled_hbm, out_sem.at[0])]
-    outs[0].start()
+                pick = pl.ds(n, half_w, stride=nm)
+                kept = index_in[h, pick, :]
+                base = n * map_rows + 2 * h * width
+                total = jnp.zeros((half_w, LANES), F32)
+                for r in range(2):
+                    for s in range(2):
+                        total = total + jnp.where(
+                            kept == 2 * r + s,
+                            result_ref[pl.ds(base + r * width + s, half_w, stride=2), :],
+                            0.0,
+                        )
+                pool32[pick, :] = total
+            pooled_ref[h] = pool32[...].astype(BF16)
+
+        cp = pltpu.make_async_copy(pooled_ref, pooled_hbm, out_sem.at[0])
+        cp.start()
+        outs.append(cp)
+
+    outs = []
 
     def gx_copy(l, z):
         return remote(gx_out.at[l, z], gx_in.at[l, z], gx_s.at[l, z], gx_r.at[l, z], (m + 1 - 2 * b, c))
@@ -403,27 +455,57 @@
     def shard(l, slot):
         return grad_w[l, pl.ds(pl.multiple_of(slot * rows_w, 8), rows_w), :]
 
-    def scatter_x(l):
+    tile = 2 * rows_w
+    fine = tile % LANES == 0
+
+    def kernel_grad(l, first, amount):
+        rows = pl.ds(pl.multiple_of(first, LANES), amount)
+        grad_w[l, rows, :] = lax.dot_general(
+            act[l, :, rows], dcat[...], (((0,), (0,)), ((), ())), preferred_element_type=F32
+        )
+
+    def kernel_grads(l):
+        if not fine:
+            coarse = (maps * rows_w) // 4
+            pl.loop(0, 4)(lambda i: kernel_grad(l, i * coarse, coarse))
+
         def go(d):
             z = lax.rem(a + d, line)
+            if fine:
+                kernel_grad(l, z * tile, tile)
             gx_out[l, z] = shard(l, z * 2 + 1 - b).astype(BF16)
-            gx_copy(l, z).start()
+            if l == 0:
+                gx_copy(l, z).start()
 
         steps(1, line + 1, go)
 
-    def scatter_z(l):
-        def go(d):
-            z = lax.rem(a + d, line)
-            gx_copy(l, z).wait_recv()
-            value = shard(l, z * 2 + b) + gx_in[l, z].astype(F32)
-            gz_out[l, z] = value.astype(BF16)
-            gz_send(l, z).start()
-
-        steps(1, line, go)
+    def scatter_x(l):
+        steps(1, line + 1, lambda d: gx_copy(l, lax.rem(a + d, line)).start())
+
+    def scatter_z(l, d):
+        z = lax.rem(a + d, line)
+        gx_copy(l, z).wait_recv()
+        value = shard(l, z * 2 + b) + gx_in[l, z].astype(F32)
+        gz_out[l, z] = value.astype(BF16)
+        gz_send(l, z).start()
+
+    def scatter_own(l):
         gx_copy(l, a).wait_recv()
         part_w = shard(l, m) + gx_in[l, a].astype(F32)
         for t in range(taps):
             wgrad_ref[l, t] = part_w[:, t * LANES : (t + 1) * LANES]
+
+    def scatter_tasks(l):
+        if line <= 8:
+            return [functools.partial(scatter_z, l, d) for d in range(1, line)] + [
+                functools.partial(scatter_own, l)
+            ]
+
+        def everything():
+            steps(1, line, lambda d: scatter_z(l, d))
+            scatter_own(l)
+
+        return [everything]
 
     def scatter_finish(l):
         def go(d):
@@ -491,9 +573,14 @@
             axis=0,
         )
         stat_send(e)
+        tasks = []
         if l + 1 < layers:
             scatter_x(l + 1)
-        stat_wait(e)
+            tasks = scatter_tasks(l + 1)
+        else:
+            pool()
+        with scope("stat_wait_back"):
+            stat_wait(e)
 
         def add_sums(s, carry):
             return carry + stat[e, s]
@@ -504,72 +591,102 @@
         bias_grad = sums[1:2, :]
         scale = scales[l]
 
-        @pl.loop(0, chunks)
-        def _(i):
-            r = rows_of(i)
-            value = (
-                mask_ref[r, :]
-                * scale
-                * (conv[r, :] - (bias_grad + normed[l, r, :] * gain_grad) / count_all)
+        def conv_grad(n):
+            @pl.loop(n * per_map, (n + 1) * per_map)
+            def _(i):
+                r = rows_of(i)
+                value = (
+                    mask_ref[r, :]
+                    * scale
+                    * (conv[r, :] - (bias_grad + normed[l, r, :] * gain_grad) / count_all)
+                )
+                pr = pl.ds(pl.multiple_of((i - n * per_map) * chunk, 16) + PAD, chunk)
+                zpad[n, pr, :] = value
+
+            @pl.loop(n * per_map, (n + 1) * per_map)
+            def _(i):
+                r = rows_of(i)
+                for k in range(3):
+                    for j in range(3):
+                        shift = PAD - (width * (k - 1) + (j - 1))
+                        pr = pl.ds(pl.multiple_of((i - n * per_map) * chunk, 16) + shift, chunk)
+                        term = zpad[n, pr, :]
+                        if j == 0:
+                            term = term * has_right
+                        if j == 2:
+                            term = term * has_left
+                        t = 3 * k + j
+                        dcat[r, t * LANES : (t + 1) * LANES] = term.astype(BF16)
+
+        def input_grad(h, n):
+            start = other_half if h == 0 else own_half
+            slots = maps // 2
+            w = wcat[l, pl.ds((start // half) * slots, slots), :, :].reshape(half, wide)
+            r = pl.ds(n * map_rows, map_rows)
+            part[h, r, :] = lax.dot_general(
+                dcat[r, :], w, (((1,), (1,)), ((), ())), preferred_element_type=F32
             )
-            n, pr = padded_rows(i, 0)
-            zpad[n, pr, :] = value
-
-        @pl.loop(0, chunks)
-        def _(i):
-            r = rows_of(i)
-            for k in range(3):
-                for j in range(3):
-                    n, pr = padded_rows(i, -(width * (k - 1) + (j - 1)))
-                    term = zpad[n, pr, :]
-                    if j == 0:
-                        term = term * has_right
-                    if j == 2:
-                        term = term * has_left
-                    t = 3 * k + j
-                    dcat[r, t * LANES : (t + 1) * LANES] = term.astype(BF16)
-
-        def half_grad(n, start):
-            w = wcat[l].reshape(maps * rows_w, wide) if False else None
-            slots = maps // 2
-            first = (start // half) * slots
-            w = wcat[l, pl.ds(first, slots), :, :].reshape(half, wide)
-            return lax.dot_general(
-                dcat[pl.ds(n * map_rows, map_rows), :], w, (((1,), (1,)), ((), ())),
-                preferred_element_type=F32,
-            )
-
-        for h, start in ((0, other_half), (1, own_half)):
+            pair_out[l, h, r, :] = part[h, r, lane_out_half].astype(BF16)
+            pair_copy(l, h, n).start()
+
+        def to_far(n):
+            r = pl.ds(n * map_rows, map_rows)
+            pair_copy(l, 0, n).wait_recv()
+            far_out[l, r, :] = (
+                part[0, r, lane_in_half] + pair_in[l, 0, r, :].astype(F32)
+            ).astype(BF16)
+            far_copy(l, n).start()
+
+        if l > 0:
             for n in range(nm):
-                r = pl.ds(n * map_rows, map_rows)
-                part[h, r, :] = half_grad(n, start)
-                pair_out[l, h, r, :] = part[h, r, lane_out_half].astype(BF16)
-                pair_copy(l, h, n).start()
-            if h == 0:
+                with scope("conv_grad"):
+                    conv_grad(n)
+                with scope("input_grad"):
+                    input_grad(0, n)
+                if n > 0:
+                    with scope("to_far"):
+                        to_far(n - 1)
+            with scope("scatter_z"):
+                run(tasks, 1)
+            for n in range(nm):
+                with scope("input_grad"):
+                    input_grad(1, n)
+                if n == 0:
+                    with scope("to_far"):
+                        to_far(nm - 1)
+            with scope("scatter_z"):
+                run(tasks, 1)
+            with scope("kernel_grad"):
+                kernel_grads(l)
+            with scope("scatter_z"):
+                run(tasks, 1)
+        else:
+            for n in range(nm):
+                conv_grad(n)
+            with scope("kernel_grad"):
+                kernel_grads(l)
+            with scope("scatter_z"):
+                run(tasks)
+            for n in range(nm):
+                with scope("input_grad"):
+                    input_grad(0, n)
+            tasks = scatter_tasks(0)
+            with scope("to_far"):
                 for n in range(nm):
-                    r = pl.ds(n * map_rows, map_rows)
-                    pair_copy(l, h, n).wait_recv()
-                    far_out[l, r, :] = (
-                        part[h, r, lane_in_half] + pair_in[l, h, r, :].astype(F32)
-                    ).astype(BF16)
-                    far_copy(l, n).start()
-        if l + 1 < layers:
-            scatter_z(l + 1)
-
-        slots = 2
-        tile = slots * rows_w if rows_w * slots >= LANES else maps * rows_w // 4
-
-        @pl.loop(0, (maps * rows_w) // tile)
-        def _(i):
-            cols = pl.ds(pl.multiple_of(i * tile, LANES), tile)
-            grad_w[l, pl.ds(pl.multiple_of(i * tile, LANES), tile), :] = lax.dot_general(
-                act[l, :, cols], dcat[...], (((0,), (0,)), ((), ())), preferred_element_type=F32
-            )
+                    to_far(n)
+            with scope("scatter_z"):
+                run(tasks, 1)
+            for n in range(nm):
+                with scope("input_grad"):
+                    input_grad(1, n)
+            with scope("scatter_z"):
+                run(tasks, 1)
 
         for n in range(nm):
             r = pl.ds(n * map_rows, map_rows)
-            pair_copy(l, 1, n).wait_recv()
-            far_copy(l, n).wait_recv()
+            with scope("far_wait"):
+                pair_copy(l, 1, n).wait_recv()
+                far_copy(l, n).wait_recv()
 
             @pl.loop(n * per_map, (n + 1) * per_map)
             def _(i):
@@ -583,8 +700,8 @@
                     value = value * mask_ref[r, :]
                 back[r, :] = value
 
-        if l + 1 < layers:
-            scatter_finish(l + 1)
+        with scope("scatter_z"):
+            run(tasks)
 
     cp = pltpu.make_async_copy(back, image_hbm, out_sem.at[1])
     cp.start()
@@ -592,9 +709,9 @@
     cp = pltpu.make_async_copy(ngrad_ref, ngrad_hbm, out_sem.at[2])
     cp.start()
     outs.append(cp)
-    scatter_x(0)
-    scatter_z(0)
-    scatter_finish(0)
+    with scope("scatter_end"):
+        for l in reversed(range(layers)):
+            scatter_finish(l)
 
     for l in range(layers):
         gather_drain(l)
@@ -619,6 +736,7 @@
     channels = chans * LANES
     map_rows = height * width
     sizes = (maps, chans, layers, taps, nm, height, width)
+    pieces = 2 if rows_w % 32 == 0 else 1
     vm = pltpu.VMEM
     dma = pltpu.SemaphoreType.DMA
     any_spec = pl.BlockSpec(memory_space=pl.ANY)
@@ -634,6 +752,8 @@
         vm((layers, pixels, LANES), F32),
         vm((pixels, LANES), F32),
         vm((pixels, LANES), F32),
+        vm((pixels, LANES), F32),
+        vm((nm * (width // 2), LANES), F32),
         vm((nm, map_rows + 2 * PAD, LANES), F32),
         vm((pixels, wide), BF16),
         vm((layers, channels, wide), F32),
@@ -643,11 +763,12 @@
         vm((layers, pixels, LANES), BF16), vm((layers, pixels, LANES), BF16),
         vm((layers, line, rows_w, wide), BF16), vm((layers, line, rows_w, wide), BF16),
         vm((layers, line, rows_w, wide), BF16), vm((layers, line, rows_w, wide), BF16),
-        vm((nm, height // 2, width // 2, LANES), BF16),
+        vm(index.shape, BF16),
         vm((layers, taps, rows_w, LANES), F32),
         vm((layers, 2, LANES), F32),
         dma((7,)), dma((3 + layers,)),
-        dma((layers, line)), dma((layers, line)), dma((layers, line)), dma((layers, maps)),
+        dma((layers, line, pieces)), dma((layers, line, pieces)), dma((layers, line, pieces)),
+        dma((layers, maps, pieces)),
         dma((2 * layers, maps)), dma((2 * layers, maps)),
         dma((layers, 3, nm)), dma((layers, 3, nm)),
         dma((layers, 2, nm)), dma((layers, 2, nm)),
@@ -657,7 +778,7 @@
     return pl.pallas_call(
         functools.partial(block_kernel, sizes),
         out_shape=(
-            jax.ShapeDtypeStruct((nm, height // 2, width // 2, LANES), BF16),
+            jax.ShapeDtypeStruct(index.shape, BF16),
             jax.ShapeDtypeStruct((pixels, LANES), F32),
             jax.ShapeDtypeStruct((layers, taps, rows_w, LANES), F32),
             jax.ShapeDtypeStruct((layers, 2, LANES), F32),
@@ -676,9 +797,15 @@
     input_maps, valid_mask, pool_index, out_grad, conv_weights, weight_first, weight_second,
     norm_gain, norm_bias, norm_first, norm_second,
 ):
+    nm, half_h, half_w, lanes = pool_index.shape
+    by_row = (half_h, half_w * nm, lanes)
     pooled, image, weight_grads, norm_grads = block_call(
-        maps, chans, input_maps, valid_mask, pool_index, out_grad, conv_weights, norm_gain, norm_bias
+        maps, chans, input_maps, valid_mask.transpose(1, 0, 2),
+        pool_index.transpose(1, 2, 0, 3).reshape(by_row),
+        out_grad.transpose(1, 2, 0, 3).reshape(by_row),
+        conv_weights, norm_gain, norm_bias,
     )
+    pooled = pooled.reshape(half_h, half_w, nm, lanes).transpose(2, 0, 1, 3)
     image_grad = image.reshape(input_maps.shape)
     new_weights, new_weight_first, new_weight_second = adamw_update(
         conv_weights, weight_grads, weight_first, weight_second, rate_conv

time: 179 us -> 138 us (0.77)
  Pallas kernels: 166 us -> 129 us
  local copies, waits for them, and re-layouts: 7.54 us -> 2.92 us
    pallas_call x1, Pallas kernels: 166 us -> 129 us  [block_call(): pl.pallas_call(functools.partial(block_kernel, sizes), out_shape=(jax.Sha...]
    unnamed x27 -> x22, local copies, waits for them, and re-layouts: 7.54 us -> 2.92 us
where the time goes in v2:
time: 138 us; the launch traced here: 137 us
  Pallas kernels  129 us (93%)
  other arithmetic  4.58 us (3%)
  local copies, waits for them, and re-layouts  2.92 us (2%)
    pallas_call x1, Pallas kernels, block_call(): pl.pallas_call(functools.partial(block_kernel, sizes), out_shape=(jax.Sha...  129 us
    convert_element_type x1, other arithmetic, local(): new_weights.astype(BF16)  3.98 us
    unnamed x22, local copies, waits for them, and re-layouts  2.92 us

profile of v2, /device:TPU:0, one launch (start us, length us, event | category | flops | bytes accessed | tf_op | source)
XLA Modules:
  0.0 137.1 jit_solution(3990732553469974466)
XLA Ops:
  0.6 0.0 copy-start
  0.7 128.8 %shard_map.194 = (bf16[9,24,128]{2,1,0:T(8,128)(2,1)}, f32[864,128]{1,0:T(8,128)}, f32[3,9,64,128]{3,2,1,0:T(8,128)}, f32[3,2,128]{2,1,0:T(2,128)}) custom-call(bf16[864,128]{1,0:T(8,128)(2,1)} %bitcast.13, s32[18,2,24]{2,1,0:T(2,128)} %bitcast.17, s32[9,24,128]{2,1,0:T(8,128)} %bitcast.14, bf16[9,24,128]{2,1,0:T(8,128)(2,1)} %bitcast.16, ...), custom_call_target="tpu_custom_call" | custom-call | tf_op jit(solution)/shard_map/pallas_call | solution.py:778
  129.4 0.0 copy-done
  129.5 0.0 copy-start.5
  129.5 0.0 copy-start.6
  129.5 0.0 copy-start.4
  129.5 0.0 copy-start.7
  129.5 0.0 copy-start.8
  129.5 0.0 copy-start.3
  129.5 0.0 copy-start.2
  129.5 4.0 %fusion.3 = (bf16[3,9,64,128]{3,2,1,0:T(8,128)(2,1)}, f32[3,9,64,128]{3,2,1,0:T(8,128)}, f32[3,9,64,128]{3,2,1,0:T(8,128)}, f32[3,9,64,128]{3,2,1,0:T(8,128)}) fusion(f32[3,9,64,128]{3,2,1,0:T(8,128)S(1)} %copy-done, f32[3,9,64,128]{3,2,1,0:T(8,128)} %get-tuple-element.39, f32[3,9,64,128]{3,2,1,0:T(8,128)} %param.17, f32[3,9,64,128]{3,2,1,0:T(8,128)} %param.16), kind=kLoop, calls=%fused_computation.9 | loop fusion | flops 3317760 | bytes 6635520 | tf_op jit(solution)/shard_map/convert_element_type | solution.py:824
  133.5 0.0 copy-start.1
  133.5 0.0 copy-done.5
  133.5 0.0 copy-done.6
  133.5 0.0 copy-done.4
  133.6 0.0 copy-done.7
  133.6 0.0 copy-done.8
  133.6 0.6 multiply_subtract_fusion.1
  134.2 0.0 copy-done.3
  134.2 0.6 copy.26
  134.8 0.0 copy-done.2
  134.8 0.8 copy.27
  135.6 0.0 copy-done.1
  135.6 0.9 copy.28
  136.5 0.6 copy.29
  (2 shorter events, 0.0 us)
Async XLA Ops:
  0.6 128.8 %copy-start = (f32[3,9,64,128]{3,2,1,0:T(8,128)S(1)}, f32[3,9,64,128]{3,2,1,0:T(8,128)}, u32[]{:S(2)}) copy-start(f32[3,9,64,128]{3,2,1,0:T(8,128)} %weight_hbm.1) | copy-start | bytes 2654212
  129.5 4.1 %copy-start.5 = (f32[3,128]{1,0:T(4,128)S(1)}, f32[3,128]{1,0:T(4,128)}, u32[]{:S(2)}) copy-start(f32[3,128]{1,0:T(4,128)} %bias_hbm.1) | copy-start | bytes 4612
  129.5 4.1 %copy-start.6 = (f32[3,128]{1,0:T(4,128)S(1)}, f32[3,128]{1,0:T(4,128)}, u32[]{:S(2)}) copy-start(f32[3,128]{1,0:T(4,128)} %gain_hbm.1) | copy-start | bytes 4612
  129.5 4.1 %copy-start.4 = (f32[3,2,128]{2,1,0:T(2,128)S(1)}, f32[3,2,128]{2,1,0:T(2,128)}, u32[]{:S(2)}) copy-start(f32[3,2,128]{2,1,0:T(2,128)} %get-tuple-element.44) | copy-start | bytes 9220
  129.5 4.1 %copy-start.7 = (f32[3,2,128]{2,1,0:T(2,128)S(1)}, f32[3,2,128]{2,1,0:T(2,128)}, u32[]{:S(2)}) copy-start(f32[3,2,128]{2,1,0:T(2,128)} %param.21) | copy-start | bytes 9220
  129.5 4.1 %copy-start.8 = (f32[3,2,128]{2,1,0:T(2,128)S(1)}, f32[3,2,128]{2,1,0:T(2,128)}, u32[]{:S(2)}) copy-start(f32[3,2,128]{2,1,0:T(2,128)} %param.20) | copy-start | bytes 9220
  129.5 4.7 %copy-start.3 = (bf16[9,24,128]{2,1,0:T(8,128)(2,1)S(1)}, bf16[9,24,128]{2,1,0:T(8,128)(2,1)}, u32[]{:S(2)}) copy-start(bf16[9,24,128]{2,1,0:T(8,128)(2,1)} %get-tuple-element.15) | copy-start | bytes 165892
  129.5 5.3 %copy-start.2 = (f32[864,128]{1,0:T(8,128)S(1)}, f32[864,128]{1,0:T(8,128)}, u32[]{:S(2)}) copy-start(f32[864,128]{1,0:T(8,128)} %get-tuple-element.16) | copy-start | bytes 1327108
  133.5 2.1 %copy-start.1 = (f32[3,9,64,128]{3,2,1,0:T(8,128)S(1)}, f32[3,9,64,128]{3,2,1,0:T(8,128)}, u32[]{:S(2)}) copy-start(f32[3,9,64,128]{3,2,1,0:T(8,128)} %get-tuple-element.39) | copy-start | bytes 2654212

commit v3 on v2

v3 whole, which is shorter than its diff:
```python
import functools

import jax
import jax.numpy as jnp
from jax import lax
from jax.experimental import pallas as pl
from jax.experimental.pallas import tpu as pltpu
from jax.sharding import PartitionSpec as P

beta_first = 0.5
beta_second = 0.5
rate_conv = 0.01
rate_norm = 0.2
decay_rate = 0.01
adam_epsilon = 1e-08
norm_epsilon = 1e-05
step_count = 5.0
first_scale = 1.0 / (1.0 - beta_first**step_count)
second_scale = 1.0 / (1.0 - beta_second**step_count)

MESH = pl.DeviceIdType.MESH
F32 = jnp.float32
BF16 = jnp.bfloat16
LANES = 128
PAD = 32


def adamw_update(parameter, gradient, first_moment, second_moment, step_rate):
    first_new = beta_first * first_moment + (1.0 - beta_first) * gradient
    second_new = beta_second * second_moment + (1.0 - beta_second) * gradient * gradient
    step = first_new * first_scale / (jnp.sqrt(second_new * second_scale) + adam_epsilon)
    return (parameter - step_rate * (step + decay_rate * parameter), first_new, second_new)


def steps(low, high, body):
    if high - low <= 8:
        for index in range(low, high):
            body(index)
    else:
        pl.loop(low, high)(body)


scope = jax.named_scope


def run(tasks, amount=None):
    for _ in range(len(tasks) if amount is None else min(amount, len(tasks))):
        tasks.pop(0)()


def tile8(values):
    rows = values.shape[0]
    return jnp.sum(values.reshape(rows // 8, 8, LANES), axis=0)


def block_kernel(
    sizes,
    x_hbm, mask_hbm, index_hbm, grad_hbm, weight_hbm, gain_hbm, bias_hbm,
    first_hbm, second_hbm, norm_first_hbm, norm_second_hbm,
    pooled_ref, back, wgrad_ref, wfirst_ref, wsecond_ref, wnew_ref, wcopy_ref,
    ngrad_ref, nfirst_ref, nsecond_ref, nnew_ref,
    x_in, mask_in, index_in, grad_in, weight_in, gain_in, bias_in,
    first_in, second_in, norm_first_in, norm_second_in,
    mask_ref, wcat, act, raw, scale_ref, prod, conv, normed, slope, result_ref, spread, pool32, zpad, dcat,
    grad_w, part, stat, pair_out, pair_in, far_out, far_in,
    gx_out, gx_in, gz_out, gz_in, total_w,
    in_sem,
    w_s, wz_r, wx_r, st_s, st_r, ag_s, ag_r, sc_s, sc_r, pr_s, pr_r, fr_s, fr_r,
    gx_s, gx_r, gz_s, gz_r,
):
    maps, chans, layers, taps, nm, height, width = sizes
    line = maps // 2
    m = lax.axis_index("maps")
    c = lax.axis_index("chan")
    a = m // 2
    b = m % 2
    core = c + 1 - 2 * (c % 2)
    far = lax.rem(c + 2, 4)
    across = core + 2 - 4 * (core // 2)
    map_rows = height * width
    pixels = nm * map_rows
    rows_w = wcat.shape[1]
    wide = taps * LANES
    chunk = 6 * width
    chunks = pixels // chunk
    per_map = map_rows // chunk

    def rows_of(i):
        return pl.ds(pl.multiple_of(i * chunk, 16), chunk)

    def padded_rows(i, shift):
        n = i // per_map
        return n, pl.ds(pl.multiple_of((i - n * per_map) * chunk, 8) + (PAD + shift), chunk)

    def remote(src, dst, ssem, rsem, dev):
        return pltpu.make_async_remote_copy(
            src_ref=src, dst_ref=dst, send_sem=ssem, recv_sem=rsem,
            device_id=dev, device_id_type=MESH,
        )

    loads = []
    for i, (src, dst) in enumerate(
        (
            (weight_hbm, weight_in), (x_hbm, x_in), (mask_hbm, mask_in),
            (index_hbm, index_in), (grad_hbm, grad_in), (gain_hbm, gain_in), (bias_hbm, bias_in),
            (first_hbm, first_in), (second_hbm, second_in),
            (norm_first_hbm, norm_first_in), (norm_second_hbm, norm_second_in),
        )
    ):
        cp = pltpu.make_async_copy(src, dst, in_sem.at[i])
        cp.start()
        loads.append(cp)

    barrier = pltpu.get_barrier_semaphore()

    def greet(d):
        peer = lax.rem(m + d, maps)
        pl.semaphore_signal(barrier, inc=1, device_id=(peer, c), device_id_type=MESH)

    steps(1, maps, greet)
    for other in (core, far, across):
        pl.semaphore_signal(barrier, inc=1, device_id=(m, other), device_id_type=MESH)

    loads[0].wait()
    for l in range(layers):
        for t in range(taps):
            wcat[l * maps + m, :, t * LANES : (t + 1) * LANES] = weight_in[l, t].astype(BF16)

    pl.semaphore_wait(barrier, maps + 2)

    pieces = wz_r.shape[2]
    piece_rows = rows_w // pieces
    right = (jnp.minimum(m + 2, maps - 1), c)
    left = (jnp.maximum(m - 2, 0), c)
    beside = (m + 1 - 2 * b, c)

    def weight_view(l, slot, g):
        return wcat.at[l * maps + slot, pl.ds(g * piece_rows, piece_rows)]

    def along(l, z, g, dev):
        view = weight_view(l, z * 2 + b, g)
        return remote(view, view, w_s.at[l, 0], wz_r.at[l, z, g], dev)

    def aside(l, z, g):
        view = weight_view(l, z * 2 + b, g)
        return remote(view, view, w_s.at[l, 1], wx_r.at[l], beside)

    def shards_of(l, count, place):
        view = wcat.at[pl.ds(0, count)]
        return remote(view, view, w_s.at[l, place], wx_r.at[l], beside)

    def gather_own(l):
        for g in range(pieces):
            pl.when(a + 1 < line)(lambda: along(l, a, g, right).start())
            pl.when(a > 0)(lambda: along(l, a, g, left).start())
            aside(l, a, g).start()

    def gather_step(l, s, g):
        def piece(cond, z, onward_cond, onward):
            @pl.when(cond)
            def _():
                along(l, z, g, onward).wait_recv()
                pl.when(onward_cond)(lambda: along(l, z, g, onward).start())
                aside(l, z, g).start()

        piece(a >= s, jnp.maximum(a - s, 0), a + 1 < line, right)
        piece(a + s < line, jnp.minimum(a + s, line - 1), a > 0, left)

    def gather_tasks(l):
        if line <= 8:
            return [
                functools.partial(gather_step, l, s, g)
                for s in range(1, line)
                for g in range(pieces)
            ]

        def everything():
            def go(s):
                for g in range(pieces):
                    gather_step(l, s, g)

            steps(1, line, go)

        return [everything]

    def gather_finish(l):
        shards_of(l, line, 1).wait_recv()

    def gather_drain(l):
        shards_of(l, line, 1).wait_send()
        inner = jnp.logical_and(a > 0, a + 1 < line)
        pl.when(inner)(lambda: shards_of(l, line + 1, 0).wait_send())
        pl.when(jnp.logical_not(inner))(lambda: shards_of(l, 1, 0).wait_send())

    def stat_send(e):
        def go(d):
            peer = lax.rem(m + d, maps)
            view = stat.at[e, m]
            remote(view, view, st_s.at[e], st_r.at[e], (peer, c)).start()

        steps(1, maps, go)

    def stat_all(e):
        view = stat.at[e, pl.ds(0, maps - 1)]
        return remote(view, view, st_s.at[e], st_r.at[e], beside)

    def stat_wait(e):
        stat_all(e).wait_recv()

    def stat_drain(e):
        stat_all(e).wait_send()

    lane_own = pl.ds(pl.multiple_of(c * LANES, LANES), LANES)

    def lanes_of(owner):
        return pl.ds(pl.multiple_of(owner * LANES, LANES), LANES)

    def act_copy(l, n, owner, dev, place):
        rows = pl.ds(n * map_rows, map_rows)
        view = act.at[0, rows, lanes_of(owner)] if l == 0 else raw.at[l - 1, owner, rows]
        return remote(view, view, ag_s.at[l], ag_r.at[l, place], dev)

    def act_blocks(l, count, place):
        view = act.at[0, :, pl.ds(0, count * LANES)] if l == 0 else raw.at[l - 1, pl.ds(0, count)]
        return remote(view, view, ag_s.at[l], ag_r.at[l, place], (m, core))

    def act_send(l, n):
        act_copy(l, n, c, (m, far), n).start()
        act_copy(l, n, c, (m, core), nm).start()

    def act_forward(l, n):
        act_copy(l, n, far, (m, far), n).wait_recv()
        act_copy(l, n, far, (m, core), nm + 1).start()

    def act_near(l):
        act_blocks(l, 1, nm).wait_recv()

    def act_across(l):
        act_blocks(l, 1, nm + 1).wait_recv()

    def act_drain(l):
        act_blocks(l, 3, 0).wait_send()

    def scale_copy(l, owner, dev, ssem):
        view = scale_ref.at[l, owner]
        return remote(view, view, ssem, sc_r.at[l, owner], dev)

    def scale_send(l):
        for other in (core, far, across):
            scale_copy(l, c, (m, other), sc_s.at[l]).start()

    def scale_wait(l, owner):
        scale_copy(l, owner, (m, core), sc_s.at[l]).wait_recv()

    def scale_drain(l):
        view = scale_ref.at[l, pl.ds(0, 3)]
        remote(view, view, sc_s.at[l], sc_r.at[l, core], (m, core)).wait_send()

    gather_own(0)

    loads[2].wait()
    col_of = lax.broadcasted_iota(jnp.int32, (width, width), 0)
    diagonal = col_of == lax.broadcasted_iota(jnp.int32, (width, width), 1)
    for n in range(nm):

        @pl.loop(0, height)
        def _(h):
            line_n = jnp.broadcast_to(mask_in[h, n : n + 1, :].astype(F32), (width, width))
            r = pl.ds(pl.multiple_of(n * map_rows + h * width, 8), width)
            conv[r, 0:width] = jnp.where(diagonal, line_n, 0.0)

    mask_ref[...] = jnp.dot(
        conv[:, 0:width].astype(BF16), jnp.ones((width, LANES), BF16), preferred_element_type=F32
    )
    loads[1].wait()

    @pl.loop(0, chunks)
    def _(i):
        r = rows_of(i)
        act[0, r, lane_own] = (x_in[r, :].astype(F32) * mask_ref[r, :]).astype(BF16)

    for n in range(nm):
        act_send(0, n)

    for n in range(nm):
        for i in range(3):
            for j in range(3):
                prod[i, j, n, 0:PAD, :] = jnp.zeros((PAD, LANES), F32)
                prod[i, j, n, PAD + map_rows :, :] = jnp.zeros((PAD, LANES), F32)
        zpad[n, 0:PAD, :] = jnp.zeros((PAD, LANES), F32)
        zpad[n, PAD + map_rows :, :] = jnp.zeros((PAD, LANES), F32)

    col_chunk = lax.broadcasted_iota(jnp.int32, (6, width, LANES), 1).reshape(chunk, LANES)
    has_left = jnp.where(col_chunk > 0, 1.0, 0.0)
    has_right = jnp.where(col_chunk < width - 1, 1.0, 0.0)

    loads[3].wait()
    loads[4].wait()
    half_h, half_w = height // 2, width // 2

    @pl.loop(0, half_h)
    def _(h):
        pool32[...] = grad_in[h].astype(F32)
        for n in range(nm):
            pick = pl.ds(n, half_w, stride=nm)
            kept = index_in[h, pick, :]
            value = pool32[pick, :]
            base = n * map_rows + 2 * h * width
            for r in range(2):
                for s in range(2):
                    spread[pl.ds(base + r * width + s, half_w, stride=2), :] = jnp.where(
                        kept == 2 * r + s, value, 0.0
                    )

    tasks = gather_tasks(0)
    with scope("gather0"):
        run(tasks)
    for n in range(nm):
        act_forward(0, n)
    with scope("gather0_end"):
        gather_finish(0)
    act_near(0)
    act_across(0)
    for cp in loads[5:]:
        cp.wait()

    for l in range(layers):
        tasks = []
        if l + 1 < layers:
            gather_own(l + 1)
            tasks = gather_tasks(l + 1)

        @pl.loop(0, 3)
        def _(i):
            cols = pl.ds(pl.multiple_of(i * (3 * LANES), LANES), 3 * LANES)
            w = wcat[l * maps : (l + 1) * maps, :, cols].reshape(maps * rows_w, 3 * LANES)
            for n in range(nm):
                out = jnp.dot(
                    act[l, pl.ds(n * map_rows, map_rows), :], w, preferred_element_type=F32
                )
                for j in range(3):
                    prod[i, j, n, PAD : PAD + map_rows, :] = out[:, j * LANES : (j + 1) * LANES]

        def conv_chunk(i, carry):
            total, count = carry
            r = rows_of(i)
            value = None
            for j in range(3):
                side = None
                for k in range(3):
                    n, pr = padded_rows(i, width * (k - 1) + (j - 1))
                    term = prod[k, j, n, pr, :]
                    side = term if side is None else side + term
                if j == 0:
                    side = side * has_left
                if j == 2:
                    side = side * has_right
                value = side if value is None else value + side
            conv[r, :] = value
            valid = mask_ref[r, :]
            return total + tile8(value * valid), count + tile8(valid)

        zero8 = jnp.zeros((8, LANES), F32)
        total, count = lax.fori_loop(0, chunks, conv_chunk, (zero8, zero8))
        total = jnp.sum(total, axis=0, keepdims=True)
        count = jnp.sum(count, axis=0, keepdims=True)
        mean = total / jnp.maximum(count, 1.0)

        def dev_chunk(i, carry):
            r = rows_of(i)
            delta = conv[r, :] - mean
            if l + 1 < layers:
                raw[l, c, r, :] = delta.astype(BF16)
            return carry + tile8(delta * delta * mask_ref[r, :])

        spread_sum = zero8
        for n in range(nm):
            spread_sum = lax.fori_loop(n * per_map, (n + 1) * per_map, dev_chunk, spread_sum)
            if l + 1 < layers:
                act_send(l + 1, n)
        spread_sum = jnp.sum(spread_sum, axis=0, keepdims=True)
        stat[l, m] = jnp.concatenate(
            [total, spread_sum, count, mean, jnp.zeros((4, LANES), F32)], axis=0
        )
        stat_send(l)
        with scope("gather_a"):
            run(tasks, pieces)
        with scope("stat_wait"):
            stat_wait(l)

        def add_totals(s, carry):
            block = stat[l, s]
            return carry[0] + block[0:1, :], carry[1] + block[2:3, :]

        zero1 = jnp.zeros((1, LANES), F32)
        total, count = lax.fori_loop(0, maps, add_totals, (zero1, zero1))
        center = total / count

        def add_spread(s, carry):
            block = stat[l, s]
            delta = block[3:4, :] - center
            return carry + block[1:2, :] + block[2:3, :] * delta * delta

        variance = lax.fori_loop(0, maps, add_spread, zero1) / count
        inv_std = lax.rsqrt(variance + norm_epsilon)
        gain = gain_in[l : l + 1, :]
        bias = bias_in[l : l + 1, :]
        if l == 0:
            count_all = count
            scales = []
        scales.append(gain * inv_std)

        if l + 1 < layers:
            factor = gain * inv_std
            scale_ref[l, c] = jnp.concatenate(
                [factor, bias + factor * (mean - center), jnp.zeros((6, LANES), F32)], axis=0
            )
            scale_send(l)

        @pl.loop(0, chunks)
        def _(i):
            r = rows_of(i)
            unit = (conv[r, :] - center) * inv_std
            pre = gain * unit + bias
            sigma = 1.0 / (1.0 + jnp.exp(-pre))
            valid = mask_ref[r, :]
            result = pre * sigma * valid
            normed[l, r, :] = unit
            slope[l, r, :] = sigma * (1.0 + pre * (1.0 - sigma)) * valid
            if l + 1 < layers:
                act[l + 1, r, lane_own] = result.astype(BF16)
            else:
                result_ref[r, :] = result

        def activate(owner, first, last):
            pair = scale_ref[l, owner]
            factor, offset = pair[0:1, :], pair[1:2, :]
            lanes = lanes_of(owner)

            @pl.loop(first * per_map, last * per_map)
            def _(i):
                r = rows_of(i)
                pre = factor * raw[l, owner, r, :].astype(F32) + offset
                result = pre / (1.0 + jnp.exp(-pre)) * mask_ref[r, :]
                act[l + 1, r, lanes] = result.astype(BF16)

        if l + 1 < layers:
            with scope("act_near"):
                act_near(l + 1)
                scale_wait(l, core)
                activate(core, 0, nm)
            with scope("gather_b"):
                run(tasks, 1)
            with scope("act_far"):
                for n in range(nm):
                    act_forward(l + 1, n)
                    if n == 0:
                        scale_wait(l, far)
                    activate(far, n, n + 1)
            with scope("gather_c"):
                run(tasks, 2)
            with scope("act_across"):
                act_across(l + 1)
                scale_wait(l, across)
                activate(across, 0, nm)
            with scope("gather_d"):
                run(tasks)
            with scope("gather_end"):
                gather_finish(l + 1)

    def pool():
        @pl.loop(0, half_h)
        def _(h):
            for n in range(nm):
                pick = pl.ds(n, half_w, stride=nm)
                kept = index_in[h, pick, :]
                base = n * map_rows + 2 * h * width
                total = jnp.zeros((half_w, LANES), F32)
                for r in range(2):
                    for s in range(2):
                        total = total + jnp.where(
                            kept == 2 * r + s,
                            result_ref[pl.ds(base + r * width + s, half_w, stride=2), :],
                            0.0,
                        )
                pool32[pick, :] = total
            pooled_ref[h] = pool32[...].astype(BF16)

    def far_first(body):
        def go(e):
            d = line - e

            @pl.when(a + d < line)
            def _():
                body(jnp.minimum(a + d, line - 1))

            @pl.when(a >= d)
            def _():
                body(jnp.maximum(a - d, 0))

        steps(1, line, go)
        body(a)

    def part_of(g):
        return pl.ds(g * piece_rows, piece_rows)

    def gx_copy(l, z, g):
        return remote(
            gx_out.at[l, z, part_of(g)], gx_in.at[l, z, part_of(g)],
            gx_s.at[l], gx_r.at[l, z, g], beside,
        )

    def gz_copy(l, z, g, slot, dev):
        return remote(
            gz_out.at[l, z, part_of(g)], gz_in.at[l, slot, part_of(g)],
            gz_s.at[l], gz_r.at[l, slot, g], dev,
        )

    def shard(l, slot, g):
        first = pl.multiple_of(slot * rows_w, 8) + g * piece_rows
        return grad_w[l, pl.ds(first, piece_rows), :]

    tile = 2 * rows_w
    fine = tile % LANES == 0

    def kernel_grad(l, first, amount):
        rows = pl.ds(pl.multiple_of(first, LANES), amount)
        grad_w[l, rows, :] = lax.dot_general(
            act[l, :, rows], dcat[...], (((0,), (0,)), ((), ())), preferred_element_type=F32
        )

    def kernel_grads(l, send):
        if not fine:
            coarse = (maps * rows_w) // 4
            pl.loop(0, 4)(lambda i: kernel_grad(l, i * coarse, coarse))

        def go(z):
            if fine:
                kernel_grad(l, z * tile, tile)
            for g in range(pieces):
                gx_out[l, z, part_of(g)] = shard(l, z * 2 + 1 - b, g).astype(BF16)
                if send:
                    gx_copy(l, z, g).start()

        far_first(go)

    def scatter_x(l):
        def go(z):
            for g in range(pieces):
                gx_copy(l, z, g).start()

        far_first(go)

    def pair_sum(l, z, g):
        gx_copy(l, z, g).wait_recv()
        return shard(l, z * 2 + b, g) + gx_in[l, z, part_of(g)].astype(F32)

    def onward(l, z, g, has_more, dev, slot):
        @pl.when(has_more)
        def _():
            gz_copy(l, z, g, z, dev).wait_recv()
            gz_out[l, z, part_of(g)] = (
                pair_sum(l, z, g) + gz_in[l, z, part_of(g)].astype(F32)
            ).astype(BF16)

        @pl.when(jnp.logical_not(has_more))
        def _():
            gz_out[l, z, part_of(g)] = pair_sum(l, z, g).astype(BF16)

        gz_copy(l, z, g, slot, dev).start()

    def scatter_step(l, d, g):
        @pl.when(a + d < line)
        def _():
            z = jnp.minimum(a + d, line - 1)
            onward(l, z, g, a > 0, right, z)

        @pl.when(a >= d)
        def _():
            z = jnp.maximum(a - d, 0)
            onward(l, z, g, a + 1 < line, left, jnp.where(z == a - 1, line, z))

    def scatter_own(l, g):
        r = part_of(g)
        total_w[r, :] = pair_sum(l, a, g)

        @pl.when(a > 0)
        def _():
            gz_copy(l, a, g, a, left).wait_recv()
            total_w[r, :] += gz_in[l, a, r].astype(F32)

        @pl.when(a + 1 < line)
        def _():
            gz_copy(l, a, g, line, right).wait_recv()
            total_w[r, :] += gz_in[l, line, r].astype(F32)

        for t in range(taps):
            gradient = total_w[r, t * LANES : (t + 1) * LANES]
            new, first, second = adamw_update(
                weight_in[l, t, r], gradient, first_in[l, t, r], second_in[l, t, r], rate_conv
            )
            wgrad_ref[l, t, r] = gradient
            wfirst_ref[l, t, r] = first
            wsecond_ref[l, t, r] = second
            wnew_ref[l, t, r] = new
            wcopy_ref[l, t, r] = new.astype(BF16)

    def scatter_tasks(l):
        owns = [functools.partial(scatter_own, l, g) for g in range(pieces)]
        if line <= 8:
            return [
                functools.partial(scatter_step, l, line - e, g)
                for e in range(1, line)
                for g in range(pieces)
            ], owns

        def everything():
            def go(e):
                for g in range(pieces):
                    scatter_step(l, line - e, g)

            steps(1, line, go)

        return [everything], owns

    def scatter_drain(l):
        remote(gx_out.at[l], gx_in.at[l], gx_s.at[l], gx_r.at[l, 0, 0], beside).wait_send()
        view = pl.ds(0, line - 1)
        remote(
            gz_out.at[l, view], gz_in.at[l, view], gz_s.at[l], gz_r.at[l, 0, 0], beside
        ).wait_send()

    def layer_drain(l):
        stat_drain(layers + l)
        remote(pair_out.at[l], pair_in.at[l], pr_s.at[l], pr_r.at[l, 0], (m, core)).wait_send()
        remote(far_out.at[l], far_in.at[l], fr_s.at[l], fr_r.at[l, 0], (m, far)).wait_send()

    half = 2 * LANES
    own_half = (c // 2) * half
    other_half = half - own_half
    lane_in_half = pl.ds(pl.multiple_of((c % 2) * LANES, LANES), LANES)
    lane_out_half = pl.ds(pl.multiple_of((1 - c % 2) * LANES, LANES), LANES)

    def pair_copy(l, h, n):
        return remote(
            pair_out.at[l, h, pl.ds(n * map_rows, map_rows), :],
            pair_in.at[l, h, pl.ds(n * map_rows, map_rows), :],
            pr_s.at[l], pr_r.at[l, n if h == 0 else nm], (m, core),
        )

    def far_copy(l, n):
        return remote(
            far_out.at[l, pl.ds(n * map_rows, map_rows), :],
            far_in.at[l, pl.ds(n * map_rows, map_rows), :],
            fr_s.at[l], fr_r.at[l, n], (m, far),
        )

    todo, owns = {}, {}
    for l in reversed(range(layers)):
        e = layers + l
        source = spread if l == layers - 1 else back

        def slope_chunk(i, carry):
            r = rows_of(i)
            value = source[r, :] * slope[l, r, :]
            conv[r, :] = value
            return carry[0] + tile8(value * normed[l, r, :]), carry[1] + tile8(value)

        zero8 = jnp.zeros((8, LANES), F32)
        gain_sum, bias_sum = lax.fori_loop(0, chunks, slope_chunk, (zero8, zero8))
        stat[e, m] = jnp.concatenate(
            [
                jnp.sum(gain_sum, axis=0, keepdims=True),
                jnp.sum(bias_sum, axis=0, keepdims=True),
                jnp.zeros((6, LANES), F32),
            ],
            axis=0,
        )
        stat_send(e)
        if l + 1 < layers:
            scatter_x(l + 1)
        else:
            pool()
        if l + 1 < layers:
            todo[l + 1], owns[l + 1] = scatter_tasks(l + 1)
        if l + 2 < layers:
            with scope("scatter_last"):
                run(todo[l + 2])
        with scope("stat_wait_back"):
            stat_wait(e)

        def add_sums(s, carry):
            return carry + stat[e, s]

        sums = lax.fori_loop(0, maps, add_sums, jnp.zeros((8, LANES), F32))
        ngrad_ref[l] = sums[0:2, :]
        gain_grad = sums[0:1, :]
        bias_grad = sums[1:2, :]
        scale = scales[l]

        def conv_grad(n):
            @pl.loop(n * per_map, (n + 1) * per_map)
            def _(i):
                r = rows_of(i)
                value = (
                    mask_ref[r, :]
                    * scale
                    * (conv[r, :] - (bias_grad + normed[l, r, :] * gain_grad) / count_all)
                )
                pr = pl.ds(pl.multiple_of((i - n * per_map) * chunk, 16) + PAD, chunk)
                zpad[n, pr, :] = value

            @pl.loop(n * per_map, (n + 1) * per_map)
            def _(i):
                r = rows_of(i)
                for k in range(3):
                    for j in range(3):
                        shift = PAD - (width * (k - 1) + (j - 1))
                        pr = pl.ds(pl.multiple_of((i - n * per_map) * chunk, 16) + shift, chunk)
                        term = zpad[n, pr, :]
                        if j == 0:
                            term = term * has_right
                        if j == 2:
                            term = term * has_left
                        t = 3 * k + j
                        dcat[r, t * LANES : (t + 1) * LANES] = term.astype(BF16)

        def input_grad(h, n):
            start = other_half if h == 0 else own_half
            slots = maps // 2
            w = wcat[pl.ds(l * maps + (start // half) * slots, slots), :, :].reshape(half, wide)
            r = pl.ds(n * map_rows, map_rows)
            part[h, r, :] = lax.dot_general(
                dcat[r, :], w, (((1,), (1,)), ((), ())), preferred_element_type=F32
            )
            pair_out[l, h, r, :] = part[h, r, lane_out_half].astype(BF16)
            pair_copy(l, h, n).start()

        def to_far(n):
            r = pl.ds(n * map_rows, map_rows)
            pair_copy(l, 0, n).wait_recv()
            far_out[l, r, :] = (
                part[0, r, lane_in_half] + pair_in[l, 0, r, :].astype(F32)
            ).astype(BF16)
            far_copy(l, n).start()

        if l > 0:
            for n in range(nm):
                with scope("conv_grad"):
                    conv_grad(n)
                with scope("input_grad"):
                    input_grad(0, n)
                if n > 0:
                    with scope("to_far"):
                        to_far(n - 1)
            for n in range(nm):
                with scope("input_grad"):
                    input_grad(1, n)
                if n == 0:
                    with scope("to_far"):
                        to_far(nm - 1)
                    if l + 1 < layers:
                        with scope("scatter_step"):
                            run(todo[l + 1], pieces)
            with scope("kernel_grad"):
                kernel_grads(l, False)
            if l + 1 < layers:
                with scope("scatter_step"):
                    run(todo[l + 1], pieces)
            with scope("drain"):
                if l + 1 == layers:
                    for k in range(layers):
                        gather_drain(k)
                        act_drain(k)
                        stat_drain(k)
                        if k + 1 < layers:
                            scale_drain(k)
                else:
                    layer_drain(l + 1)
        else:
            for n in range(nm):
                with scope("conv_grad"):
                    conv_grad(n)
            with scope("scatter_1a"):
                run(todo[1], pieces)
            with scope("kernel_grad"):
                kernel_grads(0, True)
            todo[0], owns[0] = scatter_tasks(0)
            with scope("scatter_1b"):
                run(todo[1], pieces)
            for n in range(nm):
                with scope("input_grad"):
                    input_grad(0, n)
            with scope("scatter_1c"):
                run(todo[1])
            with scope("to_far"):
                for n in range(nm):
                    to_far(n)
            with scope("scatter_0a"):
                run(todo[0], pieces)
            for n in range(nm):
                with scope("input_grad"):
                    input_grad(1, n)
            with scope("owns"):
                for k in range(layers - 1, 0, -1):
                    run(owns[k])
            with scope("scatter_0b"):
                run(todo[0], pieces)
            with scope("drain"):
                for k in range(1, layers):
                    scatter_drain(k)
                layer_drain(1)

        for n in range(nm):
            r = pl.ds(n * map_rows, map_rows)
            with scope("far_wait"):
                if n == 0:
                    remote(
                        pair_out.at[l, 1], pair_in.at[l, 1], pr_s.at[l], pr_r.at[l, nm], (m, core)
                    ).wait_recv()
                far_copy(l, n).wait_recv()

            @pl.loop(n * per_map, (n + 1) * per_map)
            def _(i):
                r = rows_of(i)
                value = (
                    part[1, r, lane_in_half]
                    + pair_in[l, 1, r, :].astype(F32)
                    + far_in[l, r, :].astype(F32)
                )
                if l == 0:
                    value = value * mask_ref[r, :]
                back[r, :] = value

    with scope("norms"):
        for values, place in ((gain_in, 0), (bias_in, 1)):
            new, first, second = adamw_update(
                values[...], ngrad_ref[:, place, :], norm_first_in[:, place, :],
                norm_second_in[:, place, :], rate_norm,
            )
            nfirst_ref[:, place, :] = first
            nsecond_ref[:, place, :] = second
            nnew_ref[:, place, :] = new
    with scope("scatter_end"):
        run(todo[0])
    with scope("owns"):
        run(owns[0])

    with scope("drain_end"):
        layer_drain(0)
        scatter_drain(0)


def store_kernel(count, *refs):
    copies = [
        pltpu.make_async_copy(refs[i], refs[count + i], refs[2 * count].at[i]) for i in range(count)
    ]
    for cp in copies:
        cp.start()
    for cp in copies:
        cp.wait()


def store_results(results):
    any_spec = pl.BlockSpec(memory_space=pl.ANY)
    count = len(results)
    return pl.pallas_call(
        functools.partial(store_kernel, count),
        out_shape=tuple(jax.ShapeDtypeStruct(r.shape, r.dtype) for r in results),
        in_specs=[any_spec] * count,
        out_specs=(any_spec,) * count,
        scratch_shapes=[pltpu.SemaphoreType.DMA((count,))],
        compiler_params=pltpu.CompilerParams(vmem_limit_bytes=1 << 20),
    )(*results)


def block_call(maps, chans, x, mask, index, grad, weights, gain, bias, *moments):
    nm, height, width, lanes = x.shape
    layers, taps, rows_w, _ = weights.shape
    pixels = nm * height * width
    line = maps // 2
    wide = taps * LANES
    channels = chans * LANES
    map_rows = height * width
    sizes = (maps, chans, layers, taps, nm, height, width)
    pieces = 2 if rows_w % 32 == 0 else 1
    vm = pltpu.VMEM
    dma = pltpu.SemaphoreType.DMA
    hbm = pl.BlockSpec(memory_space=pltpu.HBM)
    scratch = [
        vm((pixels, LANES), BF16), vm(mask.shape, jnp.int32), vm(index.shape, jnp.int32),
        vm(grad.shape, BF16), vm(weights.shape, F32), vm(gain.shape, F32), vm(bias.shape, F32),
        *(vm(v.shape, F32) for v in moments),
        vm((pixels, LANES), F32),
        vm((layers * maps, rows_w, wide), BF16),
        vm((layers, pixels, channels), BF16),
        vm((layers - 1, chans, pixels, LANES), BF16),
        vm((layers - 1, chans, 8, LANES), F32),
        vm((3, 3, nm, map_rows + 2 * PAD, LANES), F32),
        vm((pixels, LANES), F32),
        vm((layers, pixels, LANES), F32),
        vm((layers, pixels, LANES), F32),
        vm((pixels, LANES), F32),
        vm((pixels, LANES), F32),
        vm((nm * (width // 2), LANES), F32),
        vm((nm, map_rows + 2 * PAD, LANES), F32),
        vm((pixels, wide), BF16),
        vm((layers, channels, wide), F32),
        vm((2, pixels, 2 * LANES), F32),
        vm((2 * layers, maps, 8, LANES), F32),
        vm((layers, 2, pixels, LANES), BF16), vm((layers, 2, pixels, LANES), BF16),
        vm((layers, pixels, LANES), BF16), vm((layers, pixels, LANES), BF16),
        vm((layers, line, rows_w, wide), BF16), vm((layers, line, rows_w, wide), BF16),
        vm((layers, line, rows_w, wide), BF16), vm((layers, line + 1, rows_w, wide), BF16),
        vm((rows_w, wide), F32),
        dma((11,)),
        dma((layers, 2)), dma((layers, line, pieces)), dma((layers,)),
        dma((2 * layers,)), dma((2 * layers,)),
        dma((layers,)), dma((layers, nm + 2)),
        dma((layers - 1,)), dma((layers - 1, chans)),
        dma((layers,)), dma((layers, nm + 1)),
        dma((layers,)), dma((layers, nm)),
        dma((layers,)), dma((layers, line, pieces)),
        dma((layers,)), dma((layers, line + 1, pieces)),
    ]
    arrays = (
        [(index.shape, BF16), ((pixels, LANES), F32)]
        + [(weights.shape, F32)] * 4
        + [(weights.shape, BF16)]
        + [((layers, 2, LANES), F32)] * 4
    )
    return pl.pallas_call(
        functools.partial(block_kernel, sizes),
        out_shape=tuple(jax.ShapeDtypeStruct(*kind) for kind in arrays),
        in_specs=[hbm] * 11,
        out_specs=(pl.BlockSpec(memory_space=pltpu.VMEM),) * len(arrays),
        scratch_shapes=scratch,
        compiler_params=pltpu.CompilerParams(
            collective_id=0, has_side_effects=True, vmem_limit_bytes=48 << 20
        ),
    )(*(
        pltpu.with_memory_space_constraint(v, pltpu.HBM)
        for v in (x.reshape(pixels, LANES), mask, index, grad, weights, gain, bias, *moments)
    ))


def local(
    maps, chans,
    input_maps, valid_mask, pool_index, out_grad, conv_weights, weight_first, weight_second,
    norm_gain, norm_bias, norm_first, norm_second,
):
    nm, half_h, half_w, lanes = pool_index.shape
    by_row = (half_h, half_w * nm, lanes)
    pooled, image, *updates = store_results(
        block_call(
            maps, chans, input_maps, valid_mask.transpose(1, 0, 2),
            pool_index.transpose(1, 2, 0, 3).reshape(by_row),
            out_grad.transpose(1, 2, 0, 3).reshape(by_row),
            conv_weights, norm_gain, norm_bias, weight_first, weight_second, norm_first, norm_second,
        )
    )
    pooled = pooled.reshape(half_h, half_w, nm, lanes).transpose(2, 0, 1, 3)
    return (pooled, image.reshape(input_maps.shape), *updates)


def solution(mesh):
    return jax.shard_map(
        functools.partial(local, mesh.shape["maps"], mesh.shape["chan"]),
        mesh=mesh,
        in_specs=(
            P("maps", None, None, "chan"),
            P("maps", None, None),
            P("maps", None, None, "chan"),
            P("maps", None, None, "chan"),
            P(None, None, "maps", "chan"),
            P(None, None, "maps", "chan"),
            P(None, None, "maps", "chan"),
            P(None, "chan"),
            P(None, "chan"),
            P(None, None, "chan"),
            P(None, None, "chan"),
        ),
        out_specs=(
            P("maps", None, None, "chan"),
            P("maps", None, None, "chan"),
            P(None, None, "maps", "chan"),
            P(None, None, "maps", "chan"),
            P(None, None, "maps", "chan"),
            P(None, None, "maps", "chan"),
            P(None, None, "maps", "chan"),
            P(None, None, "chan"),
            P(None, None, "chan"),
            P(None, None, "chan"),
            P(None, None, "chan"),
        ),
        check_vma=False,
    )
```

time: 138 us -> 122 us (0.88)
  Pallas kernels: 129 us -> 121 us
  other arithmetic: 4.58 us -> 0 us
  local copies, waits for them, and re-layouts: 2.92 us -> 0 us
    pallas_call x1 -> x2, Pallas kernels: 129 us -> 121 us  [the longest x1 119 us: block_call(): pl.pallas_call(functools.partial(block_kernel, sizes), out_shape=tuple((j...]
    convert_element_type x1 -> x0, other arithmetic: 3.98 us -> none  [local(): new_weights.astype(BF16)]
    unnamed x22 -> x0, local copies, waits for them, and re-layouts: 2.92 us -> none
where the time goes in v3:
time: 122 us
  Pallas kernels  121 us (99%)
    pallas_call x1, Pallas kernels, block_call(): pl.pallas_call(functools.partial(block_kernel, sizes), out_shape=tuple((j...  119 us

profile of v3, /device:TPU:0, one launch (start us, length us, event | category | flops | bytes accessed | tf_op | source)
XLA Modules:
  0.0 122.1 jit_solution(11677280198332512078)
XLA Ops:
  0.6 119.0 %shard_map.194 = (bf16[9,24,128]{2,1,0:T(8,128)(2,1)S(1)}, f32[864,128]{1,0:T(8,128)S(1)}, f32[3,9,64,128]{3,2,1,0:T(8,128)S(1)}, f32[3,9,64,128]{3,2,1,0:T(8,12...) custom-call(bf16[864,128]{1,0:T(8,128)(2,1)} %bitcast.12, ...), custom_call_target="tpu_custom_call" | custom-call | tf_op jit(solution)/shard_map/pallas_call | solution.py:932
  119.7 2.2 %shard_map.195 = (bf16[9,24,128]{2,1,0:T(8,128)(2,1)}, f32[864,128]{1,0:T(8,128)}, f32[3,9,64,128]{3,2,1,0:T(8,128)}, f32[3,9,64,128]{3,2,1,0:T(8,128)}, f32[3,9...) custom-call(bf16[9,24,128]{2,1,0:T(8,128)(2,1)S(1)} %get-tuple-eleme, ...), custom_call_target="tpu_custom_call" | custom-call | tf_op jit(solution)/shard_map/pallas_call | solution.py:867

commit v4 on v3

--- a/solution.py
+++ b/solution.py
@@ -121,12 +121,14 @@
     for other in (core, far, across):
         pl.semaphore_signal(barrier, inc=1, device_id=(m, other), device_id_type=MESH)
 
-    loads[0].wait()
+    with scope("load"):
+        loads[0].wait()
     for l in range(layers):
         for t in range(taps):
             wcat[l * maps + m, :, t * LANES : (t + 1) * LANES] = weight_in[l, t].astype(BF16)
 
-    pl.semaphore_wait(barrier, maps + 2)
+    with scope("barrier"):
+        pl.semaphore_wait(barrier, maps + 2)
 
     pieces = wz_r.shape[2]
     piece_rows = rows_w // pieces
@@ -149,35 +151,46 @@
         view = wcat.at[pl.ds(0, count)]
         return remote(view, view, w_s.at[l, place], wx_r.at[l], beside)
 
-    def gather_own(l):
+    def own_along(l):
         for g in range(pieces):
             pl.when(a + 1 < line)(lambda: along(l, a, g, right).start())
             pl.when(a > 0)(lambda: along(l, a, g, left).start())
+
+    def own_aside(l):
+        for g in range(pieces):
             aside(l, a, g).start()
 
-    def gather_step(l, s, g):
+    def own_aside_late(l, late):
+        pl.when(c % 2 == late)(lambda: own_aside(l))
+
+    def step_along(l, s, g):
         def piece(cond, z, onward_cond, onward):
             @pl.when(cond)
             def _():
                 along(l, z, g, onward).wait_recv()
                 pl.when(onward_cond)(lambda: along(l, z, g, onward).start())
-                aside(l, z, g).start()
 
         piece(a >= s, jnp.maximum(a - s, 0), a + 1 < line, right)
         piece(a + s < line, jnp.minimum(a + s, line - 1), a > 0, left)
 
-    def gather_tasks(l):
+    def step_aside(l, s, g):
+        pl.when(a >= s)(lambda: aside(l, jnp.maximum(a - s, 0), g).start())
+        pl.when(a + s < line)(lambda: aside(l, jnp.minimum(a + s, line - 1), g).start())
+
+    def step_both(l, s, g):
+        step_along(l, s, g)
+        step_aside(l, s, g)
+
+    def gather_tasks(step, l):
         if line <= 8:
             return [
-                functools.partial(gather_step, l, s, g)
-                for s in range(1, line)
-                for g in range(pieces)
+                functools.partial(step, l, s, g) for s in range(1, line) for g in range(pieces)
             ]
 
         def everything():
             def go(s):
                 for g in range(pieces):
-                    gather_step(l, s, g)
+                    step(l, s, g)
 
             steps(1, line, go)
 
@@ -256,7 +269,8 @@
         view = scale_ref.at[l, pl.ds(0, 3)]
         remote(view, view, sc_s.at[l], sc_r.at[l, core], (m, core)).wait_send()
 
-    gather_own(0)
+    own_along(0)
+    own_aside(0)
 
     loads[2].wait()
     col_of = lax.broadcasted_iota(jnp.int32, (width, width), 0)
@@ -312,23 +326,33 @@
                         kept == 2 * r + s, value, 0.0
                     )
 
-    tasks = gather_tasks(0)
+    tasks = gather_tasks(step_both, 0)
+    z_tasks = {l: gather_tasks(step_along, l) for l in range(1, layers)}
+    x_tasks = {l: gather_tasks(step_aside, l) for l in range(1, layers)}
     with scope("gather0"):
+        run(tasks, 2 * pieces)
+        if layers > 1:
+            own_along(1)
         run(tasks)
+    if layers > 1:
+        own_aside_late(1, 0)
     for n in range(nm):
         act_forward(0, n)
+    if layers > 1:
+        with scope("along_1"):
+            run(z_tasks[1], pieces)
     with scope("gather0_end"):
         gather_finish(0)
+    if layers > 1:
+        own_aside_late(1, 1)
     act_near(0)
     act_across(0)
     for cp in loads[5:]:
         cp.wait()
 
     for l in range(layers):
-        tasks = []
-        if l + 1 < layers:
-            gather_own(l + 1)
-            tasks = gather_tasks(l + 1)
+        z_near, x_near = z_tasks.get(l + 1, []), x_tasks.get(l + 1, [])
+        z_next = z_tasks.get(l + 2, [])
 
         @pl.loop(0, 3)
         def _(i):
@@ -384,7 +408,13 @@
         )
         stat_send(l)
         with scope("gather_a"):
-            run(tasks, pieces)
+            done = len(x_near) - len(z_near)
+            run(x_near, done)
+            if l + 2 < layers:
+                own_along(l + 2)
+            if len(z_near) > pieces:
+                run(z_near, pieces)
+                run(x_near, pieces)
         with scope("stat_wait"):
             stat_wait(l)
 
@@ -450,7 +480,8 @@
                 scale_wait(l, core)
                 activate(core, 0, nm)
             with scope("gather_b"):
-                run(tasks, 1)
+                run(z_near)
+                run(x_near)
             with scope("act_far"):
                 for n in range(nm):
                     act_forward(l + 1, n)
@@ -458,15 +489,17 @@
                         scale_wait(l, far)
                     activate(far, n, n + 1)
             with scope("gather_c"):
-                run(tasks, 2)
+                run(z_next, pieces)
             with scope("act_across"):
                 act_across(l + 1)
                 scale_wait(l, across)
                 activate(across, 0, nm)
-            with scope("gather_d"):
-                run(tasks)
+            if l + 2 < layers:
+                own_aside_late(l + 2, 0)
             with scope("gather_end"):
                 gather_finish(l + 1)
+            if l + 2 < layers:
+                own_aside_late(l + 2, 1)
 
     def pool():
         @pl.loop(0, half_h)
@@ -539,15 +572,26 @@
                 kernel_grad(l, z * tile, tile)
             for g in range(pieces):
                 gx_out[l, z, part_of(g)] = shard(l, z * 2 + 1 - b, g).astype(BF16)
-                if send:
+            if send:
+                for g in range(pieces):
                     gx_copy(l, z, g).start()
+            else:
+
+                @pl.when(z == farthest)
+                def _():
+                    for g in range(pieces):
+                        gx_copy(l, z, g).start()
 
         far_first(go)
+
+    farthest = jnp.where(a < line // 2, line - 1, 0)
 
     def scatter_x(l):
         def go(z):
-            for g in range(pieces):
-                gx_copy(l, z, g).start()
+            @pl.when(z != farthest)
+            def _():
+                for g in range(pieces):
+                    gx_copy(l, z, g).start()
 
         far_first(go)
 

time: 122 us -> 115 us (0.943)
  Pallas kernels: 121 us -> 114 us
    pallas_call x1, Pallas kernels: 119 us -> 112 us  [block_call(): pl.pallas_call(functools.partial(block_kernel, sizes), out_shape=tuple((j...]
where the time goes in v4:
time: 115 us
  Pallas kernels  114 us (99%)
    pallas_call x1, Pallas kernels, block_call(): pl.pallas_call(functools.partial(block_kernel, sizes), out_shape=tuple((j...  112 us

profile of v4, /device:TPU:0, one launch (start us, length us, event | category | flops | bytes accessed | tf_op | source)
XLA Modules:
  0.0 115.1 jit_solution(17260294378270580943)
XLA Ops:
  0.6 112.0 %shard_map.194 = (bf16[9,24,128]{2,1,0:T(8,128)(2,1)S(1)}, f32[864,128]{1,0:T(8,128)S(1)}, f32[3,9,64,128]{3,2,1,0:T(8,128)S(1)}, f32[3,9,64,128]{3,2,1,0:T(8,12...) custom-call(bf16[864,128]{1,0:T(8,128)(2,1)} %bitcast.12, ...), custom_call_target="tpu_custom_call" | custom-call | tf_op jit(solution)/shard_map/pallas_call | solution.py:976
  112.7 2.2 %shard_map.195 = (bf16[9,24,128]{2,1,0:T(8,128)(2,1)}, f32[864,128]{1,0:T(8,128)}, f32[3,9,64,128]{3,2,1,0:T(8,128)}, f32[3,9,64,128]{3,2,1,0:T(8,128)}, f32[3,9...) custom-call(bf16[9,24,128]{2,1,0:T(8,128)(2,1)S(1)} %get-tuple-eleme, ...), custom_call_target="tpu_custom_call" | custom-call | tf_op jit(solution)/shard_map/pallas_call | solution.py:911

commit v5 on v4

--- a/solution.py
+++ b/solution.py
@@ -61,7 +61,7 @@
     ngrad_ref, nfirst_ref, nsecond_ref, nnew_ref,
     x_in, mask_in, index_in, grad_in, weight_in, gain_in, bias_in,
     first_in, second_in, norm_first_in, norm_second_in,
-    mask_ref, wcat, act, raw, scale_ref, prod, conv, normed, slope, result_ref, spread, pool32, zpad, dcat,
+    mask_ref, wcat, turned, act, raw, scale_ref, prod, conv, normed, slope, result_ref, spread, pool32, zpad, dcat,
     grad_w, part, stat, pair_out, pair_in, far_out, far_in,
     gx_out, gx_in, gz_out, gz_in, total_w,
     in_sem,
@@ -206,12 +206,26 @@
         pl.when(jnp.logical_not(inner))(lambda: shards_of(l, 1, 0).wait_send())
 
     def stat_send(e):
+        view = stat.at[e, m]
+
+        def send(peer):
+            remote(view, view, st_s.at[e], st_r.at[e], (peer, c)).start()
+
         def go(d):
-            peer = lax.rem(m + d, maps)
-            view = stat.at[e, m]
-            remote(view, view, st_s.at[e], st_r.at[e], (peer, c)).start()
-
-        steps(1, maps, go)
+            @pl.when(a + line - d < line)
+            def _():
+                first = jnp.minimum(a + line - d, line - 1) * 2
+                send(first + 1 - b)
+                send(first + b)
+
+            @pl.when(a >= line - d)
+            def _():
+                first = jnp.maximum(a - line + d, 0) * 2
+                send(first + 1 - b)
+                send(first + b)
+
+        steps(1, line, go)
+        send(m + 1 - 2 * b)
 
     def stat_all(e):
         view = stat.at[e, pl.ds(0, maps - 1)]
@@ -354,16 +368,15 @@
         z_near, x_near = z_tasks.get(l + 1, []), x_tasks.get(l + 1, [])
         z_next = z_tasks.get(l + 2, [])
 
-        @pl.loop(0, 3)
-        def _(i):
-            cols = pl.ds(pl.multiple_of(i * (3 * LANES), LANES), 3 * LANES)
-            w = wcat[l * maps : (l + 1) * maps, :, cols].reshape(maps * rows_w, 3 * LANES)
-            for n in range(nm):
-                out = jnp.dot(
-                    act[l, pl.ds(n * map_rows, map_rows), :], w, preferred_element_type=F32
-                )
+        kernel = wcat[l * maps : (l + 1) * maps, :, :].reshape(maps * rows_w, wide)
+        for n in range(nm):
+            out = jnp.dot(
+                act[l, pl.ds(n * map_rows, map_rows), :], kernel, preferred_element_type=F32
+            )
+            for i in range(3):
                 for j in range(3):
-                    prod[i, j, n, PAD : PAD + map_rows, :] = out[:, j * LANES : (j + 1) * LANES]
+                    t = 3 * i + j
+                    prod[i, j, n, PAD : PAD + map_rows, :] = out[:, t * LANES : (t + 1) * LANES]
 
         def conv_chunk(i, carry):
             total, count = carry
@@ -415,6 +428,12 @@
             if len(z_near) > pieces:
                 run(z_near, pieces)
                 run(x_near, pieces)
+        with scope("turn"):
+            slots = LANES // rows_w
+            for i in range(maps // slots):
+                turned[l, :, i * LANES : (i + 1) * LANES] = (
+                    wcat[l * maps + i * slots : l * maps + (i + 1) * slots, :, :].reshape(LANES, wide).T
+                )
         with scope("stat_wait"):
             stat_wait(l)
 
@@ -519,20 +538,15 @@
                 pool32[pick, :] = total
             pooled_ref[h] = pool32[...].astype(BF16)
 
-    def far_first(body):
-        def go(e):
-            d = line - e
-
-            @pl.when(a + d < line)
-            def _():
-                body(jnp.minimum(a + d, line - 1))
-
-            @pl.when(a >= d)
-            def _():
-                body(jnp.maximum(a - d, 0))
-
-        steps(1, line, go)
-        body(a)
+    def kth_place(k):
+        before, after = a, line - 1 - a
+        spare = jnp.maximum(before, after) - jnp.minimum(before, after)
+        q = jnp.maximum(k - spare, 0)
+        near, side = q // 2, q % 2
+        low = jnp.where(before > after, spare, 0) + near
+        high = line - 1 - jnp.where(before < after, spare, 0) - near
+        outer = jnp.where(before > after, k, line - 1 - k)
+        return jnp.where(k < spare, outer, jnp.where(side == 0, high, low))
 
     def part_of(g):
         return pl.ds(g * piece_rows, piece_rows)
@@ -562,82 +576,77 @@
             act[l, :, rows], dcat[...], (((0,), (0,)), ((), ())), preferred_element_type=F32
         )
 
-    def kernel_grads(l, send):
-        if not fine:
+    def kernel_grads(l, low=0, high=None):
+        high = line if high is None else high
+        if not fine and low == 0:
             coarse = (maps * rows_w) // 4
             pl.loop(0, 4)(lambda i: kernel_grad(l, i * coarse, coarse))
 
-        def go(z):
+        def go(k):
+            z = kth_place(k)
             if fine:
                 kernel_grad(l, z * tile, tile)
             for g in range(pieces):
                 gx_out[l, z, part_of(g)] = shard(l, z * 2 + 1 - b, g).astype(BF16)
-            if send:
+            for g in range(pieces):
+                if line > 8 or is_early(l, k, g):
+                    gx_copy(l, z, g).start()
+
+        steps(low, high, go)
+
+    def is_early(l, k, g):
+        return l == 0 or k < 2
+
+    def scatter_x(l):
+        if line <= 8:
+            for k in range(line):
                 for g in range(pieces):
-                    gx_copy(l, z, g).start()
-            else:
-
-                @pl.when(z == farthest)
-                def _():
-                    for g in range(pieces):
-                        gx_copy(l, z, g).start()
-
-        far_first(go)
-
-    farthest = jnp.where(a < line // 2, line - 1, 0)
-
-    def scatter_x(l):
-        def go(z):
-            @pl.when(z != farthest)
-            def _():
-                for g in range(pieces):
-                    gx_copy(l, z, g).start()
-
-        far_first(go)
+                    if not is_early(l, k, g):
+                        gx_copy(l, kth_place(k), g).start()
 
     def pair_sum(l, z, g):
         gx_copy(l, z, g).wait_recv()
         return shard(l, z * 2 + b, g) + gx_in[l, z, part_of(g)].astype(F32)
 
-    def onward(l, z, g, has_more, dev, slot):
-        @pl.when(has_more)
-        def _():
+    def onward(l, z, g, fed, dev, slot):
+        value = pair_sum(l, z, g)
+        if fed:
             gz_copy(l, z, g, z, dev).wait_recv()
-            gz_out[l, z, part_of(g)] = (
-                pair_sum(l, z, g) + gz_in[l, z, part_of(g)].astype(F32)
-            ).astype(BF16)
-
-        @pl.when(jnp.logical_not(has_more))
-        def _():
-            gz_out[l, z, part_of(g)] = pair_sum(l, z, g).astype(BF16)
-
+            value = value + gz_in[l, z, part_of(g)].astype(F32)
+        gz_out[l, z, part_of(g)] = value.astype(BF16)
         gz_copy(l, z, g, slot, dev).start()
 
-    def scatter_step(l, d, g):
-        @pl.when(a + d < line)
-        def _():
-            z = jnp.minimum(a + d, line - 1)
-            onward(l, z, g, a > 0, right, z)
-
-        @pl.when(a >= d)
-        def _():
-            z = jnp.maximum(a - d, 0)
-            onward(l, z, g, a + 1 < line, left, jnp.where(z == a - 1, line, z))
+    def straight(l):
+        return l == 0 and 2 < line <= 8
+
+    def scatter_step(l, d, g, fed):
+        ends = straight(l) and d == line - 1
+        zr, zl = jnp.minimum(a + d, line - 1), jnp.maximum(a - d, 0)
+        more_r, more_l = a > 0, a + 1 < line
+        if straight(l):
+            more_r = jnp.where(zr == line - 1, a > 1, more_r)
+            more_l = jnp.where(zl == 0, a + 2 < line, more_l)
+        for there, z, more, dev, slot in (
+            (a + d < line, zr, more_r, right, zr),
+            (a >= d, zl, more_l, left, jnp.where(zl == a - 1, line, zl)),
+        ):
+            if ends:
+                dev, slot = (z * 2 + b, c), line + 1
+            now = jnp.logical_and(there, more if fed else jnp.logical_not(more))
+            pl.when(now)(functools.partial(onward, l, z, g, fed, dev, slot))
 
     def scatter_own(l, g):
         r = part_of(g)
         total_w[r, :] = pair_sum(l, a, g)
 
-        @pl.when(a > 0)
-        def _():
-            gz_copy(l, a, g, a, left).wait_recv()
-            total_w[r, :] += gz_in[l, a, r].astype(F32)
-
-        @pl.when(a + 1 < line)
-        def _():
-            gz_copy(l, a, g, line, right).wait_recv()
-            total_w[r, :] += gz_in[l, line, r].astype(F32)
-
+        def add(slot):
+            gz_copy(l, a, g, slot, left).wait_recv()
+            total_w[r, :] += gz_in[l, slot, r].astype(F32)
+
+        pl.when(a > 0)(lambda: add(a))
+        pl.when(a + 1 < line)(lambda: add(line))
+        if straight(l):
+            pl.when(jnp.logical_or(a == 0, a + 1 == line))(lambda: add(line + 1))
         for t in range(taps):
             gradient = total_w[r, t * LANES : (t + 1) * LANES]
             new, first, second = adamw_update(
@@ -652,20 +661,25 @@
     def scatter_tasks(l):
         owns = [functools.partial(scatter_own, l, g) for g in range(pieces)]
         if line <= 8:
-            return [
-                functools.partial(scatter_step, l, line - e, g)
-                for e in range(1, line)
-                for g in range(pieces)
-            ], owns
+            first, fed = (
+                [
+                    functools.partial(scatter_step, l, line - e, g, kind)
+                    for e in range(1 + kind, line)
+                    for g in range(pieces)
+                ]
+                for kind in (False, True)
+            )
+            return first, fed, owns
 
         def everything():
             def go(e):
                 for g in range(pieces):
-                    scatter_step(l, line - e, g)
+                    scatter_step(l, line - e, g, False)
+                    scatter_step(l, line - e, g, True)
 
             steps(1, line, go)
 
-        return [everything], owns
+        return [everything], [], owns
 
     def scatter_drain(l):
         remote(gx_out.at[l], gx_in.at[l], gx_s.at[l], gx_r.at[l, 0, 0], beside).wait_send()
@@ -699,7 +713,7 @@
             fr_s.at[l], fr_r.at[l, n], (m, far),
         )
 
-    todo, owns = {}, {}
+    todo, fed, owns = {}, {}, {}
     for l in reversed(range(layers)):
         e = layers + l
         source = spread if l == layers - 1 else back
@@ -726,10 +740,13 @@
         else:
             pool()
         if l + 1 < layers:
-            todo[l + 1], owns[l + 1] = scatter_tasks(l + 1)
+            todo[l + 1], fed[l + 1], owns[l + 1] = scatter_tasks(l + 1)
         if l + 2 < layers:
-            with scope("scatter_last"):
-                run(todo[l + 2])
+            run(todo[l + 2])
+            run(fed[l + 2])
+        if l + 1 < layers:
+            with scope("scatter_a"):
+                run(todo[l + 1], pieces)
         with scope("stat_wait_back"):
             stat_wait(e)
 
@@ -771,11 +788,10 @@
 
         def input_grad(h, n):
             start = other_half if h == 0 else own_half
-            slots = maps // 2
-            w = wcat[pl.ds(l * maps + (start // half) * slots, slots), :, :].reshape(half, wide)
             r = pl.ds(n * map_rows, map_rows)
-            part[h, r, :] = lax.dot_general(
-                dcat[r, :], w, (((1,), (1,)), ((), ())), preferred_element_type=F32
+            part[h, r, :] = jnp.dot(
+                dcat[r, :], turned[l, :, pl.ds(pl.multiple_of(start, half), half)],
+                preferred_element_type=F32,
             )
             pair_out[l, h, r, :] = part[h, r, lane_out_half].astype(BF16)
             pair_copy(l, h, n).start()
@@ -797,20 +813,22 @@
                 if n > 0:
                     with scope("to_far"):
                         to_far(n - 1)
+            if l + 1 < layers:
+                with scope("scatter_b"):
+                    run(todo[l + 1], pieces)
+                    run(fed[l + 1], pieces)
+            with scope("kernel_grad"):
+                kernel_grads(l, 0, line // 2)
+            with scope("to_far"):
+                to_far(nm - 1)
+            if l + 1 < layers:
+                with scope("scatter_c"):
+                    run(todo[l + 1])
+            with scope("kernel_grad"):
+                kernel_grads(l, line // 2)
             for n in range(nm):
                 with scope("input_grad"):
                     input_grad(1, n)
-                if n == 0:
-                    with scope("to_far"):
-                        to_far(nm - 1)
-                    if l + 1 < layers:
-                        with scope("scatter_step"):
-                            run(todo[l + 1], pieces)
-            with scope("kernel_grad"):
-                kernel_grads(l, False)
-            if l + 1 < layers:
-                with scope("scatter_step"):
-                    run(todo[l + 1], pieces)
             with scope("drain"):
                 if l + 1 == layers:
                     for k in range(layers):
@@ -825,35 +843,35 @@
             for n in range(nm):
                 with scope("conv_grad"):
                     conv_grad(n)
-            with scope("scatter_1a"):
+            with scope("scatter_1b"):
                 run(todo[1], pieces)
             with scope("kernel_grad"):
-                kernel_grads(0, True)
-            todo[0], owns[0] = scatter_tasks(0)
-            with scope("scatter_1b"):
-                run(todo[1], pieces)
+                kernel_grads(0)
+            todo[0], fed[0], owns[0] = scatter_tasks(0)
+            with scope("scatter_1c"):
+                run(todo[1])
+                run(fed[1], pieces)
             for n in range(nm):
                 with scope("input_grad"):
                     input_grad(0, n)
-            with scope("scatter_1c"):
-                run(todo[1])
             with scope("to_far"):
                 for n in range(nm):
                     to_far(n)
+            with scope("input_grad"):
+                input_grad(1, 0)
             with scope("scatter_0a"):
                 run(todo[0], pieces)
-            for n in range(nm):
-                with scope("input_grad"):
+            with scope("scatter_1d"):
+                run(fed[1])
+            with scope("input_grad"):
+                for n in range(1, nm):
                     input_grad(1, n)
-            with scope("owns"):
-                for k in range(layers - 1, 0, -1):
-                    run(owns[k])
             with scope("scatter_0b"):
                 run(todo[0], pieces)
-            with scope("drain"):
-                for k in range(1, layers):
-                    scatter_drain(k)
-                layer_drain(1)
+                run(fed[0], pieces)
+            with scope("owns_2"):
+                for k in range(layers - 1, 1, -1):
+                    run(owns[k])
 
         for n in range(nm):
             r = pl.ds(n * map_rows, map_rows)
@@ -863,6 +881,9 @@
                         pair_out.at[l, 1], pair_in.at[l, 1], pr_s.at[l], pr_r.at[l, nm], (m, core)
                     ).wait_recv()
                 far_copy(l, n).wait_recv()
+            if n == 0 and l > 0 and l + 1 < layers:
+                with scope("scatter_d"):
+                    run(fed[l + 1])
 
             @pl.loop(n * per_map, (n + 1) * per_map)
             def _(i):
@@ -887,6 +908,14 @@
             nnew_ref[:, place, :] = new
     with scope("scatter_end"):
         run(todo[0])
+        run(fed[0])
+    with scope("owns_1"):
+        for k in range(1, min(2, layers)):
+            run(owns[k])
+    with scope("drain"):
+        for k in range(1, layers):
+            scatter_drain(k)
+        layer_drain(1)
     with scope("owns"):
         run(owns[0])
 
@@ -937,6 +966,7 @@
         *(vm(v.shape, F32) for v in moments),
         vm((pixels, LANES), F32),
         vm((layers * maps, rows_w, wide), BF16),
+        vm((layers, wide, channels), BF16),
         vm((layers, pixels, channels), BF16),
         vm((layers - 1, chans, pixels, LANES), BF16),
         vm((layers - 1, chans, 8, LANES), F32),
@@ -955,7 +985,7 @@
         vm((layers, 2, pixels, LANES), BF16), vm((layers, 2, pixels, LANES), BF16),
         vm((layers, pixels, LANES), BF16), vm((layers, pixels, LANES), BF16),
         vm((layers, line, rows_w, wide), BF16), vm((layers, line, rows_w, wide), BF16),
-        vm((layers, line, rows_w, wide), BF16), vm((layers, line + 1, rows_w, wide), BF16),
+        vm((layers, line, rows_w, wide), BF16), vm((layers, line + 2, rows_w, wide), BF16),
         vm((rows_w, wide), F32),
         dma((11,)),
         dma((layers, 2)), dma((layers, line, pieces)), dma((layers,)),
@@ -965,7 +995,7 @@
         dma((layers,)), dma((layers, nm + 1)),
         dma((layers,)), dma((layers, nm)),
         dma((layers,)), dma((layers, line, pieces)),
-        dma((layers,)), dma((layers, line + 1, pieces)),
+        dma((layers,)), dma((layers, line + 2, pieces)),
     ]
     arrays = (
         [(index.shape, BF16), ((pixels, LANES), F32)]

time: 115 us -> 111 us (0.965)
  Pallas kernels: 114 us -> 110 us
    pallas_call x1, Pallas kernels: 112 us -> 108 us  [block_call(): pl.pallas_call(functools.partial(block_kernel, sizes), out_shape=tuple((j...]
where the time goes in v5:
time: 111 us
  Pallas kernels  110 us (99%)
    pallas_call x1, Pallas kernels, block_call(): pl.pallas_call(functools.partial(block_kernel, sizes), out_shape=tuple((j...  108 us

profile of v5, /device:TPU:0, one launch (start us, length us, event | category | flops | bytes accessed | tf_op | source)
XLA Modules:
  0.0 110.8 jit_solution(4613994045585461823)
XLA Ops:
  0.6 107.8 %shard_map.194 = (bf16[9,24,128]{2,1,0:T(8,128)(2,1)S(1)}, f32[864,128]{1,0:T(8,128)S(1)}, f32[3,9,64,128]{3,2,1,0:T(8,128)S(1)}, f32[3,9,64,128]{3,2,1,0:T(8,12...) custom-call(bf16[864,128]{1,0:T(8,128)(2,1)} %bitcast.12, ...), custom_call_target="tpu_custom_call" | custom-call | tf_op jit(solution)/shard_map/pallas_call | solution.py:1006
  108.5 2.2 %shard_map.195 = (bf16[9,24,128]{2,1,0:T(8,128)(2,1)}, f32[864,128]{1,0:T(8,128)}, f32[3,9,64,128]{3,2,1,0:T(8,128)}, f32[3,9,64,128]{3,2,1,0:T(8,128)}, f32[3,9...) custom-call(bf16[9,24,128]{2,1,0:T(8,128)(2,1)S(1)} %get-tuple-eleme, ...), custom_call_target="tpu_custom_call" | custom-call | tf_op jit(solution)/shard_map/pallas_call | solution.py:940

commit v6 on v5

--- a/solution.py
+++ b/solution.py
@@ -65,7 +65,7 @@
     grad_w, part, stat, pair_out, pair_in, far_out, far_in,
     gx_out, gx_in, gz_out, gz_in, total_w,
     in_sem,
-    w_s, wz_r, wx_r, st_s, st_r, ag_s, ag_r, sc_s, sc_r, pr_s, pr_r, fr_s, fr_r,
+    w_s, wz_r, wx_r, wc_r, st_s, st_r, ag_s, ag_r, sc_s, sc_r, pr_s, pr_r, fr_s, fr_r,
     gx_s, gx_r, gz_s, gz_r,
 ):
     maps, chans, layers, taps, nm, height, width = sizes
@@ -135,21 +135,28 @@
     right = (jnp.minimum(m + 2, maps - 1), c)
     left = (jnp.maximum(m - 2, 0), c)
     beside = (m + 1 - 2 * b, c)
-
-    def weight_view(l, slot, g):
-        return wcat.at[l * maps + slot, pl.ds(g * piece_rows, piece_rows)]
+    opposite = ((line - 1 - a) * 2 + b, c)
+    straight_cross = line == 4
+
+    def crossing(l):
+        return (1 if l == 0 else 2) * LANES
 
     def along(l, z, g, dev):
-        view = weight_view(l, z * 2 + b, g)
+        view = wcat.at[l * maps + z * 2 + b, pl.ds(g * piece_rows, piece_rows)]
         return remote(view, view, w_s.at[l, 0], wz_r.at[l, z, g], dev)
 
     def aside(l, z, g):
-        view = weight_view(l, z * 2 + b, g)
-        return remote(view, view, w_s.at[l, 1], wx_r.at[l], beside)
-
-    def shards_of(l, count, place):
-        view = wcat.at[pl.ds(0, count)]
-        return remote(view, view, w_s.at[l, place], wx_r.at[l], beside)
+        lanes = pl.ds(crossing(l), wide - crossing(l))
+        view = wcat.at[l * maps + z * 2 + b, pl.ds(g * piece_rows, piece_rows), lanes]
+        return remote(view, view, w_s.at[l, 1], wx_r.at[l, 0], beside)
+
+    def aside_own(l, slot):
+        view = wcat.at[l * maps + slot]
+        return remote(view, view, w_s.at[l, 2], wx_r.at[l, 1], beside)
+
+    def across_line(l, z, dev):
+        view = wcat.at[l * maps + z * 2 + 1 - b, :, pl.ds(0, crossing(l))]
+        return remote(view, view, w_s.at[l, 3], wc_r.at[l, z], dev)
 
     def own_along(l):
         for g in range(pieces):
@@ -157,29 +164,55 @@
             pl.when(a > 0)(lambda: along(l, a, g, left).start())
 
     def own_aside(l):
-        for g in range(pieces):
-            aside(l, a, g).start()
+        aside_own(l, m).start()
 
     def own_aside_late(l, late):
         pl.when(c % 2 == late)(lambda: own_aside(l))
 
-    def step_along(l, s, g):
-        def piece(cond, z, onward_cond, onward):
-            @pl.when(cond)
+    def flows(s, body):
+        body(a >= s, jnp.maximum(a - s, 0), a + 1 < line, right)
+        body(a + s < line, jnp.minimum(a + s, line - 1), a > 0, left)
+
+    def step_along(l, s, g, both=False):
+        def piece(there, z, on, dev):
+            @pl.when(there)
             def _():
-                along(l, z, g, onward).wait_recv()
-                pl.when(onward_cond)(lambda: along(l, z, g, onward).start())
-
-        piece(a >= s, jnp.maximum(a - s, 0), a + 1 < line, right)
-        piece(a + s < line, jnp.minimum(a + s, line - 1), a > 0, left)
+                along(l, z, g, dev).wait_recv()
+                pl.when(on)(lambda: along(l, z, g, dev).start())
+                if both:
+                    aside(l, z, g).start()
+
+        flows(s, piece)
 
     def step_aside(l, s, g):
-        pl.when(a >= s)(lambda: aside(l, jnp.maximum(a - s, 0), g).start())
-        pl.when(a + s < line)(lambda: aside(l, jnp.minimum(a + s, line - 1), g).start())
+        flows(s, lambda there, z, on, dev: pl.when(there)(lambda: aside(l, z, g).start()))
 
     def step_both(l, s, g):
-        step_along(l, s, g)
-        step_aside(l, s, g)
+        step_along(l, s, g, True)
+
+    def own_cross(l):
+        aside_own(l, m + 1 - 2 * b).wait_recv()
+        pl.when(a + 1 < line)(lambda: across_line(l, a, right).start())
+        pl.when(a > 0)(lambda: across_line(l, a, left).start())
+        if straight_cross:
+            pl.when(jnp.logical_or(a == 0, a + 1 == line))(
+                lambda: across_line(l, a, opposite).start()
+            )
+
+    def step_cross(l, s):
+        def piece(there, z, on, dev):
+            if straight_cross:
+                far_end = jnp.logical_or(
+                    jnp.logical_and(z == 0, a + 2 == line), jnp.logical_and(z + 1 == line, a == 1)
+                )
+                on = jnp.logical_and(on, jnp.logical_not(far_end))
+
+            @pl.when(there)
+            def _():
+                across_line(l, z, dev).wait_recv()
+                pl.when(on)(lambda: across_line(l, z, dev).start())
+
+        flows(s, piece)
 
     def gather_tasks(step, l):
         if line <= 8:
@@ -196,14 +229,42 @@
 
         return [everything]
 
+    def cross_tasks(l):
+        if line <= 8:
+            return [functools.partial(own_cross, l)] + [
+                functools.partial(step_cross, l, s) for s in range(1, line)
+            ]
+        return [
+            functools.partial(own_cross, l),
+            lambda: steps(1, line, lambda s: step_cross(l, s)),
+        ]
+
+    def rest_of(l):
+        lanes = pl.ds(crossing(l), wide - crossing(l))
+        view = wcat.at[pl.ds(0, line - 1), :, lanes]
+        return remote(view, view, w_s.at[l, 1], wx_r.at[l, 0], beside)
+
     def gather_finish(l):
-        shards_of(l, line, 1).wait_recv()
+        rest_of(l).wait_recv()
 
     def gather_drain(l):
-        shards_of(l, line, 1).wait_send()
+        rest_of(l).wait_send()
+        aside_own(l, m).wait_send()
         inner = jnp.logical_and(a > 0, a + 1 < line)
-        pl.when(inner)(lambda: shards_of(l, line + 1, 0).wait_send())
-        pl.when(jnp.logical_not(inner))(lambda: shards_of(l, 1, 0).wait_send())
+
+        def lines(count):
+            view = wcat.at[pl.ds(0, count)]
+            remote(view, view, w_s.at[l, 0], wx_r.at[l, 0], beside).wait_send()
+
+        def crossed(count):
+            view = wcat.at[pl.ds(0, count), :, pl.ds(0, crossing(l))]
+            remote(view, view, w_s.at[l, 3], wx_r.at[l, 0], beside).wait_send()
+
+        for at, count in ((inner, line + 1), (jnp.logical_not(inner), 1)):
+            pl.when(at)(functools.partial(lines, count))
+        counts = (line, 2) if straight_cross else (line + 1, 1)
+        for at, count in zip((inner, jnp.logical_not(inner)), counts):
+            pl.when(at)(functools.partial(crossed, count))
 
     def stat_send(e):
         view = stat.at[e, m]
@@ -343,10 +404,14 @@
     tasks = gather_tasks(step_both, 0)
     z_tasks = {l: gather_tasks(step_along, l) for l in range(1, layers)}
     x_tasks = {l: gather_tasks(step_aside, l) for l in range(1, layers)}
+    c_tasks = {l: cross_tasks(l) for l in range(layers)}
     with scope("gather0"):
-        run(tasks, 2 * pieces)
+        run(tasks, pieces)
+        run(c_tasks[0], 1)
+        run(tasks, pieces)
         if layers > 1:
             own_along(1)
+        run(c_tasks[0], 1)
         run(tasks)
     if layers > 1:
         own_aside_late(1, 0)
@@ -355,6 +420,8 @@
     if layers > 1:
         with scope("along_1"):
             run(z_tasks[1], pieces)
+    with scope("gather0_cross"):
+        run(c_tasks[0])
     with scope("gather0_end"):
         gather_finish(0)
     if layers > 1:
@@ -421,10 +488,7 @@
         )
         stat_send(l)
         with scope("gather_a"):
-            done = len(x_near) - len(z_near)
-            run(x_near, done)
-            if l + 2 < layers:
-                own_along(l + 2)
+            run(x_near, len(x_near) - len(z_near))
             if len(z_near) > pieces:
                 run(z_near, pieces)
                 run(x_near, pieces)
@@ -434,6 +498,11 @@
                 turned[l, :, i * LANES : (i + 1) * LANES] = (
                     wcat[l * maps + i * slots : l * maps + (i + 1) * slots, :, :].reshape(LANES, wide).T
                 )
+        if l + 1 < layers:
+            with scope("gather_own_cross"):
+                run(c_tasks[l + 1], 1)
+                if l + 2 < layers:
+                    own_along(l + 2)
         with scope("stat_wait"):
             stat_wait(l)
 
@@ -501,6 +570,7 @@
             with scope("gather_b"):
                 run(z_near)
                 run(x_near)
+                run(c_tasks[l + 1], 1)
             with scope("act_far"):
                 for n in range(nm):
                     act_forward(l + 1, n)
@@ -508,17 +578,18 @@
                         scale_wait(l, far)
                     activate(far, n, n + 1)
             with scope("gather_c"):
+                run(c_tasks[l + 1], 1)
+                if l + 2 < layers:
+                    own_aside(l + 2)
                 run(z_next, pieces)
             with scope("act_across"):
                 act_across(l + 1)
                 scale_wait(l, across)
                 activate(across, 0, nm)
-            if l + 2 < layers:
-                own_aside_late(l + 2, 0)
+            with scope("gather_cross"):
+                run(c_tasks[l + 1])
             with scope("gather_end"):
                 gather_finish(l + 1)
-            if l + 2 < layers:
-                own_aside_late(l + 2, 1)
 
     def pool():
         @pl.loop(0, half_h)
@@ -538,7 +609,7 @@
                 pool32[pick, :] = total
             pooled_ref[h] = pool32[...].astype(BF16)
 
-    def kth_place(k):
+    def place_of(k):
         before, after = a, line - 1 - a
         spare = jnp.maximum(before, after) - jnp.minimum(before, after)
         q = jnp.maximum(k - spare, 0)
@@ -548,6 +619,16 @@
         outer = jnp.where(before > after, k, line - 1 - k)
         return jnp.where(k < spare, outer, jnp.where(side == 0, high, low))
 
+    places = {False: [place_of(k) for k in range(line)] if line <= 8 else []}
+    places[True] = list(places[False])
+    if 2 < line <= 8:
+        ends = jnp.logical_or(a == 0, a + 1 == line)
+        places[True][0] = jnp.where(ends, places[False][1], places[False][0])
+        places[True][1] = jnp.where(ends, places[False][0], places[False][1])
+
+    def kth_place(k, l):
+        return places[straight(l)][k] if line <= 8 else place_of(k)
+
     def part_of(g):
         return pl.ds(g * piece_rows, piece_rows)
 
@@ -583,7 +664,7 @@
             pl.loop(0, 4)(lambda i: kernel_grad(l, i * coarse, coarse))
 
         def go(k):
-            z = kth_place(k)
+            z = kth_place(k, l)
             if fine:
                 kernel_grad(l, z * tile, tile)
             for g in range(pieces):
@@ -602,7 +683,7 @@
             for k in range(line):
                 for g in range(pieces):
                     if not is_early(l, k, g):
-                        gx_copy(l, kth_place(k), g).start()
+                        gx_copy(l, kth_place(k, l), g).start()
 
     def pair_sum(l, z, g):
         gx_copy(l, z, g).wait_recv()
@@ -664,7 +745,8 @@
             first, fed = (
                 [
                     functools.partial(scatter_step, l, line - e, g, kind)
-                    for e in range(1 + kind, line)
+                    for e in ((2, 1, *range(3, line)) if straight(l) else range(1, line))
+                    if e > kind + (kind and straight(l))
                     for g in range(pieces)
                 ]
                 for kind in (False, True)
@@ -746,7 +828,7 @@
             run(fed[l + 2])
         if l + 1 < layers:
             with scope("scatter_a"):
-                run(todo[l + 1], pieces)
+                run(todo[l + 1], pieces if l > 0 else 2 * pieces)
         with scope("stat_wait_back"):
             stat_wait(e)
 
@@ -786,15 +868,16 @@
                         t = 3 * k + j
                         dcat[r, t * LANES : (t + 1) * LANES] = term.astype(BF16)
 
-        def input_grad(h, n):
+        def input_grad(h, first, last):
             start = other_half if h == 0 else own_half
-            r = pl.ds(n * map_rows, map_rows)
+            r = pl.ds(first * map_rows, (last - first) * map_rows)
             part[h, r, :] = jnp.dot(
                 dcat[r, :], turned[l, :, pl.ds(pl.multiple_of(start, half), half)],
                 preferred_element_type=F32,
             )
             pair_out[l, h, r, :] = part[h, r, lane_out_half].astype(BF16)
-            pair_copy(l, h, n).start()
+            for n in range(first, last):
+                pair_copy(l, h, n).start()
 
         def to_far(n):
             r = pl.ds(n * map_rows, map_rows)
@@ -809,7 +892,7 @@
                 with scope("conv_grad"):
                     conv_grad(n)
                 with scope("input_grad"):
-                    input_grad(0, n)
+                    input_grad(0, n, n + 1)
                 if n > 0:
                     with scope("to_far"):
                         to_far(n - 1)
@@ -826,9 +909,8 @@
                     run(todo[l + 1])
             with scope("kernel_grad"):
                 kernel_grads(l, line // 2)
-            for n in range(nm):
-                with scope("input_grad"):
-                    input_grad(1, n)
+            with scope("input_grad"):
+                input_grad(1, 0, nm)
             with scope("drain"):
                 if l + 1 == layers:
                     for k in range(layers):
@@ -843,32 +925,25 @@
             for n in range(nm):
                 with scope("conv_grad"):
                     conv_grad(n)
-            with scope("scatter_1b"):
-                run(todo[1], pieces)
             with scope("kernel_grad"):
                 kernel_grads(0)
             todo[0], fed[0], owns[0] = scatter_tasks(0)
             with scope("scatter_1c"):
                 run(todo[1])
                 run(fed[1], pieces)
-            for n in range(nm):
-                with scope("input_grad"):
-                    input_grad(0, n)
+            with scope("input_grad"):
+                input_grad(0, 0, nm)
             with scope("to_far"):
                 for n in range(nm):
                     to_far(n)
-            with scope("input_grad"):
-                input_grad(1, 0)
             with scope("scatter_0a"):
                 run(todo[0], pieces)
             with scope("scatter_1d"):
                 run(fed[1])
             with scope("input_grad"):
-                for n in range(1, nm):
-                    input_grad(1, n)
+                input_grad(1, 0, nm)
             with scope("scatter_0b"):
                 run(todo[0], pieces)
-                run(fed[0], pieces)
             with scope("owns_2"):
                 for k in range(layers - 1, 1, -1):
                     run(owns[k])
@@ -988,7 +1063,7 @@
         vm((layers, line, rows_w, wide), BF16), vm((layers, line + 2, rows_w, wide), BF16),
         vm((rows_w, wide), F32),
         dma((11,)),
-        dma((layers, 2)), dma((layers, line, pieces)), dma((layers,)),
+        dma((layers, 4)), dma((layers, line, pieces)), dma((layers, 2)), dma((layers, line)),
         dma((2 * layers,)), dma((2 * layers,)),
         dma((layers,)), dma((layers, nm + 2)),
         dma((layers - 1,)), dma((layers - 1, chans)),

time: 111 us -> 107 us (0.964)
  Pallas kernels: 110 us -> 106 us
    pallas_call x1, Pallas kernels: 108 us -> 104 us  [block_call(): pl.pallas_call(functools.partial(block_kernel, sizes), out_shape=tuple((j...]
where the time goes in v6:
time: 107 us
  Pallas kernels  106 us (99%)
    pallas_call x1, Pallas kernels, block_call(): pl.pallas_call(functools.partial(block_kernel, sizes), out_shape=tuple((j...  104 us
    pallas_call x1, Pallas kernels, store_results(): pl.pallas_call(functools.partial(store_kernel, count), out_shape=tuple((j...  2.2 us

profile of v6, /device:TPU:0, one launch (start us, length us, event | category | flops | bytes accessed | tf_op | source)
XLA Modules:
  0.0 107.0 jit_solution(8545177923406353037)
XLA Ops:
  0.6 104.0 %shard_map.194 = (bf16[9,24,128]{2,1,0:T(8,128)(2,1)S(1)}, f32[864,128]{1,0:T(8,128)S(1)}, f32[3,9,64,128]{3,2,1,0:T(8,128)S(1)}, f32[3,9,64,128]{3,2,1,0:T(8,12...) custom-call(bf16[864,128]{1,0:T(8,128)(2,1)} %bitcast.12, ...), custom_call_target="tpu_custom_call" | custom-call | tf_op jit(solution)/shard_map/pallas_call | solution.py:1081
  104.7 2.2 %shard_map.195 = (bf16[9,24,128]{2,1,0:T(8,128)(2,1)}, f32[864,128]{1,0:T(8,128)}, f32[3,9,64,128]{3,2,1,0:T(8,128)}, f32[3,9,64,128]{3,2,1,0:T(8,128)}, f32[3,9...) custom-call(bf16[9,24,128]{2,1,0:T(8,128)(2,1)S(1)} %get-tuple-eleme, ...), custom_call_target="tpu_custom_call" | custom-call | tf_op jit(solution)/shard_map/pallas_call | solution.py:1015

commit v7 on v6

--- a/solution.py
+++ b/solution.py
@@ -40,12 +40,20 @@
         pl.loop(low, high)(body)
 
 
-scope = jax.named_scope
+class scope:
+    def __init__(self, name): pass
+    def __enter__(self): return self
+    def __exit__(self, *a): return False
 
 
 def run(tasks, amount=None):
     for _ in range(len(tasks) if amount is None else min(amount, len(tasks))):
         tasks.pop(0)()
+
+
+def grad_parts(layers, rows_w):
+    pieces = 2 if rows_w % 32 == 0 else 1
+    return [4 if l == 0 and rows_w % 64 == 0 else pieces for l in range(layers)]
 
 
 def tile8(values):
@@ -345,7 +353,7 @@
         remote(view, view, sc_s.at[l], sc_r.at[l, core], (m, core)).wait_send()
 
     own_along(0)
-    own_aside(0)
+    own_aside_late(0, 0)
 
     loads[2].wait()
     col_of = lax.broadcasted_iota(jnp.int32, (width, width), 0)
@@ -370,6 +378,8 @@
 
     for n in range(nm):
         act_send(0, n)
+
+    own_aside_late(0, 1)
 
     for n in range(nm):
         for i in range(3):
@@ -494,10 +504,9 @@
                 run(x_near, pieces)
         with scope("turn"):
             slots = LANES // rows_w
-            for i in range(maps // slots):
-                turned[l, :, i * LANES : (i + 1) * LANES] = (
-                    wcat[l * maps + i * slots : l * maps + (i + 1) * slots, :, :].reshape(LANES, wide).T
-                )
+            for i, owner in enumerate((across, far, core, c)):
+                rows = wcat[pl.ds(l * maps + owner * slots, slots), :, :].reshape(LANES, wide)
+                turned[l, :, i * LANES : (i + 1) * LANES] = rows.T
         if l + 1 < layers:
             with scope("gather_own_cross"):
                 run(c_tasks[l + 1], 1)
@@ -535,20 +544,25 @@
             )
             scale_send(l)
 
-        @pl.loop(0, chunks)
-        def _(i):
+        def own_chunk(i, carry):
             r = rows_of(i)
             unit = (conv[r, :] - center) * inv_std
             pre = gain * unit + bias
             sigma = 1.0 / (1.0 + jnp.exp(-pre))
             valid = mask_ref[r, :]
             result = pre * sigma * valid
+            slant = sigma * (1.0 + pre * (1.0 - sigma)) * valid
             normed[l, r, :] = unit
-            slope[l, r, :] = sigma * (1.0 + pre * (1.0 - sigma)) * valid
             if l + 1 < layers:
+                slope[l, r, :] = slant
                 act[l + 1, r, lane_own] = result.astype(BF16)
-            else:
-                result_ref[r, :] = result
+                return carry
+            result_ref[r, :] = result
+            value = spread[r, :] * slant
+            conv[r, :] = value
+            return carry[0] + tile8(value * unit), carry[1] + tile8(value)
+
+        grad_sums = lax.fori_loop(0, chunks, own_chunk, (zero8, zero8))
 
         def activate(owner, first, last):
             pair = scale_ref[l, owner]
@@ -629,24 +643,28 @@
     def kth_place(k, l):
         return places[straight(l)][k] if line <= 8 else place_of(k)
 
-    def part_of(g):
-        return pl.ds(g * piece_rows, piece_rows)
+    parts = grad_parts(layers, rows_w)
+
+    def part_of(l, g):
+        rows = rows_w // parts[l]
+        return pl.ds(g * rows, rows)
 
     def gx_copy(l, z, g):
         return remote(
-            gx_out.at[l, z, part_of(g)], gx_in.at[l, z, part_of(g)],
-            gx_s.at[l], gx_r.at[l, z, g], beside,
+            gx_out.at[l, z, part_of(l, g)], gx_in.at[l, z, part_of(l, g)],
+            gx_s.at[l], gx_r.at[line * sum(parts[:l]) + z * parts[l] + g], beside,
         )
 
     def gz_copy(l, z, g, slot, dev):
         return remote(
-            gz_out.at[l, z, part_of(g)], gz_in.at[l, slot, part_of(g)],
-            gz_s.at[l], gz_r.at[l, slot, g], dev,
+            gz_out.at[l, z, part_of(l, g)], gz_in.at[l, slot, part_of(l, g)],
+            gz_s.at[l], gz_r.at[(line + 2) * sum(parts[:l]) + slot * parts[l] + g], dev,
         )
 
     def shard(l, slot, g):
-        first = pl.multiple_of(slot * rows_w, 8) + g * piece_rows
-        return grad_w[l, pl.ds(first, piece_rows), :]
+        rows = rows_w // parts[l]
+        first = pl.multiple_of(slot * rows_w, 8) + g * rows
+        return grad_w[l, pl.ds(first, rows), :]
 
     tile = 2 * rows_w
     fine = tile % LANES == 0
@@ -667,13 +685,20 @@
             z = kth_place(k, l)
             if fine:
                 kernel_grad(l, z * tile, tile)
-            for g in range(pieces):
-                gx_out[l, z, part_of(g)] = shard(l, z * 2 + 1 - b, g).astype(BF16)
-            for g in range(pieces):
+            for g in range(parts[l]):
+                gx_out[l, z, part_of(l, g)] = shard(l, z * 2 + 1 - b, g).astype(BF16)
+            if l == 0 and line <= 8 and k == line - 1 and layers > 1:
+                for g in range(parts[1]):
+                    if is_late(1, k, g):
+                        gx_copy(1, a, g).start()
+            for g in range(parts[l]):
                 if line > 8 or is_early(l, k, g):
                     gx_copy(l, z, g).start()
 
         steps(low, high, go)
+
+    def is_late(l, k, g):
+        return l == 1 and line <= 8 and k == line - 1 and g >= (parts[l] + 1) // 2
 
     def is_early(l, k, g):
         return l == 0 or k < 2
@@ -681,24 +706,24 @@
     def scatter_x(l):
         if line <= 8:
             for k in range(line):
-                for g in range(pieces):
-                    if not is_early(l, k, g):
+                for g in range(parts[l]):
+                    if not is_early(l, k, g) and not is_late(l, k, g):
                         gx_copy(l, kth_place(k, l), g).start()
 
     def pair_sum(l, z, g):
         gx_copy(l, z, g).wait_recv()
-        return shard(l, z * 2 + b, g) + gx_in[l, z, part_of(g)].astype(F32)
+        return shard(l, z * 2 + b, g) + gx_in[l, z, part_of(l, g)].astype(F32)
 
     def onward(l, z, g, fed, dev, slot):
         value = pair_sum(l, z, g)
         if fed:
             gz_copy(l, z, g, z, dev).wait_recv()
-            value = value + gz_in[l, z, part_of(g)].astype(F32)
-        gz_out[l, z, part_of(g)] = value.astype(BF16)
+            value = value + gz_in[l, z, part_of(l, g)].astype(F32)
+        gz_out[l, z, part_of(l, g)] = value.astype(BF16)
         gz_copy(l, z, g, slot, dev).start()
 
     def straight(l):
-        return l == 0 and 2 < line <= 8
+        return False
 
     def scatter_step(l, d, g, fed):
         ends = straight(l) and d == line - 1
@@ -717,7 +742,7 @@
             pl.when(now)(functools.partial(onward, l, z, g, fed, dev, slot))
 
     def scatter_own(l, g):
-        r = part_of(g)
+        r = part_of(l, g)
         total_w[r, :] = pair_sum(l, a, g)
 
         def add(slot):
@@ -740,14 +765,14 @@
             wcopy_ref[l, t, r] = new.astype(BF16)
 
     def scatter_tasks(l):
-        owns = [functools.partial(scatter_own, l, g) for g in range(pieces)]
+        owns = [functools.partial(scatter_own, l, g) for g in range(parts[l])]
         if line <= 8:
             first, fed = (
                 [
                     functools.partial(scatter_step, l, line - e, g, kind)
                     for e in ((2, 1, *range(3, line)) if straight(l) else range(1, line))
                     if e > kind + (kind and straight(l))
-                    for g in range(pieces)
+                    for g in range(parts[l])
                 ]
                 for kind in (False, True)
             )
@@ -755,7 +780,7 @@
 
         def everything():
             def go(e):
-                for g in range(pieces):
+                for g in range(parts[l]):
                     scatter_step(l, line - e, g, False)
                     scatter_step(l, line - e, g, True)
 
@@ -764,10 +789,10 @@
         return [everything], [], owns
 
     def scatter_drain(l):
-        remote(gx_out.at[l], gx_in.at[l], gx_s.at[l], gx_r.at[l, 0, 0], beside).wait_send()
+        remote(gx_out.at[l], gx_in.at[l], gx_s.at[l], gx_r.at[0], beside).wait_send()
         view = pl.ds(0, line - 1)
         remote(
-            gz_out.at[l, view], gz_in.at[l, view], gz_s.at[l], gz_r.at[l, 0, 0], beside
+            gz_out.at[l, view], gz_in.at[l, view], gz_s.at[l], gz_r.at[0], beside
         ).wait_send()
 
     def layer_drain(l):
@@ -776,11 +801,6 @@
         remote(far_out.at[l], far_in.at[l], fr_s.at[l], fr_r.at[l, 0], (m, far)).wait_send()
 
     half = 2 * LANES
-    own_half = (c // 2) * half
-    other_half = half - own_half
-    lane_in_half = pl.ds(pl.multiple_of((c % 2) * LANES, LANES), LANES)
-    lane_out_half = pl.ds(pl.multiple_of((1 - c % 2) * LANES, LANES), LANES)
-
     def pair_copy(l, h, n):
         return remote(
             pair_out.at[l, h, pl.ds(n * map_rows, map_rows), :],
@@ -798,16 +818,7 @@
     todo, fed, owns = {}, {}, {}
     for l in reversed(range(layers)):
         e = layers + l
-        source = spread if l == layers - 1 else back
-
-        def slope_chunk(i, carry):
-            r = rows_of(i)
-            value = source[r, :] * slope[l, r, :]
-            conv[r, :] = value
-            return carry[0] + tile8(value * normed[l, r, :]), carry[1] + tile8(value)
-
-        zero8 = jnp.zeros((8, LANES), F32)
-        gain_sum, bias_sum = lax.fori_loop(0, chunks, slope_chunk, (zero8, zero8))
+        gain_sum, bias_sum = grad_sums
         stat[e, m] = jnp.concatenate(
             [
                 jnp.sum(gain_sum, axis=0, keepdims=True),
@@ -828,7 +839,7 @@
             run(fed[l + 2])
         if l + 1 < layers:
             with scope("scatter_a"):
-                run(todo[l + 1], pieces if l > 0 else 2 * pieces)
+                run(todo[l + 1], parts[l + 1] if l > 0 else 2 * parts[l + 1])
         with scope("stat_wait_back"):
             stat_wait(e)
 
@@ -869,22 +880,19 @@
                         dcat[r, t * LANES : (t + 1) * LANES] = term.astype(BF16)
 
         def input_grad(h, first, last):
-            start = other_half if h == 0 else own_half
             r = pl.ds(first * map_rows, (last - first) * map_rows)
-            part[h, r, :] = jnp.dot(
-                dcat[r, :], turned[l, :, pl.ds(pl.multiple_of(start, half), half)],
-                preferred_element_type=F32,
+            out = jnp.dot(
+                dcat[r, :], turned[l, :, h * half : (h + 1) * half], preferred_element_type=F32
             )
-            pair_out[l, h, r, :] = part[h, r, lane_out_half].astype(BF16)
+            pair_out[l, h, r, :] = out[:, :LANES].astype(BF16)
             for n in range(first, last):
                 pair_copy(l, h, n).start()
+            part[h, r, :] = out[:, LANES:]
 
         def to_far(n):
             r = pl.ds(n * map_rows, map_rows)
             pair_copy(l, 0, n).wait_recv()
-            far_out[l, r, :] = (
-                part[0, r, lane_in_half] + pair_in[l, 0, r, :].astype(F32)
-            ).astype(BF16)
+            far_out[l, r, :] = (part[0, r, :] + pair_in[l, 0, r, :].astype(F32)).astype(BF16)
             far_copy(l, n).start()
 
         if l > 0:
@@ -898,8 +906,8 @@
                         to_far(n - 1)
             if l + 1 < layers:
                 with scope("scatter_b"):
-                    run(todo[l + 1], pieces)
-                    run(fed[l + 1], pieces)
+                    run(todo[l + 1], parts[l + 1])
+                    run(fed[l + 1], parts[l + 1])
             with scope("kernel_grad"):
                 kernel_grads(l, 0, line // 2)
             with scope("to_far"):
@@ -930,24 +938,27 @@
             todo[0], fed[0], owns[0] = scatter_tasks(0)
             with scope("scatter_1c"):
                 run(todo[1])
-                run(fed[1], pieces)
+                run(fed[1], parts[1])
             with scope("input_grad"):
                 input_grad(0, 0, nm)
             with scope("to_far"):
                 for n in range(nm):
                     to_far(n)
             with scope("scatter_0a"):
-                run(todo[0], pieces)
+                run(todo[0], parts[0])
             with scope("scatter_1d"):
                 run(fed[1])
             with scope("input_grad"):
                 input_grad(1, 0, nm)
             with scope("scatter_0b"):
-                run(todo[0], pieces)
+                run(todo[0], parts[0])
+                run(fed[0], parts[0])
             with scope("owns_2"):
                 for k in range(layers - 1, 1, -1):
                     run(owns[k])
 
+        zero8 = jnp.zeros((8, LANES), F32)
+        grad_sums = (zero8, zero8)
         for n in range(nm):
             r = pl.ds(n * map_rows, map_rows)
             with scope("far_wait"):
@@ -960,17 +971,17 @@
                 with scope("scatter_d"):
                     run(fed[l + 1])
 
-            @pl.loop(n * per_map, (n + 1) * per_map)
-            def _(i):
+            def back_chunk(i, carry):
                 r = rows_of(i)
-                value = (
-                    part[1, r, lane_in_half]
-                    + pair_in[l, 1, r, :].astype(F32)
-                    + far_in[l, r, :].astype(F32)
-                )
+                value = part[1, r, :] + pair_in[l, 1, r, :].astype(F32) + far_in[l, r, :].astype(F32)
                 if l == 0:
-                    value = value * mask_ref[r, :]
-                back[r, :] = value
+                    back[r, :] = value * mask_ref[r, :]
+                    return carry
+                value = value * slope[l - 1, r, :]
+                conv[r, :] = value
+                return carry[0] + tile8(value * normed[l - 1, r, :]), carry[1] + tile8(value)
+
+            grad_sums = lax.fori_loop(n * per_map, (n + 1) * per_map, back_chunk, grad_sums)
 
     with scope("norms"):
         for values, place in ((gain_in, 0), (bias_in, 1)):
@@ -1055,7 +1066,7 @@
         vm((nm, map_rows + 2 * PAD, LANES), F32),
         vm((pixels, wide), BF16),
         vm((layers, channels, wide), F32),
-        vm((2, pixels, 2 * LANES), F32),
+        vm((2, pixels, LANES), F32),
         vm((2 * layers, maps, 8, LANES), F32),
         vm((layers, 2, pixels, LANES), BF16), vm((layers, 2, pixels, LANES), BF16),
         vm((layers, pixels, LANES), BF16), vm((layers, pixels, LANES), BF16),
@@ -1069,8 +1080,8 @@
         dma((layers - 1,)), dma((layers - 1, chans)),
         dma((layers,)), dma((layers, nm + 1)),
         dma((layers,)), dma((layers, nm)),
-        dma((layers,)), dma((layers, line, pieces)),
-        dma((layers,)), dma((layers, line + 2, pieces)),
+        dma((layers,)), dma((line * sum(grad_parts(layers, rows_w)),)),
+        dma((layers,)), dma(((line + 2) * sum(grad_parts(layers, rows_w)),)),
     ]
     arrays = (
         [(index.shape, BF16), ((pixels, LANES), F32)]

time: 107 us -> 106 us (level)
    pallas_call x1, Pallas kernels: 104 us -> 102 us  [block_call(): pl.pallas_call(functools.partial(block_kernel, sizes), out_shape=tuple((j...]
where the time goes in v7:
time: 106 us; the launch traced here: 105 us
  Pallas kernels  105 us (99%)
    pallas_call x1, Pallas kernels, block_call(): pl.pallas_call(functools.partial(block_kernel, sizes), out_shape=tuple((j...  102 us
    pallas_call x1, Pallas kernels, store_results(): pl.pallas_call(functools.partial(store_kernel, count), out_shape=tuple((j...  2.2 us

profile of v7, /device:TPU:0, one launch (start us, length us, event | category | flops | bytes accessed | tf_op | source)
XLA Modules:
  0.0 105.4 jit_solution(2429122057599729053)
XLA Ops:
  0.6 102.3 %shard_map.194 = (bf16[9,24,128]{2,1,0:T(8,128)(2,1)S(1)}, f32[864,128]{1,0:T(8,128)S(1)}, f32[3,9,64,128]{3,2,1,0:T(8,128)S(1)}, f32[3,9,64,128]{3,2,1,0:T(8,12...) custom-call(bf16[864,128]{1,0:T(8,128)(2,1)} %bitcast.12, ...), custom_call_target="tpu_custom_call" | custom-call | tf_op jit(solution)/shard_map/pallas_call | solution.py:1092
  103.0 2.2 %shard_map.195 = (bf16[9,24,128]{2,1,0:T(8,128)(2,1)}, f32[864,128]{1,0:T(8,128)}, f32[3,9,64,128]{3,2,1,0:T(8,128)}, f32[3,9,64,128]{3,2,1,0:T(8,128)}, f32[3,9...) custom-call(bf16[9,24,128]{2,1,0:T(8,128)(2,1)S(1)} %get-tuple-eleme, ...), custom_call_target="tpu_custom_call" | custom-call | tf_op jit(solution)/shard_map/pallas_call | solution.py:1026

commit v8 on v7

--- a/solution.py
+++ b/solution.py
@@ -274,11 +274,16 @@
         for at, count in zip((inner, jnp.logical_not(inner)), counts):
             pl.when(at)(functools.partial(crossed, count))
 
+    exchanged = []
+
     def stat_send(e):
+        if exchanged:
+            stat_all(exchanged[-1]).wait_send()
+        exchanged.append(e)
         view = stat.at[e, m]
 
         def send(peer):
-            remote(view, view, st_s.at[e], st_r.at[e], (peer, c)).start()
+            remote(view, view, st_s.at[0], st_r.at[len(exchanged) % 2], (peer, c)).start()
 
         def go(d):
             @pl.when(a + line - d < line)
@@ -298,13 +303,10 @@
 
     def stat_all(e):
         view = stat.at[e, pl.ds(0, maps - 1)]
-        return remote(view, view, st_s.at[e], st_r.at[e], beside)
+        return remote(view, view, st_s.at[0], st_r.at[(exchanged.index(e) + 1) % 2], beside)
 
     def stat_wait(e):
         stat_all(e).wait_recv()
-
-    def stat_drain(e):
-        stat_all(e).wait_send()
 
     lane_own = pl.ds(pl.multiple_of(c * LANES, LANES), LANES)
 
@@ -658,7 +660,7 @@
     def gz_copy(l, z, g, slot, dev):
         return remote(
             gz_out.at[l, z, part_of(l, g)], gz_in.at[l, slot, part_of(l, g)],
-            gz_s.at[l], gz_r.at[(line + 2) * sum(parts[:l]) + slot * parts[l] + g], dev,
+            gz_s.at[l], gz_r.at[(line + 1) * sum(parts[:l]) + slot * parts[l] + g], dev,
         )
 
     def shard(l, slot, g):
@@ -796,7 +798,6 @@
         ).wait_send()
 
     def layer_drain(l):
-        stat_drain(layers + l)
         remote(pair_out.at[l], pair_in.at[l], pr_s.at[l], pr_r.at[l, 0], (m, core)).wait_send()
         remote(far_out.at[l], far_in.at[l], fr_s.at[l], fr_r.at[l, 0], (m, far)).wait_send()
 
@@ -924,7 +925,6 @@
                     for k in range(layers):
                         gather_drain(k)
                         act_drain(k)
-                        stat_drain(k)
                         if k + 1 < layers:
                             scale_drain(k)
                 else:
@@ -1008,6 +1008,7 @@
     with scope("drain_end"):
         layer_drain(0)
         scatter_drain(0)
+        stat_all(exchanged[-1]).wait_send()
 
 
 def store_kernel(count, *refs):
@@ -1071,17 +1072,17 @@
         vm((layers, 2, pixels, LANES), BF16), vm((layers, 2, pixels, LANES), BF16),
         vm((layers, pixels, LANES), BF16), vm((layers, pixels, LANES), BF16),
         vm((layers, line, rows_w, wide), BF16), vm((layers, line, rows_w, wide), BF16),
-        vm((layers, line, rows_w, wide), BF16), vm((layers, line + 2, rows_w, wide), BF16),
+        vm((layers, line, rows_w, wide), BF16), vm((layers, line + 1, rows_w, wide), BF16),
         vm((rows_w, wide), F32),
         dma((11,)),
         dma((layers, 4)), dma((layers, line, pieces)), dma((layers, 2)), dma((layers, line)),
-        dma((2 * layers,)), dma((2 * layers,)),
+        dma((1,)), dma((2,)),
         dma((layers,)), dma((layers, nm + 2)),
         dma((layers - 1,)), dma((layers - 1, chans)),
         dma((layers,)), dma((layers, nm + 1)),
         dma((layers,)), dma((layers, nm)),
         dma((layers,)), dma((line * sum(grad_parts(layers, rows_w)),)),
-        dma((layers,)), dma(((line + 2) * sum(grad_parts(layers, rows_w)),)),
+        dma((layers,)), dma(((line + 1) * sum(grad_parts(layers, rows_w)),)),
     ]
     arrays = (
         [(index.shape, BF16), ((pixels, LANES), F32)]

time: 106 us -> 105 us (level)
  no operation moved by 1% of the time
where the time goes in v8:
time: 105 us
  Pallas kernels  104 us (99%)
    pallas_call x1, Pallas kernels, block_call(): pl.pallas_call(functools.partial(block_kernel, sizes), out_shape=tuple((j...  102 us
    pallas_call x1, Pallas kernels, store_results(): pl.pallas_call(functools.partial(store_kernel, count), out_shape=tuple((j...  2.2 us

profile of v8, /device:TPU:0, one launch (start us, length us, event | category | flops | bytes accessed | tf_op | source)
XLA Modules:
  0.0 105.2 jit_solution(5787692066444525310)
XLA Ops:
  0.6 102.2 %shard_map.194 = (bf16[9,24,128]{2,1,0:T(8,128)(2,1)S(1)}, f32[864,128]{1,0:T(8,128)S(1)}, f32[3,9,64,128]{3,2,1,0:T(8,128)S(1)}, f32[3,9,64,128]{3,2,1,0:T(8,12...) custom-call(bf16[864,128]{1,0:T(8,128)(2,1)} %bitcast.12, ...), custom_call_target="tpu_custom_call" | custom-call | tf_op jit(solution)/shard_map/pallas_call | solution.py:1093
  102.9 2.2 %shard_map.195 = (bf16[9,24,128]{2,1,0:T(8,128)(2,1)}, f32[864,128]{1,0:T(8,128)}, f32[3,9,64,128]{3,2,1,0:T(8,128)}, f32[3,9,64,128]{3,2,1,0:T(8,128)}, f32[3,9...) custom-call(bf16[9,24,128]{2,1,0:T(8,128)(2,1)S(1)} %get-tuple-eleme, ...), custom_call_target="tpu_custom_call" | custom-call | tf_op jit(solution)/shard_map/pallas_call | solution.py:1027

commit v9 on v8

--- a/solution.py
+++ b/solution.py
@@ -316,13 +316,15 @@
     def act_copy(l, n, owner, dev, place):
         rows = pl.ds(n * map_rows, map_rows)
         view = act.at[0, rows, lanes_of(owner)] if l == 0 else raw.at[l - 1, owner, rows]
-        return remote(view, view, ag_s.at[l], ag_r.at[l, place], dev)
+        return remote(view, view, ag_s.at[0], ag_r.at[l, place], dev)
 
     def act_blocks(l, count, place):
         view = act.at[0, :, pl.ds(0, count * LANES)] if l == 0 else raw.at[l - 1, pl.ds(0, count)]
-        return remote(view, view, ag_s.at[l], ag_r.at[l, place], (m, core))
+        return remote(view, view, ag_s.at[0], ag_r.at[l, place], (m, core))
 
     def act_send(l, n):
+        if l > 0 and n == 0:
+            act_drain(l - 1)
         act_copy(l, n, c, (m, far), n).start()
         act_copy(l, n, c, (m, core), nm).start()
 
@@ -344,15 +346,17 @@
         return remote(view, view, ssem, sc_r.at[l, owner], dev)
 
     def scale_send(l):
+        if l > 0:
+            scale_drain(l - 1)
         for other in (core, far, across):
-            scale_copy(l, c, (m, other), sc_s.at[l]).start()
+            scale_copy(l, c, (m, other), sc_s.at[0]).start()
 
     def scale_wait(l, owner):
-        scale_copy(l, owner, (m, core), sc_s.at[l]).wait_recv()
+        scale_copy(l, owner, (m, core), sc_s.at[0]).wait_recv()
 
     def scale_drain(l):
         view = scale_ref.at[l, pl.ds(0, 3)]
-        remote(view, view, sc_s.at[l], sc_r.at[l, core], (m, core)).wait_send()
+        remote(view, view, sc_s.at[0], sc_r.at[l, core], (m, core)).wait_send()
 
     own_along(0)
     own_aside_late(0, 0)
@@ -924,9 +928,9 @@
                 if l + 1 == layers:
                     for k in range(layers):
                         gather_drain(k)
-                        act_drain(k)
-                        if k + 1 < layers:
-                            scale_drain(k)
+                    act_drain(layers - 1)
+                    if layers > 1:
+                        scale_drain(layers - 2)
                 else:
                     layer_drain(l + 1)
         else:
@@ -1077,8 +1081,8 @@
         dma((11,)),
         dma((layers, 4)), dma((layers, line, pieces)), dma((layers, 2)), dma((layers, line)),
         dma((1,)), dma((2,)),
-        dma((layers,)), dma((layers, nm + 2)),
-        dma((layers - 1,)), dma((layers - 1, chans)),
+        dma((1,)), dma((layers, nm + 2)),
+        dma((1,)), dma((layers - 1, chans)),
         dma((layers,)), dma((layers, nm + 1)),
         dma((layers,)), dma((layers, nm)),
         dma((layers,)), dma((line * sum(grad_parts(layers, rows_w)),)),

time: 105 us -> 105 us (level)
  no operation moved by 1% of the time
where the time goes in v9:
time: 105 us
  Pallas kernels  104 us (99%)
    pallas_call x1, Pallas kernels, block_call(): pl.pallas_call(functools.partial(block_kernel, sizes), out_shape=tuple((j...  102 us
    pallas_call x1, Pallas kernels, store_results(): pl.pallas_call(functools.partial(store_kernel, count), out_shape=tuple((j...  2.2 us

profile of v9, /device:TPU:0, one launch (start us, length us, event | category | flops | bytes accessed | tf_op | source)
XLA Modules:
  0.0 105.2 jit_solution(5690617785460288713)
XLA Ops:
  0.6 102.2 %shard_map.194 = (bf16[9,24,128]{2,1,0:T(8,128)(2,1)S(1)}, f32[864,128]{1,0:T(8,128)S(1)}, f32[3,9,64,128]{3,2,1,0:T(8,128)S(1)}, f32[3,9,64,128]{3,2,1,0:T(8,12...) custom-call(bf16[864,128]{1,0:T(8,128)(2,1)} %bitcast.12, ...), custom_call_target="tpu_custom_call" | custom-call | tf_op jit(solution)/shard_map/pallas_call | solution.py:1097
  102.8 2.2 %shard_map.195 = (bf16[9,24,128]{2,1,0:T(8,128)(2,1)}, f32[864,128]{1,0:T(8,128)}, f32[3,9,64,128]{3,2,1,0:T(8,128)}, f32[3,9,64,128]{3,2,1,0:T(8,128)}, f32[3,9...) custom-call(bf16[9,24,128]{2,1,0:T(8,128)(2,1)S(1)} %get-tuple-eleme, ...), custom_call_target="tpu_custom_call" | custom-call | tf_op jit(solution)/shard_map/pallas_call | solution.py:1031
